TPU v7x, 32 devices: a whole 2x2x4 slice. The times are simulated.
32 devices in a mesh: dom: 16 (over z, x, core), col: 2 (over y).
Axes of the slice: x: 2, y: 2, z: 4, core: 2. Of those that a mesh axis runs over, the one named last changes fastest.
Arguments:
- feats: bfloat16 [8192, 256], P('dom', 'col'), may hold values from -6 to 6
- w_first: bfloat16 [256, 256], replicated, may hold values from -0.375 to 0.375
- w_second: bfloat16 [256, 256], replicated, may hold values from -0.375 to 0.375
- block_cols: int32 [64, 32], P('dom'), may hold values from 0 to 63, as said below
- block_count: int32 [64], P('dom'), may hold values from 1 to 32
- block_vals: bfloat16 [64, 32, 128, 128], P('dom', 'col'), may hold values from -0.125 to 0.125
- cotangent: bfloat16 [8192, 256], P('dom', 'col'), may hold values from -6 to 6
Outputs:
- output: float32 [8192, 256], P('dom', 'col')
- grad_first: float32 [256, 256], P(None, 'col')
- grad_second: float32 [256, 256], P(None, 'col')
Inputs may be any that keep to these rules, and one draw needn't show every extreme that they name: Each row of block_cols names 32 different column blocks.
All inputs are finite; a program needn't handle non-finite values.
Results may differ from a plain program's by a relative error of at most 0.019.
Values may be sent and summed in bfloat16 or wider, within the bound.
No kernel may reach another device: no remote copies, remote signals or barrier semaphores. Data moves between devices by JAX's collectives and lax.ppermute only.
A program may use at most 64 MiB of HBM per device.

v0:
```python
import functools

import jax
import jax.numpy as jnp
from jax import lax
from jax.experimental import pallas as pl
from jax.experimental.pallas import tpu as pltpu
from jax.sharding import PartitionSpec as P


BLK = 128
GROUP = 4
LANES = 128
F32 = jnp.float32
BF16 = jnp.bfloat16


def swap(value, axis, mask):
    size = lax.axis_size(axis)
    return lax.ppermute(value, axis, [(i, i ^ mask) for i in range(size)])


def widen(own):
    if own.shape[1] % LANES:
        return lax.all_gather(own, "col", axis=1, tiled=True)
    return own


def gather_order(nd, nc):
    far = list(range(4, nd, 4))
    order = [(v, 0, (0, 0), "dom") for v in far[:2]]
    late = [(v, 0, (0, 0), "dom") for v in far[2:]]
    corners = []
    for n, v in enumerate((0, *far)):
        if nd >= 4:
            order.append((v | 2, 0, (v, 0), "dom"))
        order += [(v, cx, (v, 0), "col") for cx in range(1, nc)]
        order += late + corners
        late, corners = [], []
        for cx in range(1, nc):
            if nd >= 4 and (n + cx) % 2:
                corners.append((v | 2, cx, (v, cx), "dom"))
            elif nd >= 4:
                corners.append((v | 2, cx, (v | 2, 0), "col"))
    return order + corners


def gather(own, nc):
    nd = lax.axis_size("dom")
    got = {(0, 0): own}
    for v, cx, (sv, sc), axis in gather_order(nd, nc):
        mask = v ^ sv if axis == "dom" else cx ^ sc
        got[v, cx] = swap(got[sv, sc], axis, mask)
    return [[got[v, cx] for cx in range(nc)] for v in range(0, nd, 2)]


def load(groups, dest, sems, first=0):
    copies = []
    col = lax.axis_index("col")
    for g, pieces in enumerate(groups):
        for cx, piece in enumerate(pieces):
            rows, wide = piece.shape
            lane = 0
            if len(pieces) > 1:
                lane = pl.multiple_of((col ^ cx) * wide, LANES)
            copies.append(
                pltpu.make_async_copy(
                    piece,
                    dest.at[pl.ds(g * rows, rows), pl.ds(lane, wide)],
                    sems.at[first + len(copies)],
                )
            )
    for copy in copies:
        copy.start()
    return copies


def split(refs, counts):
    out, at = [], 0
    for n in counts:
        out.append(refs[at : at + n])
        at += n
    return out, refs[at:]


def tiles(vals, r, lk, at):
    return jnp.concatenate([vals[r, lk[at + t]] for t in range(GROUP)], axis=1)


def place(lx, at):
    return pl.ds(pl.multiple_of(lx[at] * BLK, BLK), BLK)


def back_rows(nb, slots, first, lk, lx, ln, vals, cw, hg):
    for i in range(nb):
        grad = cw[i * BLK : (i + 1) * BLK, :]
        base = (first + i) * (slots + GROUP)

        def step(g, carry, i=i, grad=grad, base=base):
            at = base + g * GROUP
            prod = lax.dot_general(
                tiles(vals, i, lk, at),
                grad,
                (((0,), (0,)), ((), ())),
                preferred_element_type=F32,
            )
            for t in range(GROUP):
                hg[place(lx, at + t), :] += prod[t * BLK : (t + 1) * BLK, :]
            return carry

        lax.fori_loop(0, (ln[first + i] + GROUP - 1) // GROUP, step, 0)


def project(cot, w2, cw):
    cw[...] = lax.dot_general(
        cot[...], w2[...], (((1,), (1,)), ((), ())), preferred_element_type=F32
    ).astype(BF16)


def back_kernel(nb, slots, counts, first, lk, lx, ln, w2, vals, *refs):
    groups, (hg, cot, cw, sems) = split(refs, counts)
    copies = load(groups, cot, sems)
    hg[...] = jnp.zeros_like(hg)
    for copy in copies:
        copy.wait()
    project(cot, w2, cw)
    back_rows(nb, slots, first, lk, lx, ln, vals, cw, hg)


def lists_kernel(nb, slots, blank, *refs):
    cols_own, used_own, cols_far, used_far, v_hbm, lk, lx, ln, v_own, sem = refs
    bring = pltpu.make_async_copy(v_hbm, v_own, sem)
    bring.start()
    cols = ((cols_own, used_own), (cols_far, used_far))
    dom = lax.axis_index("dom")
    base = lax.axis_index("col") * slots
    stride = slots + GROUP
    for r in range(2 * nb):
        names, used = cols[r // nb]
        limit = used[r % nb]
        n = jnp.int32(0)
        for k in range(slots):
            block = names[r % nb, base + k]
            rel = lax.div(block, jnp.int32(nb)) ^ dom
            lk[r * stride + n] = k
            lx[r * stride + n] = (rel >> 1) * nb + lax.rem(block, jnp.int32(nb))
            ok = jnp.logical_and(base + k < limit, (rel & 1) == 0)
            n = n + ok.astype(jnp.int32)
        ln[r] = n
        for t in range(GROUP):
            lk[r * stride + n + t] = 0
            lx[r * stride + n + t] = blank
    bring.wait()


def put(ref, rows, value, narrow):
    width = value.shape[1]
    if narrow % LANES:
        ref[rows, :] = value.astype(ref.dtype)
        return
    col = lax.axis_index("col")
    for q in range(width // narrow):
        at = pl.ds(pl.multiple_of((col ^ q) * narrow, LANES), narrow)
        ref[rows, at] = value[:, q * narrow : (q + 1) * narrow].astype(ref.dtype)


def rows_product(nb, slots, r, lk, lx, ln, vals, source, width):
    base = r * (slots + GROUP)

    def step(g, acc):
        at = base + g * GROUP
        right = jnp.concatenate(
            [source[place(lx, at + t), :] for t in range(GROUP)], axis=0
        )
        return acc + jnp.dot(
            tiles(vals, r % nb, lk, at), right, preferred_element_type=F32
        )

    steps = (ln[r] + GROUP - 1) // GROUP
    return lax.fori_loop(0, steps, step, jnp.zeros((BLK, width), F32))


def first_kernel(nb, slots, counts, narrow, lk, lx, ln, v_own, v_far, *refs):
    groups, (keep, send, src, sems) = split(refs, counts)
    copies = load(groups, src, sems)
    width = src.shape[1]
    src[src.shape[0] - BLK :, :] = jnp.zeros((BLK, width), BF16)
    for copy in copies:
        copy.wait()
    for r in range(2 * nb):
        acc = rows_product(nb, slots, r, lk, lx, ln, v_own if r < nb else v_far, src, width)
        put(keep if r < nb else send, pl.ds(r % nb * BLK, BLK), acc, narrow)


def second_kernel(nb, slots, counts, narrow, lk, lx, ln, w1, w2, v_own, v_far, hg, hg_far, *refs):
    groups, (keep, send, gkeep, gsend, agg, hid, cot, mix, total, sems) = split(refs, counts)
    copies = load(groups[:-2], agg, sems)
    more = load(groups[-2:], cot, sems, len(copies))
    blocks, width = agg.shape
    chunk = nb * BLK
    hid[blocks:, :] = jnp.zeros((BLK, width), BF16)
    for copy in copies:
        copy.wait()
    total[...] = jnp.zeros_like(total)
    for g in range(blocks // chunk):
        rows = pl.ds(g * chunk, chunk)
        a = agg[rows, :]
        first = jnp.dot(a, w1[...], preferred_element_type=F32)
        sig = 0.5 * jnp.tanh(0.5 * first) + 0.5
        act = first * sig
        hid[rows, :] = act.astype(BF16)
        slope = sig + act * (1.0 - sig)
        grad = ((hg[rows, :] + hg_far[rows, :]) * slope).astype(BF16)
        total[...] += lax.dot_general(
            a, grad, (((0,), (0,)), ((), ())), preferred_element_type=F32
        )
    for r in range(2 * nb):
        acc = rows_product(nb, slots, r, lk, lx, ln, v_own if r < nb else v_far, hid, width)
        mix[r * BLK : (r + 1) * BLK, :] = acc.astype(BF16)
    for copy in more:
        copy.wait()
    core = lax.axis_index("dom") & 1
    everything = pl.ds(0, width)
    second = lax.dot_general(
        mix[...], cot[...], (((0,), (0,)), ((), ())), preferred_element_type=F32
    )

    @pl.when(core == 0)
    def _():
        put(gkeep, everything, total[...], narrow)
        put(gsend, everything, second, narrow)

    @pl.when(core == 1)
    def _():
        put(gkeep, everything, second, narrow)
        put(gsend, everything, total[...], narrow)

    for half, ref in enumerate((keep, send)):
        mine = mix[half * chunk : (half + 1) * chunk, :]
        value = jnp.dot(mine, w2[...], preferred_element_type=F32)
        put(ref, pl.ds(0, chunk), value, narrow)


def last_kernel(mine, other, grad_first, grad_second):
    core = lax.axis_index("dom") & 1

    @pl.when(core == 0)
    def _():
        grad_first[...] = mine[...]
        grad_second[...] = other[...]

    @pl.when(core == 1)
    def _():
        grad_first[...] = other[...]
        grad_second[...] = mine[...]


def any_spec():
    return pl.BlockSpec(memory_space=pl.ANY)


def vmem():
    return pl.BlockSpec(memory_space=pltpu.VMEM)


def smem():
    return pl.BlockSpec(memory_space=pltpu.SMEM)


def in_hbm(value):
    return pltpu.with_memory_space_constraint(value, pltpu.HBM)


def call(kernel, out, out_specs, in_specs, scratch, args, flops, grant=16):
    return pl.pallas_call(
        kernel,
        out_shape=tuple(jax.ShapeDtypeStruct(*o) for o in out),
        in_specs=in_specs,
        out_specs=tuple(out_specs),
        scratch_shapes=scratch,
        compiler_params=pltpu.CompilerParams(vmem_limit_bytes=grant << 20),
        cost_estimate=pl.CostEstimate(
            flops=flops, bytes_accessed=4 << 20, transcendentals=0
        ),
    )(*args)


def work(feats, w_first, w_second, block_cols, block_count, block_vals, cotangent):
    nd, nc = lax.axis_size("dom"), lax.axis_size("col")
    col = lax.axis_index("col")
    rows, narrow = feats.shape
    nb, slots = block_vals.shape[:2]
    width = narrow * nc
    blocks = nd // 2 * rows
    lists = 2 * nb * (slots + GROUP)
    dense = 2 * 2 * nb * slots * BLK * BLK * width // 2

    pieces = 1 if narrow % LANES else nc
    chunks = gather(widen(feats), pieces)
    cot_own = [widen(cotangent)]
    for cx in range(1, pieces):
        cot_own.append(swap(cotangent, "col", cx))
    v_far = swap(block_vals, "dom", 1)
    cols = (
        block_cols, block_count, swap(block_cols, "dom", 1), swap(block_count, "dom", 1)
    )
    cot_far = [swap(piece, "dom", 1) for piece in cot_own]

    lk, lx, ln, v_own = call(
        functools.partial(lists_kernel, nb, slots, blocks // BLK),
        [
            ((lists,), jnp.int32),
            ((lists,), jnp.int32),
            ((2 * nb,), jnp.int32),
            (block_vals.shape, BF16),
        ],
        [smem()] * 3 + [vmem()],
        [smem()] * 4 + [any_spec()],
        [pltpu.SemaphoreType.DMA],
        (*cols, in_hbm(block_vals)),
        1 << 20,
    )

    counts = tuple(len(g) for g in chunks)
    if pieces > 1:
        chunks[0][0] = in_hbm(feats)
    keep, send = call(
        functools.partial(first_kernel, nb, slots, counts, narrow),
        [((rows, width), F32), ((rows, width), BF16)],
        [vmem()] * 2,
        [smem()] * 3 + [vmem()] * 2 + [any_spec()] * sum(counts),
        [
            pltpu.VMEM((blocks + BLK, width), BF16),
            pltpu.SemaphoreType.DMA((sum(counts),)),
        ],
        (lk, lx, ln, v_own, v_far, *[p for g in chunks for p in g]),
        dense,
    )

    def back(first, vals, pieces):
        n = len(pieces)
        return call(
            functools.partial(back_kernel, nb, slots, (n,), first),
            [((blocks + BLK, width), F32)],
            [vmem()],
            [smem()] * 3 + [vmem()] * 2 + [any_spec()] * n,
            [
                pltpu.VMEM((rows, width), BF16),
                pltpu.VMEM((rows, width), BF16),
                pltpu.SemaphoreType.DMA((n,)),
            ],
            (lk, lx, ln, w_second, vals, *pieces),
            dense // 2,
        )[0]

    hg = back(0, v_own, cot_own)
    hg_far = back(nb, v_far, cot_far)

    def feature(value, cx):
        axis = value.ndim - 1
        if narrow % LANES:
            at = (col ^ cx) * narrow
            return lax.dynamic_slice_in_dim(value, at, narrow, axis)
        return lax.slice_in_dim(value, cx * narrow, (cx + 1) * narrow, axis=axis)

    def reduce_rows(keep, send):
        part = keep + swap(send, "dom", 1).astype(F32)
        total = feature(part, 0)
        for cx in range(1, nc):
            piece = feature(part, cx).astype(BF16)
            total = total + swap(piece, "col", cx).astype(F32)
        return total

    agg = reduce_rows(keep, send).astype(BF16)

    chunks = gather(widen(agg), pieces)
    groups = chunks + [cot_own, cot_far]
    counts = tuple(len(g) for g in groups)
    keep, send, gkeep, gsend = call(
        functools.partial(second_kernel, nb, slots, counts, narrow),
        [
            ((rows, width), F32),
            ((rows, width), BF16),
            ((width, width), F32),
            ((width, width), BF16),
        ],
        [vmem()] * 4,
        [smem()] * 3 + [vmem()] * 6 + [any_spec()] * sum(counts),
        [
            pltpu.VMEM((blocks, width), BF16),
            pltpu.VMEM((blocks + BLK, width), BF16),
            pltpu.VMEM((2 * rows, width), BF16),
            pltpu.VMEM((2 * rows, width), BF16),
            pltpu.VMEM((width, width), F32),
            pltpu.SemaphoreType.DMA((sum(counts),)),
        ],
        (lk, lx, ln, w_first, w_second, v_own, v_far, hg, hg_far)
        + tuple(p for g in groups for p in g),
        4 * dense,
    )

    part = gkeep + swap(gsend, "dom", 1).astype(F32)
    mine = feature(part, 0)
    for cx in range(1, nc):
        piece = swap(feature(part, cx).astype(BF16), "col", cx)
        mine = mine + piece.astype(F32)
    bit = 2
    while bit < nd:
        half = mine.astype(BF16)
        mine = half.astype(F32) + swap(half, "dom", bit).astype(F32)
        bit *= 2
    other = swap(mine, "dom", 1)
    grad_first, grad_second = call(
        last_kernel,
        [((width, narrow), F32)] * 2,
        [vmem()] * 2,
        [vmem()] * 2,
        [],
        (mine, other),
        width * narrow,
    )
    output = reduce_rows(keep, send)
    return output, grad_first, grad_second


def solution(mesh):
    in_specs = (
        P("dom", "col"),
        P(),
        P(),
        P("dom", None),
        P("dom"),
        P("dom", "col", None, None),
        P("dom", "col"),
    )
    out_specs = (P("dom", "col"), P(None, "col"), P(None, "col"))
    return jax.shard_map(work, mesh=mesh, in_specs=in_specs, out_specs=out_specs, check_vma=False)
```

profile of v0, /device:TPU:0, one launch (start us, length us, event | category | flops | bytes accessed | tf_op | source)
XLA Modules:
  0.0 110.3 jit_solution(18409095648511857224)
XLA Ops:
  1.2 3.6 %collective-permute-start.13 = (bf16[512,128]{1,0:T(8,128)(2,1)}, bf16[512,128]{1,0:T(8,128)(2,1)S(1)}, u32[]{:S(2)}, u32[]{:S(2)}) collective-permute-start(bf16[512,128]{1,0:T(8,128)(2,1)} %refs_0_.5), channel_id=1, source_target_pairs={{0,16},{2,18},{4,20},{6,22},{8,24},{10,26},{12,28},{14,30},{16,0},... | collective-permute-start | bytes 393224 | tf_op jit(solution)/shard_map/ppermute | solution.py:20
  4.8 1.6 %collective-permute-start.9 = (bf16[512,128]{1,0:T(8,128)(2,1)}, bf16[512,128]{1,0:T(8,128)(2,1)S(1)}, u32[]{:S(2)}, u32[]{:S(2)}) collective-permute-start(bf16[512,128]{1,0:T(8,128)(2,1)} %refs_0_.5), channel_id=1, source_target_pairs={{0,8},{2,10},{4,12},{6,14},{8,0},{10,2},{12,4},{14,6},{16,24},{18,... | collective-permute-start | bytes 393224 | tf_op jit(solution)/shard_map/ppermute | solution.py:20
  6.4 1.5 %collective-permute-start.7 = (bf16[512,128]{1,0:T(8,128)(2,1)}, bf16[512,128]{1,0:T(8,128)(2,1)S(1)}, u32[]{:S(2)}, u32[]{:S(2)}) collective-permute-start(bf16[512,128]{1,0:T(8,128)(2,1)} %refs_0_.5), channel_id=1, source_target_pairs={{0,4},{2,6},{4,0},{6,2},{8,12},{10,14},{12,8},{14,10},{16,20},{18,... | collective-permute-start | bytes 393224 | tf_op jit(solution)/shard_map/ppermute | solution.py:20
  10.6 1.5 %collective-permute-start.6 = (bf16[512,128]{1,0:T(8,128)(2,1)}, bf16[512,128]{1,0:T(8,128)(2,1)S(1)}, u32[]{:S(2)}, u32[]{:S(2)}) collective-permute-start(bf16[512,128]{1,0:T(8,128)(2,1)} %refs_0_.5), channel_id=1, source_target_pairs={{0,1},{1,0},{2,3},{3,2},{4,5},{5,4},{6,7},{7,6},{8,9},{9,8},{10,11... | collective-permute-start | bytes 393224 | tf_op jit(solution)/shard_map/ppermute | solution.py:20
  12.1 3.4 %collective-permute-start.17 = (bf16[512,128]{1,0:T(8,128)(2,1)}, bf16[512,128]{1,0:T(8,128)(2,1)S(1)}, u32[]{:S(2)}, u32[]{:S(2)}) collective-permute-start(bf16[512,128]{1,0:T(8,128)(2,1)} %refs_0_.5), channel_id=1, source_target_pairs={{0,24},{2,26},{4,28},{6,30},{8,16},{10,18},{12,20},{14,22},{16,8},... | collective-permute-start | bytes 393224 | tf_op jit(solution)/shard_map/ppermute | solution.py:20
  15.5 1.5 %collective-permute-start.15 = (bf16[512,128]{1,0:T(8,128)(2,1)S(1)}, bf16[512,128]{1,0:T(8,128)(2,1)S(1)}, u32[]{:S(2)}, u32[]{:S(2)}) collective-permute-start(bf16[512,128]{1,0:T(8,128)(2,1)S(1)} %collective-permute-done.13.refs_8_), channel_id=1, source_target_pairs={{0,4},{2,6},{4,0},{6,2},{8,12},{10,14},{12,8},{14,10},{16,20},{18,... | collective-permute-start | bytes 393224 | tf_op jit(solution)/shard_map/ppermute | solution.py:20
  17.0 1.5 %collective-permute-start.14 = (bf16[512,128]{1,0:T(8,128)(2,1)S(1)}, bf16[512,128]{1,0:T(8,128)(2,1)S(1)}, u32[]{:S(2)}, u32[]{:S(2)}) collective-permute-start(bf16[512,128]{1,0:T(8,128)(2,1)S(1)} %collective-permute-done.13.refs_8_), channel_id=1, source_target_pairs={{0,1},{1,0},{2,3},{3,2},{4,5},{5,4},{6,7},{7,6},{8,9},{9,8},{10,11... | collective-permute-start | bytes 393224 | tf_op jit(solution)/shard_map/ppermute | solution.py:20
  19.5 1.5 %collective-permute-start.10 = (bf16[512,128]{1,0:T(8,128)(2,1)S(1)}, bf16[512,128]{1,0:T(8,128)(2,1)S(1)}, u32[]{:S(2)}, u32[]{:S(2)}) collective-permute-start(bf16[512,128]{1,0:T(8,128)(2,1)S(1)} %collective-permute-done.9.refs_4_), channel_id=1, source_target_pairs={{0,1},{1,0},{2,3},{3,2},{4,5},{5,4},{6,7},{7,6},{8,9},{9,8},{10,11... | collective-permute-start | bytes 393224 | tf_op jit(solution)/shard_map/ppermute | solution.py:20
  21.1 2.3 %collective-permute-start.8 = (bf16[512,128]{1,0:T(8,128)(2,1)S(1)}, bf16[512,128]{1,0:T(8,128)(2,1)S(1)}, u32[]{:S(2)}, u32[]{:S(2)}) collective-permute-start(bf16[512,128]{1,0:T(8,128)(2,1)S(1)} %collective-permute-done.6.refs_1_), channel_id=1, source_target_pairs={{0,4},{2,6},{4,0},{6,2},{8,12},{10,14},{12,8},{14,10},{16,20},{18,... | collective-permute-start | bytes 393224 | tf_op jit(solution)/shard_map/ppermute | solution.py:20
  24.6 1.6 %collective-permute-start.18 = (bf16[512,128]{1,0:T(8,128)(2,1)S(1)}, bf16[512,128]{1,0:T(8,128)(2,1)S(1)}, u32[]{:S(2)}, u32[]{:S(2)}) collective-permute-start(bf16[512,128]{1,0:T(8,128)(2,1)S(1)} %collective-permute-done.17.refs_12_), channel_id=1, source_target_pairs={{0,1},{1,0},{2,3},{3,2},{4,5},{5,4},{6,7},{7,6},{8,9},{9,8},{10,11... | collective-permute-start | bytes 393224 | tf_op jit(solution)/shard_map/ppermute | solution.py:20
  26.2 1.5 %collective-permute-start.16 = (bf16[512,128]{1,0:T(8,128)(2,1)S(1)}, bf16[512,128]{1,0:T(8,128)(2,1)S(1)}, u32[]{:S(2)}, u32[]{:S(2)}) collective-permute-start(bf16[512,128]{1,0:T(8,128)(2,1)S(1)} %collective-permute-done.14.refs_9_), channel_id=1, source_target_pairs={{0,4},{2,6},{4,0},{6,2},{8,12},{10,14},{12,8},{14,10},{16,20},{18,... | collective-permute-start | bytes 393224 | tf_op jit(solution)/shard_map/ppermute | solution.py:20
  27.7 2.1 %collective-permute-start.12 = (bf16[512,128]{1,0:T(8,128)(2,1)S(1)}, bf16[512,128]{1,0:T(8,128)(2,1)S(1)}, u32[]{:S(2)}, u32[]{:S(2)}) collective-permute-start(bf16[512,128]{1,0:T(8,128)(2,1)S(1)} %collective-permute-done.11.refs_6_), channel_id=1, source_target_pairs={{0,1},{1,0},{2,3},{3,2},{4,5},{5,4},{6,7},{7,6},{8,9},{9,8},{10,11... | collective-permute-start | bytes 393224 | tf_op jit(solution)/shard_map/ppermute | solution.py:20
  30.5 1.5 %collective-permute-start.20 = (bf16[512,128]{1,0:T(8,128)(2,1)S(1)}, bf16[512,128]{1,0:T(8,128)(2,1)S(1)}, u32[]{:S(2)}, u32[]{:S(2)}) collective-permute-start(bf16[512,128]{1,0:T(8,128)(2,1)S(1)} %collective-permute-done.19.refs_14_), channel_id=1, source_target_pairs={{0,1},{1,0},{2,3},{3,2},{4,5},{5,4},{6,7},{7,6},{8,9},{9,8},{10,11... | collective-permute-start | bytes 393224 | tf_op jit(solution)/shard_map/ppermute | solution.py:20
  33.4 2.8 %shard_map.94 = (s32[160]{0:T(256)S(1)}, s32[160]{0:T(256)S(1)}, s32[8]{0:T(128)S(1)}, bf16[4,16,128,128]{3,2,1,0:T(8,128)(2,1)S(1)}) custom-call(s32[4,32]{1,0:T(4,128)S(1)} %copy-done.3, s32[4]{0:T(128)S(1)} %copy-done.4, s32[4,32]{1,0:T(4,128)S(1)} %collective-permute-done.refs_2_, s32[4]{0:T(128)S(1)} %collective-permute-done.1.refs_3_, ...), custom_call_target="tpu_custom_call" | custom-call | flops 1048576 | bytes 4194304 | tf_op jit(solution)/shard_map/pallas_call | solution.py:275
  36.3 4.5 %shard_map.97 = (f32[512,256]{1,0:T(8,128)S(1)}, bf16[512,256]{1,0:T(8,128)(2,1)S(1)}) custom-call(s32[160]{0:T(256)S(1)} %get-tuple-element.15.lk, s32[160]{0:T(256)S(1)} %get-tuple-element.16.lx, s32[8]{0:T(128)S(1)} %get-tuple-element.17.ln, bf16[4,16,128,128]{3,2,1,0:T(8,128)(2,1)S(1)} %get-tuple-element.18.vals.v_own, ...), custom_call_target="tpu_custom_call" | custom-call | flops 536870912 | bytes 4194304 | tf_op jit(solution)/shard_map/pallas_call | solution.py:275
  43.2 4.2 %collective-permute-done.3.refs_1_.refs_17_ = bf16[512,128]{1,0:T(8,128)(2,1)S(1)} collective-permute-done((bf16[512,128]{1,0:T(8,128)(2,1)S(1)}, bf16[512,128]{1,0:T(8,128)(2,1)S(1)}, u32[]{:S(2)}, u32[]{:S(2)}) %collective-permute-start.3) | collective-permute-done | bytes 131104 | tf_op jit(solution)/shard_map/ppermute | solution.py:20
  47.4 2.3 %collective-permute-done.22 = bf16[512,128]{1,0:T(8,128)(2,1)S(1)} collective-permute-done((bf16[512,128]{1,0:T(8,128)(2,1)S(1)}, bf16[512,128]{1,0:T(8,128)(2,1)S(1)}, u32[]{:S(2)}, u32[]{:S(2)}) %collective-permute-start.22) | collective-permute-done | bytes 131104 | tf_op jit(solution)/shard_map/ppermute | solution.py:20
  49.7 2.0 %collective-permute-start.34 = (bf16[512,128]{1,0:T(8,128)(2,1)S(1)}, bf16[512,128]{1,0:T(8,128)(2,1)S(1)}, u32[]{:S(2)}, u32[]{:S(2)}) collective-permute-start(bf16[512,128]{1,0:T(8,128)(2,1)S(1)} %fusion.refs_0_), channel_id=1, source_target_pairs={{0,24},{2,26},{4,28},{6,30},{8,16},{10,18},{12,20},{14,22},{16,8},... | collective-permute-start | bytes 393224 | tf_op jit(solution)/shard_map/ppermute | solution.py:20
  51.6 2.5 %collective-permute-start.26 = (bf16[512,128]{1,0:T(8,128)(2,1)S(1)}, bf16[512,128]{1,0:T(8,128)(2,1)S(1)}, u32[]{:S(2)}, u32[]{:S(2)}) collective-permute-start(bf16[512,128]{1,0:T(8,128)(2,1)S(1)} %fusion.refs_0_), channel_id=1, source_target_pairs={{0,8},{2,10},{4,12},{6,14},{8,0},{10,2},{12,4},{14,6},{16,24},{18,... | collective-permute-start | bytes 393224 | tf_op jit(solution)/shard_map/ppermute | solution.py:20
  54.1 2.1 %collective-permute-start.24 = (bf16[512,128]{1,0:T(8,128)(2,1)S(1)}, bf16[512,128]{1,0:T(8,128)(2,1)S(1)}, u32[]{:S(2)}, u32[]{:S(2)}) collective-permute-start(bf16[512,128]{1,0:T(8,128)(2,1)S(1)} %fusion.refs_0_), channel_id=1, source_target_pairs={{0,4},{2,6},{4,0},{6,2},{8,12},{10,14},{12,8},{14,10},{16,20},{18,... | collective-permute-start | bytes 393224 | tf_op jit(solution)/shard_map/ppermute | solution.py:20
  58.0 2.1 %collective-permute-start.36 = (bf16[512,128]{1,0:T(8,128)(2,1)S(1)}, bf16[512,128]{1,0:T(8,128)(2,1)S(1)}, u32[]{:S(2)}, u32[]{:S(2)}) collective-permute-start(bf16[512,128]{1,0:T(8,128)(2,1)S(1)} %collective-permute-done.34.refs_12_), channel_id=1, source_target_pairs={{0,4},{2,6},{4,0},{6,2},{8,12},{10,14},{12,8},{14,10},{16,20},{18,... | collective-permute-start | bytes 393224 | tf_op jit(solution)/shard_map/ppermute | solution.py:20
  60.1 2.7 %collective-permute-done.30.refs_8_ = bf16[512,128]{1,0:T(8,128)(2,1)S(1)} collective-permute-done((bf16[512,128]{1,0:T(8,128)(2,1)S(1)}, bf16[512,128]{1,0:T(8,128)(2,1)S(1)}, u32[]{:S(2)}, u32[]{:S(2)}) %collective-permute-start.30) | collective-permute-done | bytes 131104 | tf_op jit(solution)/shard_map/ppermute | solution.py:20
  68.7 1.9 %collective-permute-start.25 = (bf16[512,128]{1,0:T(8,128)(2,1)S(1)}, bf16[512,128]{1,0:T(8,128)(2,1)S(1)}, u32[]{:S(2)}, u32[]{:S(2)}) collective-permute-start(bf16[512,128]{1,0:T(8,128)(2,1)S(1)} %collective-permute-done.23.refs_1_), channel_id=1, source_target_pairs={{0,4},{2,6},{4,0},{6,2},{8,12},{10,14},{12,8},{14,10},{16,20},{18,... | collective-permute-start | bytes 393224 | tf_op jit(solution)/shard_map/ppermute | solution.py:20
  71.5 1.9 %collective-permute-start.33 = (bf16[512,128]{1,0:T(8,128)(2,1)S(1)}, bf16[512,128]{1,0:T(8,128)(2,1)S(1)}, u32[]{:S(2)}, u32[]{:S(2)}) collective-permute-start(bf16[512,128]{1,0:T(8,128)(2,1)S(1)} %collective-permute-done.31.refs_9_), channel_id=1, source_target_pairs={{0,4},{2,6},{4,0},{6,2},{8,12},{10,14},{12,8},{14,10},{16,20},{18,... | collective-permute-start | bytes 393224 | tf_op jit(solution)/shard_map/ppermute | solution.py:20
  73.9 3.1 %shard_map.95.hg = f32[4224,256]{1,0:T(8,128)S(1)} custom-call(s32[160]{0:T(256)S(1)} %get-tuple-element.15.lk, s32[160]{0:T(256)S(1)} %get-tuple-element.16.lx, s32[8]{0:T(128)S(1)} %get-tuple-element.17.ln, bf16[256,256]{1,0:T(8,128)(2,1)S(1)} %copy-done, bf16[4,16,128,128]{3,2,1,0:T(8,128)(2,1)S(1)} %get-tuple-element.18.vals.v_own, ...), custom_call_target="tpu_custom_call" | custom-call | flops 268435456 | bytes 4194304 | tf_op jit(solution)/shard_map/pallas_call | solution.py:275
  77.1 3.2 %shard_map.96.hg_far = f32[4224,256]{1,0:T(8,128)S(1)} custom-call(s32[160]{0:T(256)S(1)} %get-tuple-element.15.lk, s32[160]{0:T(256)S(1)} %get-tuple-element.16.lx, s32[8]{0:T(128)S(1)} %get-tuple-element.17.ln, bf16[256,256]{1,0:T(8,128)(2,1)S(1)} %copy-done, bf16[4,16,128,128]{3,2,1,0:T(8,128)(2,1)S(1)} %collective-permute-done.2.vals.v_far, ...), custom_call_target="tpu_custom_call" | custom-call | flops 268435456 | bytes 4194304 | tf_op jit(solution)/shard_map/pallas_call | solution.py:275
  80.3 7.1 %shard_map.98 = (f32[512,256]{1,0:T(8,128)S(1)}, bf16[512,256]{1,0:T(8,128)(2,1)S(1)}, f32[256,256]{1,0:T(8,128)S(1)}, bf16[256,256]{1,0:T(8,128)(2,1)S(1)}) custom-call(s32[160]{0:T(256)S(1)} %get-tuple-element.15.lk, s32[160]{0:T(256)S(1)} %get-tuple-element.16.lx, s32[8]{0:T(128)S(1)} %get-tuple-element.17.ln, bf16[256,256]{1,0:T(8,128)(2,1)S(1)} %copy-done.2, ...), custom_call_target="tpu_custom_call" | custom-call | flops 2147483648 | bytes 4194304 | tf_op jit(solution)/shard_map/pallas_call | solution.py:275
  89.0 4.3 %collective-permute-done.41 = bf16[256,128]{1,0:T(8,128)(2,1)S(1)} collective-permute-done((bf16[256,128]{1,0:T(8,128)(2,1)S(1)}, bf16[256,128]{1,0:T(8,128)(2,1)S(1)}, u32[]{:S(2)}, u32[]{:S(2)}) %collective-permute-start.41) | collective-permute-done | bytes 65568 | tf_op jit(solution)/shard_map/ppermute | solution.py:20
  93.3 2.9 %collective-permute-start.42 = (bf16[256,128]{1,0:T(8,128)(2,1)S(1)}, bf16[256,128]{1,0:T(8,128)(2,1)S(1)}, u32[]{:S(2)}, u32[]{:S(2)}) collective-permute-start(bf16[256,128]{1,0:T(8,128)(2,1)S(1)} %fusion.1), channel_id=1, source_target_pairs={{0,4},{2,6},{4,0},{6,2},{8,12},{10,14},{12,8},{14,10},{16,20},{18,... | collective-permute-start | bytes 196616 | tf_op jit(solution)/shard_map/ppermute | solution.py:20
  96.2 2.2 %collective-permute-done.42 = bf16[256,128]{1,0:T(8,128)(2,1)S(1)} collective-permute-done((bf16[256,128]{1,0:T(8,128)(2,1)S(1)}, bf16[256,128]{1,0:T(8,128)(2,1)S(1)}, u32[]{:S(2)}, u32[]{:S(2)}) %collective-permute-start.42) | collective-permute-done | bytes 65568 | tf_op jit(solution)/shard_map/ppermute | solution.py:20
  98.6 4.2 %collective-permute-done.43 = bf16[256,128]{1,0:T(8,128)(2,1)S(1)} collective-permute-done((bf16[256,128]{1,0:T(8,128)(2,1)S(1)}, bf16[256,128]{1,0:T(8,128)(2,1)S(1)}, u32[]{:S(2)}, u32[]{:S(2)}) %collective-permute-start.43) | collective-permute-done | bytes 65568 | tf_op jit(solution)/shard_map/ppermute | solution.py:20
  103.3 4.9 %collective-permute-done.44 = bf16[256,128]{1,0:T(8,128)(2,1)S(1)} collective-permute-done((bf16[256,128]{1,0:T(8,128)(2,1)S(1)}, bf16[256,128]{1,0:T(8,128)(2,1)S(1)}, u32[]{:S(2)}, u32[]{:S(2)}) %collective-permute-start.44) | collective-permute-done | bytes 65568 | tf_op jit(solution)/shard_map/ppermute | solution.py:20
  (88 shorter events, 23.4 us)
Async XLA Ops:
  0.6 35.6 %collective-permute-start.2 = (bf16[4,16,128,128]{3,2,1,0:T(8,128)(2,1)}, bf16[4,16,128,128]{3,2,1,0:T(8,128)(2,1)S(1)}, u32[]{:S(2)}, u32[]{:S(2)}) collective-permute-start(bf16[4,16,128,128]{3,2,1,0:T(8,128)(2,1)} %refs_4_.1), channel_id=1, source_target_pairs={{0,2},{2,0},{4,6},{6,4},{8,10},{10,8},{12,14},{14,12},{16,18},{18,... | collective-permute-start | bytes 6291464 | tf_op jit(solution)/shard_map/ppermute | solution.py:20
  1.2 10.9 %collective-permute-start.13 = (bf16[512,128]{1,0:T(8,128)(2,1)}, bf16[512,128]{1,0:T(8,128)(2,1)S(1)}, u32[]{:S(2)}, u32[]{:S(2)}) collective-permute-start(bf16[512,128]{1,0:T(8,128)(2,1)} %refs_0_.5), channel_id=1, source_target_pairs={{0,16},{2,18},{4,20},{6,22},{8,24},{10,26},{12,28},{14,30},{16,0},... | collective-permute-start | bytes 393224 | tf_op jit(solution)/shard_map/ppermute | solution.py:20
  4.8 10.7 %collective-permute-start.9 = (bf16[512,128]{1,0:T(8,128)(2,1)}, bf16[512,128]{1,0:T(8,128)(2,1)S(1)}, u32[]{:S(2)}, u32[]{:S(2)}) collective-permute-start(bf16[512,128]{1,0:T(8,128)(2,1)} %refs_0_.5), channel_id=1, source_target_pairs={{0,8},{2,10},{4,12},{6,14},{8,0},{10,2},{12,4},{14,6},{16,24},{18,... | collective-permute-start | bytes 393224 | tf_op jit(solution)/shard_map/ppermute | solution.py:20
  6.4 10.6 %collective-permute-start.7 = (bf16[512,128]{1,0:T(8,128)(2,1)}, bf16[512,128]{1,0:T(8,128)(2,1)S(1)}, u32[]{:S(2)}, u32[]{:S(2)}) collective-permute-start(bf16[512,128]{1,0:T(8,128)(2,1)} %refs_0_.5), channel_id=1, source_target_pairs={{0,4},{2,6},{4,0},{6,2},{8,12},{10,14},{12,8},{14,10},{16,20},{18,... | collective-permute-start | bytes 393224 | tf_op jit(solution)/shard_map/ppermute | solution.py:20
  10.6 7.9 %collective-permute-start.6 = (bf16[512,128]{1,0:T(8,128)(2,1)}, bf16[512,128]{1,0:T(8,128)(2,1)S(1)}, u32[]{:S(2)}, u32[]{:S(2)}) collective-permute-start(bf16[512,128]{1,0:T(8,128)(2,1)} %refs_0_.5), channel_id=1, source_target_pairs={{0,1},{1,0},{2,3},{3,2},{4,5},{5,4},{6,7},{7,6},{8,9},{9,8},{10,11... | collective-permute-start | bytes 393224 | tf_op jit(solution)/shard_map/ppermute | solution.py:20
  12.1 7.4 %collective-permute-start.17 = (bf16[512,128]{1,0:T(8,128)(2,1)}, bf16[512,128]{1,0:T(8,128)(2,1)S(1)}, u32[]{:S(2)}, u32[]{:S(2)}) collective-permute-start(bf16[512,128]{1,0:T(8,128)(2,1)} %refs_0_.5), channel_id=1, source_target_pairs={{0,24},{2,26},{4,28},{6,30},{8,16},{10,18},{12,20},{14,22},{16,8},... | collective-permute-start | bytes 393224 | tf_op jit(solution)/shard_map/ppermute | solution.py:20
  17.0 6.4 %collective-permute-start.14 = (bf16[512,128]{1,0:T(8,128)(2,1)S(1)}, bf16[512,128]{1,0:T(8,128)(2,1)S(1)}, u32[]{:S(2)}, u32[]{:S(2)}) collective-permute-start(bf16[512,128]{1,0:T(8,128)(2,1)S(1)} %collective-permute-done.13.refs_8_), channel_id=1, source_target_pairs={{0,1},{1,0},{2,3},{3,2},{4,5},{5,4},{6,7},{7,6},{8,9},{9,8},{10,11... | collective-permute-start | bytes 393224 | tf_op jit(solution)/shard_map/ppermute | solution.py:20
  18.5 6.0 %collective-permute-start.11 = (bf16[512,128]{1,0:T(8,128)(2,1)S(1)}, bf16[512,128]{1,0:T(8,128)(2,1)S(1)}, u32[]{:S(2)}, u32[]{:S(2)}) collective-permute-start(bf16[512,128]{1,0:T(8,128)(2,1)S(1)} %collective-permute-done.9.refs_4_), channel_id=1, source_target_pairs={{0,4},{2,6},{4,0},{6,2},{8,12},{10,14},{12,8},{14,10},{16,20},{18,... | collective-permute-start | bytes 393224 | tf_op jit(solution)/shard_map/ppermute | solution.py:20
  19.5 6.7 %collective-permute-start.10 = (bf16[512,128]{1,0:T(8,128)(2,1)S(1)}, bf16[512,128]{1,0:T(8,128)(2,1)S(1)}, u32[]{:S(2)}, u32[]{:S(2)}) collective-permute-start(bf16[512,128]{1,0:T(8,128)(2,1)S(1)} %collective-permute-done.9.refs_4_), channel_id=1, source_target_pairs={{0,1},{1,0},{2,3},{3,2},{4,5},{5,4},{6,7},{7,6},{8,9},{9,8},{10,11... | collective-permute-start | bytes 393224 | tf_op jit(solution)/shard_map/ppermute | solution.py:20
  21.1 6.6 %collective-permute-start.8 = (bf16[512,128]{1,0:T(8,128)(2,1)S(1)}, bf16[512,128]{1,0:T(8,128)(2,1)S(1)}, u32[]{:S(2)}, u32[]{:S(2)}) collective-permute-start(bf16[512,128]{1,0:T(8,128)(2,1)S(1)} %collective-permute-done.6.refs_1_), channel_id=1, source_target_pairs={{0,4},{2,6},{4,0},{6,2},{8,12},{10,14},{12,8},{14,10},{16,20},{18,... | collective-permute-start | bytes 393224 | tf_op jit(solution)/shard_map/ppermute | solution.py:20
  23.4 7.2 %collective-permute-start.19 = (bf16[512,128]{1,0:T(8,128)(2,1)S(1)}, bf16[512,128]{1,0:T(8,128)(2,1)S(1)}, u32[]{:S(2)}, u32[]{:S(2)}) collective-permute-start(bf16[512,128]{1,0:T(8,128)(2,1)S(1)} %collective-permute-done.17.refs_12_), channel_id=1, source_target_pairs={{0,4},{2,6},{4,0},{6,2},{8,12},{10,14},{12,8},{14,10},{16,20},{18,... | collective-permute-start | bytes 393224 | tf_op jit(solution)/shard_map/ppermute | solution.py:20
  24.6 11.7 %collective-permute-start.18 = (bf16[512,128]{1,0:T(8,128)(2,1)S(1)}, bf16[512,128]{1,0:T(8,128)(2,1)S(1)}, u32[]{:S(2)}, u32[]{:S(2)}) collective-permute-start(bf16[512,128]{1,0:T(8,128)(2,1)S(1)} %collective-permute-done.17.refs_12_), channel_id=1, source_target_pairs={{0,1},{1,0},{2,3},{3,2},{4,5},{5,4},{6,7},{7,6},{8,9},{9,8},{10,11... | collective-permute-start | bytes 393224 | tf_op jit(solution)/shard_map/ppermute | solution.py:20
  26.2 10.0 %collective-permute-start.16 = (bf16[512,128]{1,0:T(8,128)(2,1)S(1)}, bf16[512,128]{1,0:T(8,128)(2,1)S(1)}, u32[]{:S(2)}, u32[]{:S(2)}) collective-permute-start(bf16[512,128]{1,0:T(8,128)(2,1)S(1)} %collective-permute-done.14.refs_9_), channel_id=1, source_target_pairs={{0,4},{2,6},{4,0},{6,2},{8,12},{10,14},{12,8},{14,10},{16,20},{18,... | collective-permute-start | bytes 393224 | tf_op jit(solution)/shard_map/ppermute | solution.py:20
  27.7 8.5 %collective-permute-start.12 = (bf16[512,128]{1,0:T(8,128)(2,1)S(1)}, bf16[512,128]{1,0:T(8,128)(2,1)S(1)}, u32[]{:S(2)}, u32[]{:S(2)}) collective-permute-start(bf16[512,128]{1,0:T(8,128)(2,1)S(1)} %collective-permute-done.11.refs_6_), channel_id=1, source_target_pairs={{0,1},{1,0},{2,3},{3,2},{4,5},{5,4},{6,7},{7,6},{8,9},{9,8},{10,11... | collective-permute-start | bytes 393224 | tf_op jit(solution)/shard_map/ppermute | solution.py:20
  40.9 6.4 %collective-permute-start.3 = (bf16[512,128]{1,0:T(8,128)(2,1)S(1)}, bf16[512,128]{1,0:T(8,128)(2,1)S(1)}, u32[]{:S(2)}, u32[]{:S(2)}) collective-permute-start(bf16[512,128]{1,0:T(8,128)(2,1)S(1)} %copy-done.1), channel_id=1, source_target_pairs={{0,1},{1,0},{2,3},{3,2},{4,5},{5,4},{6,7},{7,6},{8,9},{9,8},{10,11... | collective-permute-start | bytes 393224 | tf_op jit(solution)/shard_map/ppermute | solution.py:20
  42.6 7.1 %collective-permute-start.22 = (bf16[512,128]{1,0:T(8,128)(2,1)S(1)}, bf16[512,128]{1,0:T(8,128)(2,1)S(1)}, u32[]{:S(2)}, u32[]{:S(2)}) collective-permute-start(bf16[512,128]{1,0:T(8,128)(2,1)S(1)} %slice.44), channel_id=1, source_target_pairs={{0,1},{1,0},{2,3},{3,2},{4,5},{5,4},{6,7},{7,6},{8,9},{9,8},{10,11... | collective-permute-start | bytes 393224 | tf_op jit(solution)/shard_map/ppermute | solution.py:20
  43.2 10.9 %collective-permute-start.4 = (bf16[512,128]{1,0:T(8,128)(2,1)S(1)}, bf16[512,128]{1,0:T(8,128)(2,1)S(1)}, u32[]{:S(2)}, u32[]{:S(2)}) collective-permute-start(bf16[512,128]{1,0:T(8,128)(2,1)S(1)} %copy-done.1), channel_id=1, source_target_pairs={{0,2},{2,0},{4,6},{6,4},{8,10},{10,8},{12,14},{14,12},{16,18},{18,... | collective-permute-start | bytes 393224 | tf_op jit(solution)/shard_map/ppermute | solution.py:20
  47.4 8.8 %collective-permute-start.5 = (bf16[512,128]{1,0:T(8,128)(2,1)S(1)}, bf16[512,128]{1,0:T(8,128)(2,1)S(1)}, u32[]{:S(2)}, u32[]{:S(2)}) collective-permute-start(bf16[512,128]{1,0:T(8,128)(2,1)S(1)} %collective-permute-done.3.refs_1_.refs_17_), channel_id=1, source_target_pairs={{0,2},{2,0},{4,6},{6,4},{8,10},{10,8},{12,14},{14,12},{16,18},{18,... | collective-permute-start | bytes 393224 | tf_op jit(solution)/shard_map/ppermute | solution.py:20
  49.7 8.3 %collective-permute-start.34 = (bf16[512,128]{1,0:T(8,128)(2,1)S(1)}, bf16[512,128]{1,0:T(8,128)(2,1)S(1)}, u32[]{:S(2)}, u32[]{:S(2)}) collective-permute-start(bf16[512,128]{1,0:T(8,128)(2,1)S(1)} %fusion.refs_0_), channel_id=1, source_target_pairs={{0,24},{2,26},{4,28},{6,30},{8,16},{10,18},{12,20},{14,22},{16,8},... | collective-permute-start | bytes 393224 | tf_op jit(solution)/shard_map/ppermute | solution.py:20
  51.6 11.1 %collective-permute-start.30 = (bf16[512,128]{1,0:T(8,128)(2,1)S(1)}, bf16[512,128]{1,0:T(8,128)(2,1)S(1)}, u32[]{:S(2)}, u32[]{:S(2)}) collective-permute-start(bf16[512,128]{1,0:T(8,128)(2,1)S(1)} %fusion.refs_0_), channel_id=1, source_target_pairs={{0,16},{2,18},{4,20},{6,22},{8,24},{10,26},{12,28},{14,30},{16,0},... | collective-permute-start | bytes 393224 | tf_op jit(solution)/shard_map/ppermute | solution.py:20
  51.6 11.7 %collective-permute-start.26 = (bf16[512,128]{1,0:T(8,128)(2,1)S(1)}, bf16[512,128]{1,0:T(8,128)(2,1)S(1)}, u32[]{:S(2)}, u32[]{:S(2)}) collective-permute-start(bf16[512,128]{1,0:T(8,128)(2,1)S(1)} %fusion.refs_0_), channel_id=1, source_target_pairs={{0,8},{2,10},{4,12},{6,14},{8,0},{10,2},{12,4},{14,6},{16,24},{18,... | collective-permute-start | bytes 393224 | tf_op jit(solution)/shard_map/ppermute | solution.py:20
  54.1 10.6 %collective-permute-start.24 = (bf16[512,128]{1,0:T(8,128)(2,1)S(1)}, bf16[512,128]{1,0:T(8,128)(2,1)S(1)}, u32[]{:S(2)}, u32[]{:S(2)}) collective-permute-start(bf16[512,128]{1,0:T(8,128)(2,1)S(1)} %fusion.refs_0_), channel_id=1, source_target_pairs={{0,4},{2,6},{4,0},{6,2},{8,12},{10,14},{12,8},{14,10},{16,20},{18,... | collective-permute-start | bytes 393224 | tf_op jit(solution)/shard_map/ppermute | solution.py:20
  56.2 10.0 %collective-permute-start.23 = (bf16[512,128]{1,0:T(8,128)(2,1)S(1)}, bf16[512,128]{1,0:T(8,128)(2,1)S(1)}, u32[]{:S(2)}, u32[]{:S(2)}) collective-permute-start(bf16[512,128]{1,0:T(8,128)(2,1)S(1)} %fusion.refs_0_), channel_id=1, source_target_pairs={{0,1},{1,0},{2,3},{3,2},{4,5},{5,4},{6,7},{7,6},{8,9},{9,8},{10,11... | collective-permute-start | bytes 393224 | tf_op jit(solution)/shard_map/ppermute | solution.py:20
  58.0 8.9 %collective-permute-start.36 = (bf16[512,128]{1,0:T(8,128)(2,1)S(1)}, bf16[512,128]{1,0:T(8,128)(2,1)S(1)}, u32[]{:S(2)}, u32[]{:S(2)}) collective-permute-start(bf16[512,128]{1,0:T(8,128)(2,1)S(1)} %collective-permute-done.34.refs_12_), channel_id=1, source_target_pairs={{0,4},{2,6},{4,0},{6,2},{8,12},{10,14},{12,8},{14,10},{16,20},{18,... | collective-permute-start | bytes 393224 | tf_op jit(solution)/shard_map/ppermute | solution.py:20
  63.3 7.2 %collective-permute-start.32 = (bf16[512,128]{1,0:T(8,128)(2,1)S(1)}, bf16[512,128]{1,0:T(8,128)(2,1)S(1)}, u32[]{:S(2)}, u32[]{:S(2)}) collective-permute-start(bf16[512,128]{1,0:T(8,128)(2,1)S(1)} %collective-permute-done.30.refs_8_), channel_id=1, source_target_pairs={{0,4},{2,6},{4,0},{6,2},{8,12},{10,14},{12,8},{14,10},{16,20},{18,... | collective-permute-start | bytes 393224 | tf_op jit(solution)/shard_map/ppermute | solution.py:20
  64.8 6.7 %collective-permute-start.31 = (bf16[512,128]{1,0:T(8,128)(2,1)S(1)}, bf16[512,128]{1,0:T(8,128)(2,1)S(1)}, u32[]{:S(2)}, u32[]{:S(2)}) collective-permute-start(bf16[512,128]{1,0:T(8,128)(2,1)S(1)} %collective-permute-done.30.refs_8_), channel_id=1, source_target_pairs={{0,1},{1,0},{2,3},{3,2},{4,5},{5,4},{6,7},{7,6},{8,9},{9,8},{10,11... | collective-permute-start | bytes 393224 | tf_op jit(solution)/shard_map/ppermute | solution.py:20
  66.2 7.1 %collective-permute-start.28 = (bf16[512,128]{1,0:T(8,128)(2,1)S(1)}, bf16[512,128]{1,0:T(8,128)(2,1)S(1)}, u32[]{:S(2)}, u32[]{:S(2)}) collective-permute-start(bf16[512,128]{1,0:T(8,128)(2,1)S(1)} %collective-permute-done.26.refs_4_), channel_id=1, source_target_pairs={{0,4},{2,6},{4,0},{6,2},{8,12},{10,14},{12,8},{14,10},{16,20},{18,... | collective-permute-start | bytes 393224 | tf_op jit(solution)/shard_map/ppermute | solution.py:20
  66.8 13.4 %collective-permute-start.27 = (bf16[512,128]{1,0:T(8,128)(2,1)S(1)}, bf16[512,128]{1,0:T(8,128)(2,1)S(1)}, u32[]{:S(2)}, u32[]{:S(2)}) collective-permute-start(bf16[512,128]{1,0:T(8,128)(2,1)S(1)} %collective-permute-done.26.refs_4_), channel_id=1, source_target_pairs={{0,1},{1,0},{2,3},{3,2},{4,5},{5,4},{6,7},{7,6},{8,9},{9,8},{10,11... | collective-permute-start | bytes 393224 | tf_op jit(solution)/shard_map/ppermute | solution.py:20
  68.7 11.6 %collective-permute-start.25 = (bf16[512,128]{1,0:T(8,128)(2,1)S(1)}, bf16[512,128]{1,0:T(8,128)(2,1)S(1)}, u32[]{:S(2)}, u32[]{:S(2)}) collective-permute-start(bf16[512,128]{1,0:T(8,128)(2,1)S(1)} %collective-permute-done.23.refs_1_), channel_id=1, source_target_pairs={{0,4},{2,6},{4,0},{6,2},{8,12},{10,14},{12,8},{14,10},{16,20},{18,... | collective-permute-start | bytes 393224 | tf_op jit(solution)/shard_map/ppermute | solution.py:20
  70.6 9.7 %collective-permute-start.37 = (bf16[512,128]{1,0:T(8,128)(2,1)S(1)}, bf16[512,128]{1,0:T(8,128)(2,1)S(1)}, u32[]{:S(2)}, u32[]{:S(2)}) collective-permute-start(bf16[512,128]{1,0:T(8,128)(2,1)S(1)} %collective-permute-done.36.refs_14_), channel_id=1, source_target_pairs={{0,1},{1,0},{2,3},{3,2},{4,5},{5,4},{6,7},{7,6},{8,9},{9,8},{10,11... | collective-permute-start | bytes 393224 | tf_op jit(solution)/shard_map/ppermute | solution.py:20
  71.5 8.8 %collective-permute-start.33 = (bf16[512,128]{1,0:T(8,128)(2,1)S(1)}, bf16[512,128]{1,0:T(8,128)(2,1)S(1)}, u32[]{:S(2)}, u32[]{:S(2)}) collective-permute-start(bf16[512,128]{1,0:T(8,128)(2,1)S(1)} %collective-permute-done.31.refs_9_), channel_id=1, source_target_pairs={{0,4},{2,6},{4,0},{6,2},{8,12},{10,14},{12,8},{14,10},{16,20},{18,... | collective-permute-start | bytes 393224 | tf_op jit(solution)/shard_map/ppermute | solution.py:20
  73.4 6.9 %collective-permute-start.29 = (bf16[512,128]{1,0:T(8,128)(2,1)S(1)}, bf16[512,128]{1,0:T(8,128)(2,1)S(1)}, u32[]{:S(2)}, u32[]{:S(2)}) collective-permute-start(bf16[512,128]{1,0:T(8,128)(2,1)S(1)} %collective-permute-done.28.refs_6_), channel_id=1, source_target_pairs={{0,1},{1,0},{2,3},{3,2},{4,5},{5,4},{6,7},{7,6},{8,9},{9,8},{10,11... | collective-permute-start | bytes 393224 | tf_op jit(solution)/shard_map/ppermute | solution.py:20
  (19 other events, 95.5 us)
where the time goes:
time: 111 us; the launch traced here: 110 us
  starting transfers between devices  49.3 us (44%)
  waiting for transfers between devices  36.2 us (33%)
  Pallas kernels  21.5 us (19%)
  local copies, waits for them, and re-layouts  1.4 us (1%)
    ppermute x46, starting transfers between devices, swap(): return lax.ppermute(value, axis, [(i, i ^ mask) for i in range(size)])  49.3 us
    ppermute x46, waiting for transfers between devices, swap(): return lax.ppermute(value, axis, [(i, i ^ mask) for i in range(size)])  36.2 us
    pallas_call x6, Pallas kernels, call(): pl.pallas_call(kernel, out_shape=tuple((jax.ShapeDtypeStruct(*o) for o in...  21.5 us
  transfers between devices with their start and end apart: 46, of which 18 were waited for; matrix products, arithmetic and copies ran while one was open for 1% of the time, Pallas kernels for 8%

commit v1 on v0

--- a/solution.py
+++ b/solution.py
@@ -9,7 +9,9 @@
 
 
 BLK = 128
-GROUP = 4
+GROUP = 8
+BACK = 4
+PART = 512
 LANES = 128
 F32 = jnp.float32
 BF16 = jnp.bfloat16
@@ -83,32 +85,58 @@
     return out, refs[at:]
 
 
-def tiles(vals, r, lk, at):
-    return jnp.concatenate([vals[r, lk[at + t]] for t in range(GROUP)], axis=1)
+class Part:
+    def __init__(self, ref, start):
+        self.ref, self.start = ref, start
+
+    def __getitem__(self, i):
+        return self.ref[self.start + i]
+
+    def __setitem__(self, i, value):
+        self.ref[self.start + i] = value
+
+
+def plan_size(nb, slots):
+    return 2 * nb * (2 * (slots + GROUP) + 1)
+
+
+def plan_parts(plan, nb, slots):
+    size = 2 * nb * (slots + GROUP)
+    return Part(plan, 0), Part(plan, size), Part(plan, 2 * size)
+
+
+def tiles(vals, r, lk, at, count):
+    return jnp.concatenate([vals[r, lk[at + t]] for t in range(count)], axis=1)
 
 
 def place(lx, at):
     return pl.ds(pl.multiple_of(lx[at] * BLK, BLK), BLK)
 
 
+def row_of(i, size):
+    return pl.ds(pl.multiple_of(i * size, size), size)
+
+
 def back_rows(nb, slots, first, lk, lx, ln, vals, cw, hg):
-    for i in range(nb):
-        grad = cw[i * BLK : (i + 1) * BLK, :]
+    def row(i, carry):
+        grad = cw[row_of(i, BLK), :]
         base = (first + i) * (slots + GROUP)
 
-        def step(g, carry, i=i, grad=grad, base=base):
-            at = base + g * GROUP
+        def step(g, carry):
+            at = base + g * BACK
             prod = lax.dot_general(
-                tiles(vals, i, lk, at),
+                tiles(vals, i, lk, at, BACK),
                 grad,
                 (((0,), (0,)), ((), ())),
                 preferred_element_type=F32,
             )
-            for t in range(GROUP):
+            for t in range(BACK):
                 hg[place(lx, at + t), :] += prod[t * BLK : (t + 1) * BLK, :]
             return carry
 
-        lax.fori_loop(0, (ln[first + i] + GROUP - 1) // GROUP, step, 0)
+        return lax.fori_loop(0, (ln[first + i] + BACK - 1) // BACK, step, carry)
+
+    lax.fori_loop(0, nb, row, 0)
 
 
 def project(cot, w2, cw):
@@ -117,8 +145,9 @@
     ).astype(BF16)
 
 
-def back_kernel(nb, slots, counts, first, lk, lx, ln, w2, vals, *refs):
+def back_kernel(nb, slots, counts, first, plan, w2, vals, *refs):
     groups, (hg, cot, cw, sems) = split(refs, counts)
+    lk, lx, ln = plan_parts(plan, nb, slots)
     copies = load(groups, cot, sems)
     hg[...] = jnp.zeros_like(hg)
     for copy in copies:
@@ -128,28 +157,50 @@
 
 
 def lists_kernel(nb, slots, blank, *refs):
-    cols_own, used_own, cols_far, used_far, v_hbm, lk, lx, ln, v_own, sem = refs
-    bring = pltpu.make_async_copy(v_hbm, v_own, sem)
+    v_hbm, plan, v_own, cols_own, used_own, cols_far, used_far, sem = refs[4:]
+    lk, lx, ln = plan_parts(plan, nb, slots)
+    held = (cols_own, used_own, cols_far, used_far)
+    scalars = [
+        pltpu.make_async_copy(ref, here, sem.at[1 + n])
+        for n, (ref, here) in enumerate(zip(refs[:4], held))
+    ]
+    for copy in scalars:
+        copy.start()
+    bring = pltpu.make_async_copy(v_hbm, v_own, sem.at[0])
     bring.start()
-    cols = ((cols_own, used_own), (cols_far, used_far))
+    for copy in scalars:
+        copy.wait()
     dom = lax.axis_index("dom")
     base = lax.axis_index("col") * slots
     stride = slots + GROUP
-    for r in range(2 * nb):
-        names, used = cols[r // nb]
-        limit = used[r % nb]
-        n = jnp.int32(0)
-        for k in range(slots):
-            block = names[r % nb, base + k]
-            rel = lax.div(block, jnp.int32(nb)) ^ dom
-            lk[r * stride + n] = k
-            lx[r * stride + n] = (rel >> 1) * nb + lax.rem(block, jnp.int32(nb))
-            ok = jnp.logical_and(base + k < limit, (rel & 1) == 0)
-            n = n + ok.astype(jnp.int32)
-        ln[r] = n
-        for t in range(GROUP):
-            lk[r * stride + n + t] = 0
-            lx[r * stride + n + t] = blank
+    bits = nb.bit_length() - 1
+    halves = ((cols_own, used_own), (cols_far, used_far))
+    for half, (names, used) in enumerate(halves):
+
+        def row(i, carry, half=half, names=names, used=used):
+            start = (half * nb + i) * stride
+            limit = used[i] - base
+            n = start
+            for k in range(slots):
+                block = names[i, base + k]
+                if nb == 1 << bits:
+                    rel = block ^ (dom << bits)
+                    ok = (rel & nb) == 0
+                    spot = ((rel >> (bits + 1)) << bits) | (rel & (nb - 1))
+                else:
+                    rel = lax.div(block, jnp.int32(nb)) ^ dom
+                    ok = (rel & 1) == 0
+                    spot = (rel >> 1) * nb + lax.rem(block, jnp.int32(nb))
+                lk[n] = k
+                lx[n] = spot
+                n = n + jnp.logical_and(k < limit, ok).astype(jnp.int32)
+            ln[half * nb + i] = n - start
+            for t in range(GROUP):
+                lk[n + t] = 0
+                lx[n + t] = blank
+            return carry
+
+        lax.fori_loop(0, nb, row, 0)
     bring.wait()
 
 
@@ -164,7 +215,7 @@
         ref[rows, at] = value[:, q * narrow : (q + 1) * narrow].astype(ref.dtype)
 
 
-def rows_product(nb, slots, r, lk, lx, ln, vals, source, width):
+def rows_product(slots, r, i, lk, lx, ln, vals, source, width):
     base = r * (slots + GROUP)
 
     def step(g, acc):
@@ -173,26 +224,36 @@
             [source[place(lx, at + t), :] for t in range(GROUP)], axis=0
         )
         return acc + jnp.dot(
-            tiles(vals, r % nb, lk, at), right, preferred_element_type=F32
+            tiles(vals, i, lk, at, GROUP), right, preferred_element_type=F32
         )
 
     steps = (ln[r] + GROUP - 1) // GROUP
     return lax.fori_loop(0, steps, step, jnp.zeros((BLK, width), F32))
 
 
-def first_kernel(nb, slots, counts, narrow, lk, lx, ln, v_own, v_far, *refs):
+def first_kernel(nb, slots, counts, narrow, plan, v_own, v_far, *refs):
     groups, (keep, send, src, sems) = split(refs, counts)
+    lk, lx, ln = plan_parts(plan, nb, slots)
     copies = load(groups, src, sems)
     width = src.shape[1]
     src[src.shape[0] - BLK :, :] = jnp.zeros((BLK, width), BF16)
     for copy in copies:
         copy.wait()
-    for r in range(2 * nb):
-        acc = rows_product(nb, slots, r, lk, lx, ln, v_own if r < nb else v_far, src, width)
-        put(keep if r < nb else send, pl.ds(r % nb * BLK, BLK), acc, narrow)
-
-
-def second_kernel(nb, slots, counts, narrow, lk, lx, ln, w1, w2, v_own, v_far, hg, hg_far, *refs):
+    for half, (vals, ref) in enumerate(((v_own, keep), (v_far, send))):
+
+        def row(i, carry, half=half, vals=vals, ref=ref):
+            r = half * nb + i
+            acc = rows_product(slots, r, i, lk, lx, ln, vals, src, width)
+            put(ref, row_of(i, BLK), acc, narrow)
+            return carry
+
+        lax.fori_loop(0, nb, row, 0)
+
+
+def second_kernel(
+    nb, slots, counts, narrow, plan, w1, w2, v_own, v_far, hg, hg_far, *refs
+):
+    lk, lx, ln = plan_parts(plan, nb, slots)
     groups, (keep, send, gkeep, gsend, agg, hid, cot, mix, total, sems) = split(refs, counts)
     copies = load(groups[:-2], agg, sems)
     more = load(groups[-2:], cot, sems, len(copies))
@@ -202,8 +263,9 @@
     for copy in copies:
         copy.wait()
     total[...] = jnp.zeros_like(total)
-    for g in range(blocks // chunk):
-        rows = pl.ds(g * chunk, chunk)
+
+    for g in range(blocks // PART):
+        rows = pl.ds(g * PART, PART)
         a = agg[rows, :]
         first = jnp.dot(a, w1[...], preferred_element_type=F32)
         sig = 0.5 * jnp.tanh(0.5 * first) + 0.5
@@ -214,9 +276,15 @@
         total[...] += lax.dot_general(
             a, grad, (((0,), (0,)), ((), ())), preferred_element_type=F32
         )
-    for r in range(2 * nb):
-        acc = rows_product(nb, slots, r, lk, lx, ln, v_own if r < nb else v_far, hid, width)
-        mix[r * BLK : (r + 1) * BLK, :] = acc.astype(BF16)
+    for half, vals in enumerate((v_own, v_far)):
+
+        def row(i, carry, half=half, vals=vals):
+            r = half * nb + i
+            acc = rows_product(slots, r, i, lk, lx, ln, vals, hid, width)
+            mix[row_of(r, BLK), :] = acc.astype(BF16)
+            return carry
+
+        lax.fori_loop(0, nb, row, 0)
     for copy in more:
         copy.wait()
     core = lax.axis_index("dom") & 1
@@ -292,7 +360,6 @@
     nb, slots = block_vals.shape[:2]
     width = narrow * nc
     blocks = nd // 2 * rows
-    lists = 2 * nb * (slots + GROUP)
     dense = 2 * 2 * nb * slots * BLK * BLK * width // 2
 
     pieces = 1 if narrow % LANES else nc
@@ -306,18 +373,22 @@
     )
     cot_far = [swap(piece, "dom", 1) for piece in cot_own]
 
-    lk, lx, ln, v_own = call(
+    plan, v_own = call(
         functools.partial(lists_kernel, nb, slots, blocks // BLK),
         [
-            ((lists,), jnp.int32),
-            ((lists,), jnp.int32),
-            ((2 * nb,), jnp.int32),
+            ((plan_size(nb, slots),), jnp.int32),
             (block_vals.shape, BF16),
         ],
-        [smem()] * 3 + [vmem()],
-        [smem()] * 4 + [any_spec()],
-        [pltpu.SemaphoreType.DMA],
-        (*cols, in_hbm(block_vals)),
+        [smem(), vmem()],
+        [any_spec()] * 5,
+        [
+            pltpu.SMEM(block_cols.shape, jnp.int32),
+            pltpu.SMEM(block_count.shape, jnp.int32),
+            pltpu.SMEM(block_cols.shape, jnp.int32),
+            pltpu.SMEM(block_count.shape, jnp.int32),
+            pltpu.SemaphoreType.DMA((5,)),
+        ],
+        (*[in_hbm(c) for c in cols[:2]], *cols[2:], in_hbm(block_vals)),
         1 << 20,
     )
 
@@ -328,12 +399,12 @@
         functools.partial(first_kernel, nb, slots, counts, narrow),
         [((rows, width), F32), ((rows, width), BF16)],
         [vmem()] * 2,
-        [smem()] * 3 + [vmem()] * 2 + [any_spec()] * sum(counts),
+        [smem()] + [vmem()] * 2 + [any_spec()] * sum(counts),
         [
             pltpu.VMEM((blocks + BLK, width), BF16),
             pltpu.SemaphoreType.DMA((sum(counts),)),
         ],
-        (lk, lx, ln, v_own, v_far, *[p for g in chunks for p in g]),
+        (plan, v_own, v_far, *[p for g in chunks for p in g]),
         dense,
     )
 
@@ -343,13 +414,13 @@
             functools.partial(back_kernel, nb, slots, (n,), first),
             [((blocks + BLK, width), F32)],
             [vmem()],
-            [smem()] * 3 + [vmem()] * 2 + [any_spec()] * n,
+            [smem()] + [vmem()] * 2 + [any_spec()] * n,
             [
                 pltpu.VMEM((rows, width), BF16),
                 pltpu.VMEM((rows, width), BF16),
                 pltpu.SemaphoreType.DMA((n,)),
             ],
-            (lk, lx, ln, w_second, vals, *pieces),
+            (plan, w_second, vals, *pieces),
             dense // 2,
         )[0]
 
@@ -385,7 +456,7 @@
             ((width, width), BF16),
         ],
         [vmem()] * 4,
-        [smem()] * 3 + [vmem()] * 6 + [any_spec()] * sum(counts),
+        [smem()] + [vmem()] * 6 + [any_spec()] * sum(counts),
         [
             pltpu.VMEM((blocks, width), BF16),
             pltpu.VMEM((blocks + BLK, width), BF16),
@@ -394,7 +465,7 @@
             pltpu.VMEM((width, width), F32),
             pltpu.SemaphoreType.DMA((sum(counts),)),
         ],
-        (lk, lx, ln, w_first, w_second, v_own, v_far, hg, hg_far)
+        (plan, w_first, w_second, v_own, v_far, hg, hg_far)
         + tuple(p for g in groups for p in g),
         4 * dense,
     )

time: 111 us -> 110 us (level)
  Pallas kernels: 21.5 us -> 19.6 us
  waiting for transfers between devices: 36.2 us -> 37.6 us
  local copies, waits for them, and re-layouts: 1.4 us -> 0.07 us
    pallas_call x6, Pallas kernels: 21.5 us -> 19.6 us  [call(): pl.pallas_call(kernel, out_shape=tuple((jax.ShapeDtypeStruct(*o) for o in...]
    ppermute x46, waiting for transfers between devices: 36.2 us -> 37.6 us  [swap(): return lax.ppermute(value, axis, [(i, i ^ mask) for i in range(size)])]
    unnamed x10 -> x6, local copies, waits for them, and re-layouts: 1.35 us -> 0.02 us
  transfers between devices with their start and end apart: 46 -> 46, of which waited for: 18 -> 19; matrix products, arithmetic and copies ran while one was open for 1% -> 1% of each run, Pallas kernels for 8% -> 8%
where the time goes in v1:
time: 110 us; the launch traced here: 109 us
  starting transfers between devices  50.2 us (46%)
  waiting for transfers between devices  37.6 us (34%)
  Pallas kernels  19.6 us (18%)
    ppermute x46, starting transfers between devices, swap(): return lax.ppermute(value, axis, [(i, i ^ mask) for i in range(size)])  50.2 us
    ppermute x46, waiting for transfers between devices, swap(): return lax.ppermute(value, axis, [(i, i ^ mask) for i in range(size)])  37.6 us
    pallas_call x6, Pallas kernels, call(): pl.pallas_call(kernel, out_shape=tuple((jax.ShapeDtypeStruct(*o) for o in...  19.6 us
  transfers between devices with their start and end apart: 46, of which 19 were waited for; matrix products, arithmetic and copies ran while one was open for 1% of the time, Pallas kernels for 8%

profile of v1, /device:TPU:0, one launch (start us, length us, event | category | flops | bytes accessed | tf_op | source)
XLA Modules:
  0.0 109.3 jit_solution(15052087849708676469)
XLA Ops:
  1.2 3.6 %collective-permute-start.13 = (bf16[512,128]{1,0:T(8,128)(2,1)}, bf16[512,128]{1,0:T(8,128)(2,1)S(1)}, u32[]{:S(2)}, u32[]{:S(2)}) collective-permute-start(bf16[512,128]{1,0:T(8,128)(2,1)} %refs_0_.5), channel_id=1, source_target_pairs={{0,16},{2,18},{4,20},{6,22},{8,24},{10,26},{12,28},{14,30},{16,0},... | collective-permute-start | bytes 393224 | tf_op jit(solution)/shard_map/ppermute | solution.py:22
  4.8 1.6 %collective-permute-start.9 = (bf16[512,128]{1,0:T(8,128)(2,1)}, bf16[512,128]{1,0:T(8,128)(2,1)S(1)}, u32[]{:S(2)}, u32[]{:S(2)}) collective-permute-start(bf16[512,128]{1,0:T(8,128)(2,1)} %refs_0_.5), channel_id=1, source_target_pairs={{0,8},{2,10},{4,12},{6,14},{8,0},{10,2},{12,4},{14,6},{16,24},{18,... | collective-permute-start | bytes 393224 | tf_op jit(solution)/shard_map/ppermute | solution.py:22
  6.4 1.5 %collective-permute-start.7 = (bf16[512,128]{1,0:T(8,128)(2,1)}, bf16[512,128]{1,0:T(8,128)(2,1)S(1)}, u32[]{:S(2)}, u32[]{:S(2)}) collective-permute-start(bf16[512,128]{1,0:T(8,128)(2,1)} %refs_0_.5), channel_id=1, source_target_pairs={{0,4},{2,6},{4,0},{6,2},{8,12},{10,14},{12,8},{14,10},{16,20},{18,... | collective-permute-start | bytes 393224 | tf_op jit(solution)/shard_map/ppermute | solution.py:22
  10.6 1.5 %collective-permute-start.6 = (bf16[512,128]{1,0:T(8,128)(2,1)}, bf16[512,128]{1,0:T(8,128)(2,1)S(1)}, u32[]{:S(2)}, u32[]{:S(2)}) collective-permute-start(bf16[512,128]{1,0:T(8,128)(2,1)} %refs_0_.5), channel_id=1, source_target_pairs={{0,1},{1,0},{2,3},{3,2},{4,5},{5,4},{6,7},{7,6},{8,9},{9,8},{10,11... | collective-permute-start | bytes 393224 | tf_op jit(solution)/shard_map/ppermute | solution.py:22
  12.1 3.4 %collective-permute-start.17 = (bf16[512,128]{1,0:T(8,128)(2,1)}, bf16[512,128]{1,0:T(8,128)(2,1)S(1)}, u32[]{:S(2)}, u32[]{:S(2)}) collective-permute-start(bf16[512,128]{1,0:T(8,128)(2,1)} %refs_0_.5), channel_id=1, source_target_pairs={{0,24},{2,26},{4,28},{6,30},{8,16},{10,18},{12,20},{14,22},{16,8},... | collective-permute-start | bytes 393224 | tf_op jit(solution)/shard_map/ppermute | solution.py:22
  15.5 1.5 %collective-permute-start.15 = (bf16[512,128]{1,0:T(8,128)(2,1)S(1)}, bf16[512,128]{1,0:T(8,128)(2,1)S(1)}, u32[]{:S(2)}, u32[]{:S(2)}) collective-permute-start(bf16[512,128]{1,0:T(8,128)(2,1)S(1)} %collective-permute-done.13.refs_8_), channel_id=1, source_target_pairs={{0,4},{2,6},{4,0},{6,2},{8,12},{10,14},{12,8},{14,10},{16,20},{18,... | collective-permute-start | bytes 393224 | tf_op jit(solution)/shard_map/ppermute | solution.py:22
  17.0 1.5 %collective-permute-start.14 = (bf16[512,128]{1,0:T(8,128)(2,1)S(1)}, bf16[512,128]{1,0:T(8,128)(2,1)S(1)}, u32[]{:S(2)}, u32[]{:S(2)}) collective-permute-start(bf16[512,128]{1,0:T(8,128)(2,1)S(1)} %collective-permute-done.13.refs_8_), channel_id=1, source_target_pairs={{0,1},{1,0},{2,3},{3,2},{4,5},{5,4},{6,7},{7,6},{8,9},{9,8},{10,11... | collective-permute-start | bytes 393224 | tf_op jit(solution)/shard_map/ppermute | solution.py:22
  19.5 1.5 %collective-permute-start.10 = (bf16[512,128]{1,0:T(8,128)(2,1)S(1)}, bf16[512,128]{1,0:T(8,128)(2,1)S(1)}, u32[]{:S(2)}, u32[]{:S(2)}) collective-permute-start(bf16[512,128]{1,0:T(8,128)(2,1)S(1)} %collective-permute-done.9.refs_4_), channel_id=1, source_target_pairs={{0,1},{1,0},{2,3},{3,2},{4,5},{5,4},{6,7},{7,6},{8,9},{9,8},{10,11... | collective-permute-start | bytes 393224 | tf_op jit(solution)/shard_map/ppermute | solution.py:22
  21.1 2.3 %collective-permute-start.8 = (bf16[512,128]{1,0:T(8,128)(2,1)S(1)}, bf16[512,128]{1,0:T(8,128)(2,1)S(1)}, u32[]{:S(2)}, u32[]{:S(2)}) collective-permute-start(bf16[512,128]{1,0:T(8,128)(2,1)S(1)} %collective-permute-done.6.refs_1_), channel_id=1, source_target_pairs={{0,4},{2,6},{4,0},{6,2},{8,12},{10,14},{12,8},{14,10},{16,20},{18,... | collective-permute-start | bytes 393224 | tf_op jit(solution)/shard_map/ppermute | solution.py:22
  24.6 1.6 %collective-permute-start.18 = (bf16[512,128]{1,0:T(8,128)(2,1)S(1)}, bf16[512,128]{1,0:T(8,128)(2,1)S(1)}, u32[]{:S(2)}, u32[]{:S(2)}) collective-permute-start(bf16[512,128]{1,0:T(8,128)(2,1)S(1)} %collective-permute-done.17.refs_12_), channel_id=1, source_target_pairs={{0,1},{1,0},{2,3},{3,2},{4,5},{5,4},{6,7},{7,6},{8,9},{9,8},{10,11... | collective-permute-start | bytes 393224 | tf_op jit(solution)/shard_map/ppermute | solution.py:22
  26.2 1.5 %collective-permute-start.16 = (bf16[512,128]{1,0:T(8,128)(2,1)S(1)}, bf16[512,128]{1,0:T(8,128)(2,1)S(1)}, u32[]{:S(2)}, u32[]{:S(2)}) collective-permute-start(bf16[512,128]{1,0:T(8,128)(2,1)S(1)} %collective-permute-done.14.refs_9_), channel_id=1, source_target_pairs={{0,4},{2,6},{4,0},{6,2},{8,12},{10,14},{12,8},{14,10},{16,20},{18,... | collective-permute-start | bytes 393224 | tf_op jit(solution)/shard_map/ppermute | solution.py:22
  27.7 2.1 %collective-permute-start.12 = (bf16[512,128]{1,0:T(8,128)(2,1)S(1)}, bf16[512,128]{1,0:T(8,128)(2,1)S(1)}, u32[]{:S(2)}, u32[]{:S(2)}) collective-permute-start(bf16[512,128]{1,0:T(8,128)(2,1)S(1)} %collective-permute-done.11.refs_6_), channel_id=1, source_target_pairs={{0,1},{1,0},{2,3},{3,2},{4,5},{5,4},{6,7},{7,6},{8,9},{9,8},{10,11... | collective-permute-start | bytes 393224 | tf_op jit(solution)/shard_map/ppermute | solution.py:22
  30.5 1.5 %collective-permute-start.20 = (bf16[512,128]{1,0:T(8,128)(2,1)S(1)}, bf16[512,128]{1,0:T(8,128)(2,1)S(1)}, u32[]{:S(2)}, u32[]{:S(2)}) collective-permute-start(bf16[512,128]{1,0:T(8,128)(2,1)S(1)} %collective-permute-done.19.refs_14_), channel_id=1, source_target_pairs={{0,1},{1,0},{2,3},{3,2},{4,5},{5,4},{6,7},{7,6},{8,9},{9,8},{10,11... | collective-permute-start | bytes 393224 | tf_op jit(solution)/shard_map/ppermute | solution.py:22
  32.0 2.4 %shard_map.94 = (s32[392]{0:T(512)S(1)}, bf16[4,16,128,128]{3,2,1,0:T(8,128)(2,1)S(1)}) custom-call(s32[4,32]{1,0:T(4,128)} %refs_0_.3, s32[4]{0:T(128)} %refs_1_.1, s32[4,32]{1,0:T(4,128)S(1)} %collective-permute-done.refs_2_, s32[4]{0:T(128)S(1)} %collective-permute-done.1.refs_3_, bf16[4,16,128,128]{3,2,1,0:T(8,128)(2,1)} %refs_4_.1), custom_call_target="tpu_custom_call" | custom-call | flops 1048576 | bytes 4194304 | tf_op jit(solution)/shard_map/pallas_call | solution.py:343
  35.5 3.8 %shard_map.97 = (f32[512,256]{1,0:T(8,128)S(1)}, bf16[512,256]{1,0:T(8,128)(2,1)S(1)}) custom-call(s32[392]{0:T(512)S(1)} %get-tuple-element.13.plan, bf16[4,16,128,128]{3,2,1,0:T(8,128)(2,1)S(1)} %get-tuple-element.14.vals.v_own, bf16[4,16,128,128]{3,2,1,0:T(8,128)(2,1)S(1)} %collective-permute-done.2.vals.v_far, bf16[512,128]{1,0:T(8,128)(2,1)} %refs_0_.5, ...), custom_call_target="tpu_custom_call" | custom-call | flops 536870912 | bytes 4194304 | tf_op jit(solution)/shard_map/pallas_call | solution.py:343
  42.1 3.7 %collective-permute-done.3.refs_1_.refs_17_ = bf16[512,128]{1,0:T(8,128)(2,1)S(1)} collective-permute-done((bf16[512,128]{1,0:T(8,128)(2,1)S(1)}, bf16[512,128]{1,0:T(8,128)(2,1)S(1)}, u32[]{:S(2)}, u32[]{:S(2)}) %collective-permute-start.3) | collective-permute-done | bytes 131104 | tf_op jit(solution)/shard_map/ppermute | solution.py:22
  45.8 2.3 %collective-permute-done.22 = bf16[512,128]{1,0:T(8,128)(2,1)S(1)} collective-permute-done((bf16[512,128]{1,0:T(8,128)(2,1)S(1)}, bf16[512,128]{1,0:T(8,128)(2,1)S(1)}, u32[]{:S(2)}, u32[]{:S(2)}) %collective-permute-start.22) | collective-permute-done | bytes 131104 | tf_op jit(solution)/shard_map/ppermute | solution.py:22
  48.1 3.1 %collective-permute-start.34 = (bf16[512,128]{1,0:T(8,128)(2,1)S(1)}, bf16[512,128]{1,0:T(8,128)(2,1)S(1)}, u32[]{:S(2)}, u32[]{:S(2)}) collective-permute-start(bf16[512,128]{1,0:T(8,128)(2,1)S(1)} %fusion.refs_0_), channel_id=1, source_target_pairs={{0,24},{2,26},{4,28},{6,30},{8,16},{10,18},{12,20},{14,22},{16,8},... | collective-permute-start | bytes 393224 | tf_op jit(solution)/shard_map/ppermute | solution.py:22
  51.2 1.4 %collective-permute-start.26 = (bf16[512,128]{1,0:T(8,128)(2,1)S(1)}, bf16[512,128]{1,0:T(8,128)(2,1)S(1)}, u32[]{:S(2)}, u32[]{:S(2)}) collective-permute-start(bf16[512,128]{1,0:T(8,128)(2,1)S(1)} %fusion.refs_0_), channel_id=1, source_target_pairs={{0,8},{2,10},{4,12},{6,14},{8,0},{10,2},{12,4},{14,6},{16,24},{18,... | collective-permute-start | bytes 393224 | tf_op jit(solution)/shard_map/ppermute | solution.py:22
  52.6 2.2 %collective-permute-start.24 = (bf16[512,128]{1,0:T(8,128)(2,1)S(1)}, bf16[512,128]{1,0:T(8,128)(2,1)S(1)}, u32[]{:S(2)}, u32[]{:S(2)}) collective-permute-start(bf16[512,128]{1,0:T(8,128)(2,1)S(1)} %fusion.refs_0_), channel_id=1, source_target_pairs={{0,4},{2,6},{4,0},{6,2},{8,12},{10,14},{12,8},{14,10},{16,20},{18,... | collective-permute-start | bytes 393224 | tf_op jit(solution)/shard_map/ppermute | solution.py:22
  56.4 2.2 %collective-permute-start.36 = (bf16[512,128]{1,0:T(8,128)(2,1)S(1)}, bf16[512,128]{1,0:T(8,128)(2,1)S(1)}, u32[]{:S(2)}, u32[]{:S(2)}) collective-permute-start(bf16[512,128]{1,0:T(8,128)(2,1)S(1)} %collective-permute-done.34.refs_12_), channel_id=1, source_target_pairs={{0,4},{2,6},{4,0},{6,2},{8,12},{10,14},{12,8},{14,10},{16,20},{18,... | collective-permute-start | bytes 393224 | tf_op jit(solution)/shard_map/ppermute | solution.py:22
  58.6 3.7 %collective-permute-done.30.refs_8_ = bf16[512,128]{1,0:T(8,128)(2,1)S(1)} collective-permute-done((bf16[512,128]{1,0:T(8,128)(2,1)S(1)}, bf16[512,128]{1,0:T(8,128)(2,1)S(1)}, u32[]{:S(2)}, u32[]{:S(2)}) %collective-permute-start.30) | collective-permute-done | bytes 131104 | tf_op jit(solution)/shard_map/ppermute | solution.py:22
  64.1 1.5 %collective-permute-start.31 = (bf16[512,128]{1,0:T(8,128)(2,1)S(1)}, bf16[512,128]{1,0:T(8,128)(2,1)S(1)}, u32[]{:S(2)}, u32[]{:S(2)}) collective-permute-start(bf16[512,128]{1,0:T(8,128)(2,1)S(1)} %collective-permute-done.30.refs_8_), channel_id=1, source_target_pairs={{0,1},{1,0},{2,3},{3,2},{4,5},{5,4},{6,7},{7,6},{8,9},{9,8},{10,11... | collective-permute-start | bytes 393224 | tf_op jit(solution)/shard_map/ppermute | solution.py:22
  67.0 1.7 %collective-permute-done.35.refs_13_ = bf16[512,128]{1,0:T(8,128)(2,1)S(1)} collective-permute-done((bf16[512,128]{1,0:T(8,128)(2,1)S(1)}, bf16[512,128]{1,0:T(8,128)(2,1)S(1)}, u32[]{:S(2)}, u32[]{:S(2)}) %collective-permute-start.35) | collective-permute-done | bytes 131104 | tf_op jit(solution)/shard_map/ppermute | solution.py:22
  73.5 3.2 %shard_map.95.hg = f32[4224,256]{1,0:T(8,128)S(1)} custom-call(s32[392]{0:T(512)S(1)} %get-tuple-element.13.plan, bf16[256,256]{1,0:T(8,128)(2,1)S(1)} %copy-done, bf16[4,16,128,128]{3,2,1,0:T(8,128)(2,1)S(1)} %get-tuple-element.14.vals.v_own, bf16[512,128]{1,0:T(8,128)(2,1)S(1)} %copy-done.1, bf16[512,128]{1,0:T(8,128)(2,1)S(1)} %collective-permute-done.3.refs_1_.refs_17_), custom_call_target="tpu_custom_call" | custom-call | flops 268435456 | bytes 4194304 | tf_op jit(solution)/shard_map/pallas_call | solution.py:343
  76.8 3.2 %shard_map.96.hg_far = f32[4224,256]{1,0:T(8,128)S(1)} custom-call(s32[392]{0:T(512)S(1)} %get-tuple-element.13.plan, bf16[256,256]{1,0:T(8,128)(2,1)S(1)} %copy-done, bf16[4,16,128,128]{3,2,1,0:T(8,128)(2,1)S(1)} %collective-permute-done.2.vals.v_far, bf16[512,128]{1,0:T(8,128)(2,1)S(1)} %collective-permute-done.4.refs_0_.refs_18_, ...), custom_call_target="tpu_custom_call" | custom-call | flops 268435456 | bytes 4194304 | tf_op jit(solution)/shard_map/pallas_call | solution.py:343
  80.0 6.3 %shard_map.98 = (f32[512,256]{1,0:T(8,128)S(1)}, bf16[512,256]{1,0:T(8,128)(2,1)S(1)}, f32[256,256]{1,0:T(8,128)S(1)}, bf16[256,256]{1,0:T(8,128)(2,1)S(1)}) custom-call(s32[392]{0:T(512)S(1)} %get-tuple-element.13.plan, bf16[256,256]{1,0:T(8,128)(2,1)S(1)} %copy-done.2, bf16[256,256]{1,0:T(8,128)(2,1)S(1)} %copy-done, ...), custom_call_target="tpu_custom_call" | custom-call | flops 2147483648 | bytes 4194304 | tf_op jit(solution)/shard_map/pallas_call | solution.py:343
  87.9 4.3 %collective-permute-done.41 = bf16[256,128]{1,0:T(8,128)(2,1)S(1)} collective-permute-done((bf16[256,128]{1,0:T(8,128)(2,1)S(1)}, bf16[256,128]{1,0:T(8,128)(2,1)S(1)}, u32[]{:S(2)}, u32[]{:S(2)}) %collective-permute-start.41) | collective-permute-done | bytes 65568 | tf_op jit(solution)/shard_map/ppermute | solution.py:22
  92.1 2.8 %collective-permute-start.42 = (bf16[256,128]{1,0:T(8,128)(2,1)S(1)}, bf16[256,128]{1,0:T(8,128)(2,1)S(1)}, u32[]{:S(2)}, u32[]{:S(2)}) collective-permute-start(bf16[256,128]{1,0:T(8,128)(2,1)S(1)} %fusion.1), channel_id=1, source_target_pairs={{0,4},{2,6},{4,0},{6,2},{8,12},{10,14},{12,8},{14,10},{16,20},{18,... | collective-permute-start | bytes 196616 | tf_op jit(solution)/shard_map/ppermute | solution.py:22
  95.0 2.2 %collective-permute-done.42 = bf16[256,128]{1,0:T(8,128)(2,1)S(1)} collective-permute-done((bf16[256,128]{1,0:T(8,128)(2,1)S(1)}, bf16[256,128]{1,0:T(8,128)(2,1)S(1)}, u32[]{:S(2)}, u32[]{:S(2)}) %collective-permute-start.42) | collective-permute-done | bytes 65568 | tf_op jit(solution)/shard_map/ppermute | solution.py:22
  97.5 4.1 %collective-permute-done.43 = bf16[256,128]{1,0:T(8,128)(2,1)S(1)} collective-permute-done((bf16[256,128]{1,0:T(8,128)(2,1)S(1)}, bf16[256,128]{1,0:T(8,128)(2,1)S(1)}, u32[]{:S(2)}, u32[]{:S(2)}) %collective-permute-start.43) | collective-permute-done | bytes 65568 | tf_op jit(solution)/shard_map/ppermute | solution.py:22
  102.0 5.2 %collective-permute-done.44 = bf16[256,128]{1,0:T(8,128)(2,1)S(1)} collective-permute-done((bf16[256,128]{1,0:T(8,128)(2,1)S(1)}, bf16[256,128]{1,0:T(8,128)(2,1)S(1)}, u32[]{:S(2)}, u32[]{:S(2)}) %collective-permute-start.44) | collective-permute-done | bytes 65568 | tf_op jit(solution)/shard_map/ppermute | solution.py:22
  (84 shorter events, 24.1 us)
Async XLA Ops:
  0.6 34.9 %collective-permute-start.2 = (bf16[4,16,128,128]{3,2,1,0:T(8,128)(2,1)}, bf16[4,16,128,128]{3,2,1,0:T(8,128)(2,1)S(1)}, u32[]{:S(2)}, u32[]{:S(2)}) collective-permute-start(bf16[4,16,128,128]{3,2,1,0:T(8,128)(2,1)} %refs_4_.1), channel_id=1, source_target_pairs={{0,2},{2,0},{4,6},{6,4},{8,10},{10,8},{12,14},{14,12},{16,18},{18,... | collective-permute-start | bytes 6291464 | tf_op jit(solution)/shard_map/ppermute | solution.py:22
  1.2 10.9 %collective-permute-start.13 = (bf16[512,128]{1,0:T(8,128)(2,1)}, bf16[512,128]{1,0:T(8,128)(2,1)S(1)}, u32[]{:S(2)}, u32[]{:S(2)}) collective-permute-start(bf16[512,128]{1,0:T(8,128)(2,1)} %refs_0_.5), channel_id=1, source_target_pairs={{0,16},{2,18},{4,20},{6,22},{8,24},{10,26},{12,28},{14,30},{16,0},... | collective-permute-start | bytes 393224 | tf_op jit(solution)/shard_map/ppermute | solution.py:22
  4.8 10.7 %collective-permute-start.9 = (bf16[512,128]{1,0:T(8,128)(2,1)}, bf16[512,128]{1,0:T(8,128)(2,1)S(1)}, u32[]{:S(2)}, u32[]{:S(2)}) collective-permute-start(bf16[512,128]{1,0:T(8,128)(2,1)} %refs_0_.5), channel_id=1, source_target_pairs={{0,8},{2,10},{4,12},{6,14},{8,0},{10,2},{12,4},{14,6},{16,24},{18,... | collective-permute-start | bytes 393224 | tf_op jit(solution)/shard_map/ppermute | solution.py:22
  6.4 10.6 %collective-permute-start.7 = (bf16[512,128]{1,0:T(8,128)(2,1)}, bf16[512,128]{1,0:T(8,128)(2,1)S(1)}, u32[]{:S(2)}, u32[]{:S(2)}) collective-permute-start(bf16[512,128]{1,0:T(8,128)(2,1)} %refs_0_.5), channel_id=1, source_target_pairs={{0,4},{2,6},{4,0},{6,2},{8,12},{10,14},{12,8},{14,10},{16,20},{18,... | collective-permute-start | bytes 393224 | tf_op jit(solution)/shard_map/ppermute | solution.py:22
  10.6 7.9 %collective-permute-start.6 = (bf16[512,128]{1,0:T(8,128)(2,1)}, bf16[512,128]{1,0:T(8,128)(2,1)S(1)}, u32[]{:S(2)}, u32[]{:S(2)}) collective-permute-start(bf16[512,128]{1,0:T(8,128)(2,1)} %refs_0_.5), channel_id=1, source_target_pairs={{0,1},{1,0},{2,3},{3,2},{4,5},{5,4},{6,7},{7,6},{8,9},{9,8},{10,11... | collective-permute-start | bytes 393224 | tf_op jit(solution)/shard_map/ppermute | solution.py:22
  12.1 7.4 %collective-permute-start.17 = (bf16[512,128]{1,0:T(8,128)(2,1)}, bf16[512,128]{1,0:T(8,128)(2,1)S(1)}, u32[]{:S(2)}, u32[]{:S(2)}) collective-permute-start(bf16[512,128]{1,0:T(8,128)(2,1)} %refs_0_.5), channel_id=1, source_target_pairs={{0,24},{2,26},{4,28},{6,30},{8,16},{10,18},{12,20},{14,22},{16,8},... | collective-permute-start | bytes 393224 | tf_op jit(solution)/shard_map/ppermute | solution.py:22
  17.0 6.4 %collective-permute-start.14 = (bf16[512,128]{1,0:T(8,128)(2,1)S(1)}, bf16[512,128]{1,0:T(8,128)(2,1)S(1)}, u32[]{:S(2)}, u32[]{:S(2)}) collective-permute-start(bf16[512,128]{1,0:T(8,128)(2,1)S(1)} %collective-permute-done.13.refs_8_), channel_id=1, source_target_pairs={{0,1},{1,0},{2,3},{3,2},{4,5},{5,4},{6,7},{7,6},{8,9},{9,8},{10,11... | collective-permute-start | bytes 393224 | tf_op jit(solution)/shard_map/ppermute | solution.py:22
  19.5 6.7 %collective-permute-start.10 = (bf16[512,128]{1,0:T(8,128)(2,1)S(1)}, bf16[512,128]{1,0:T(8,128)(2,1)S(1)}, u32[]{:S(2)}, u32[]{:S(2)}) collective-permute-start(bf16[512,128]{1,0:T(8,128)(2,1)S(1)} %collective-permute-done.9.refs_4_), channel_id=1, source_target_pairs={{0,1},{1,0},{2,3},{3,2},{4,5},{5,4},{6,7},{7,6},{8,9},{9,8},{10,11... | collective-permute-start | bytes 393224 | tf_op jit(solution)/shard_map/ppermute | solution.py:22
  21.1 6.6 %collective-permute-start.8 = (bf16[512,128]{1,0:T(8,128)(2,1)S(1)}, bf16[512,128]{1,0:T(8,128)(2,1)S(1)}, u32[]{:S(2)}, u32[]{:S(2)}) collective-permute-start(bf16[512,128]{1,0:T(8,128)(2,1)S(1)} %collective-permute-done.6.refs_1_), channel_id=1, source_target_pairs={{0,4},{2,6},{4,0},{6,2},{8,12},{10,14},{12,8},{14,10},{16,20},{18,... | collective-permute-start | bytes 393224 | tf_op jit(solution)/shard_map/ppermute | solution.py:22
  23.4 7.2 %collective-permute-start.19 = (bf16[512,128]{1,0:T(8,128)(2,1)S(1)}, bf16[512,128]{1,0:T(8,128)(2,1)S(1)}, u32[]{:S(2)}, u32[]{:S(2)}) collective-permute-start(bf16[512,128]{1,0:T(8,128)(2,1)S(1)} %collective-permute-done.17.refs_12_), channel_id=1, source_target_pairs={{0,4},{2,6},{4,0},{6,2},{8,12},{10,14},{12,8},{14,10},{16,20},{18,... | collective-permute-start | bytes 393224 | tf_op jit(solution)/shard_map/ppermute | solution.py:22
  24.6 9.8 %collective-permute-start.18 = (bf16[512,128]{1,0:T(8,128)(2,1)S(1)}, bf16[512,128]{1,0:T(8,128)(2,1)S(1)}, u32[]{:S(2)}, u32[]{:S(2)}) collective-permute-start(bf16[512,128]{1,0:T(8,128)(2,1)S(1)} %collective-permute-done.17.refs_12_), channel_id=1, source_target_pairs={{0,1},{1,0},{2,3},{3,2},{4,5},{5,4},{6,7},{7,6},{8,9},{9,8},{10,11... | collective-permute-start | bytes 393224 | tf_op jit(solution)/shard_map/ppermute | solution.py:22
  26.2 8.2 %collective-permute-start.16 = (bf16[512,128]{1,0:T(8,128)(2,1)S(1)}, bf16[512,128]{1,0:T(8,128)(2,1)S(1)}, u32[]{:S(2)}, u32[]{:S(2)}) collective-permute-start(bf16[512,128]{1,0:T(8,128)(2,1)S(1)} %collective-permute-done.14.refs_9_), channel_id=1, source_target_pairs={{0,4},{2,6},{4,0},{6,2},{8,12},{10,14},{12,8},{14,10},{16,20},{18,... | collective-permute-start | bytes 393224 | tf_op jit(solution)/shard_map/ppermute | solution.py:22
  27.7 6.7 %collective-permute-start.12 = (bf16[512,128]{1,0:T(8,128)(2,1)S(1)}, bf16[512,128]{1,0:T(8,128)(2,1)S(1)}, u32[]{:S(2)}, u32[]{:S(2)}) collective-permute-start(bf16[512,128]{1,0:T(8,128)(2,1)S(1)} %collective-permute-done.11.refs_6_), channel_id=1, source_target_pairs={{0,1},{1,0},{2,3},{3,2},{4,5},{5,4},{6,7},{7,6},{8,9},{9,8},{10,11... | collective-permute-start | bytes 393224 | tf_op jit(solution)/shard_map/ppermute | solution.py:22
  39.4 6.4 %collective-permute-start.3 = (bf16[512,128]{1,0:T(8,128)(2,1)S(1)}, bf16[512,128]{1,0:T(8,128)(2,1)S(1)}, u32[]{:S(2)}, u32[]{:S(2)}) collective-permute-start(bf16[512,128]{1,0:T(8,128)(2,1)S(1)} %copy-done.1), channel_id=1, source_target_pairs={{0,1},{1,0},{2,3},{3,2},{4,5},{5,4},{6,7},{7,6},{8,9},{9,8},{10,11... | collective-permute-start | bytes 393224 | tf_op jit(solution)/shard_map/ppermute | solution.py:22
  41.0 7.1 %collective-permute-start.22 = (bf16[512,128]{1,0:T(8,128)(2,1)S(1)}, bf16[512,128]{1,0:T(8,128)(2,1)S(1)}, u32[]{:S(2)}, u32[]{:S(2)}) collective-permute-start(bf16[512,128]{1,0:T(8,128)(2,1)S(1)} %slice.44), channel_id=1, source_target_pairs={{0,1},{1,0},{2,3},{3,2},{4,5},{5,4},{6,7},{7,6},{8,9},{9,8},{10,11... | collective-permute-start | bytes 393224 | tf_op jit(solution)/shard_map/ppermute | solution.py:22
  42.1 10.5 %collective-permute-start.4 = (bf16[512,128]{1,0:T(8,128)(2,1)S(1)}, bf16[512,128]{1,0:T(8,128)(2,1)S(1)}, u32[]{:S(2)}, u32[]{:S(2)}) collective-permute-start(bf16[512,128]{1,0:T(8,128)(2,1)S(1)} %copy-done.1), channel_id=1, source_target_pairs={{0,2},{2,0},{4,6},{6,4},{8,10},{10,8},{12,14},{14,12},{16,18},{18,... | collective-permute-start | bytes 393224 | tf_op jit(solution)/shard_map/ppermute | solution.py:22
  45.8 9.0 %collective-permute-start.5 = (bf16[512,128]{1,0:T(8,128)(2,1)S(1)}, bf16[512,128]{1,0:T(8,128)(2,1)S(1)}, u32[]{:S(2)}, u32[]{:S(2)}) collective-permute-start(bf16[512,128]{1,0:T(8,128)(2,1)S(1)} %collective-permute-done.3.refs_1_.refs_17_), channel_id=1, source_target_pairs={{0,2},{2,0},{4,6},{6,4},{8,10},{10,8},{12,14},{14,12},{16,18},{18,... | collective-permute-start | bytes 393224 | tf_op jit(solution)/shard_map/ppermute | solution.py:22
  48.1 8.3 %collective-permute-start.34 = (bf16[512,128]{1,0:T(8,128)(2,1)S(1)}, bf16[512,128]{1,0:T(8,128)(2,1)S(1)}, u32[]{:S(2)}, u32[]{:S(2)}) collective-permute-start(bf16[512,128]{1,0:T(8,128)(2,1)S(1)} %fusion.refs_0_), channel_id=1, source_target_pairs={{0,24},{2,26},{4,28},{6,30},{8,16},{10,18},{12,20},{14,22},{16,8},... | collective-permute-start | bytes 393224 | tf_op jit(solution)/shard_map/ppermute | solution.py:22
  51.2 11.2 %collective-permute-start.30 = (bf16[512,128]{1,0:T(8,128)(2,1)S(1)}, bf16[512,128]{1,0:T(8,128)(2,1)S(1)}, u32[]{:S(2)}, u32[]{:S(2)}) collective-permute-start(bf16[512,128]{1,0:T(8,128)(2,1)S(1)} %fusion.refs_0_), channel_id=1, source_target_pairs={{0,16},{2,18},{4,20},{6,22},{8,24},{10,26},{12,28},{14,30},{16,0},... | collective-permute-start | bytes 393224 | tf_op jit(solution)/shard_map/ppermute | solution.py:22
  51.2 11.7 %collective-permute-start.26 = (bf16[512,128]{1,0:T(8,128)(2,1)S(1)}, bf16[512,128]{1,0:T(8,128)(2,1)S(1)}, u32[]{:S(2)}, u32[]{:S(2)}) collective-permute-start(bf16[512,128]{1,0:T(8,128)(2,1)S(1)} %fusion.refs_0_), channel_id=1, source_target_pairs={{0,8},{2,10},{4,12},{6,14},{8,0},{10,2},{12,4},{14,6},{16,24},{18,... | collective-permute-start | bytes 393224 | tf_op jit(solution)/shard_map/ppermute | solution.py:22
  52.6 11.6 %collective-permute-start.24 = (bf16[512,128]{1,0:T(8,128)(2,1)S(1)}, bf16[512,128]{1,0:T(8,128)(2,1)S(1)}, u32[]{:S(2)}, u32[]{:S(2)}) collective-permute-start(bf16[512,128]{1,0:T(8,128)(2,1)S(1)} %fusion.refs_0_), channel_id=1, source_target_pairs={{0,4},{2,6},{4,0},{6,2},{8,12},{10,14},{12,8},{14,10},{16,20},{18,... | collective-permute-start | bytes 393224 | tf_op jit(solution)/shard_map/ppermute | solution.py:22
  54.8 10.8 %collective-permute-start.23 = (bf16[512,128]{1,0:T(8,128)(2,1)S(1)}, bf16[512,128]{1,0:T(8,128)(2,1)S(1)}, u32[]{:S(2)}, u32[]{:S(2)}) collective-permute-start(bf16[512,128]{1,0:T(8,128)(2,1)S(1)} %fusion.refs_0_), channel_id=1, source_target_pairs={{0,1},{1,0},{2,3},{3,2},{4,5},{5,4},{6,7},{7,6},{8,9},{9,8},{10,11... | collective-permute-start | bytes 393224 | tf_op jit(solution)/shard_map/ppermute | solution.py:22
  56.4 10.0 %collective-permute-start.36 = (bf16[512,128]{1,0:T(8,128)(2,1)S(1)}, bf16[512,128]{1,0:T(8,128)(2,1)S(1)}, u32[]{:S(2)}, u32[]{:S(2)}) collective-permute-start(bf16[512,128]{1,0:T(8,128)(2,1)S(1)} %collective-permute-done.34.refs_12_), channel_id=1, source_target_pairs={{0,4},{2,6},{4,0},{6,2},{8,12},{10,14},{12,8},{14,10},{16,20},{18,... | collective-permute-start | bytes 393224 | tf_op jit(solution)/shard_map/ppermute | solution.py:22
  62.3 6.4 %collective-permute-start.35 = (bf16[512,128]{1,0:T(8,128)(2,1)S(1)}, bf16[512,128]{1,0:T(8,128)(2,1)S(1)}, u32[]{:S(2)}, u32[]{:S(2)}) collective-permute-start(bf16[512,128]{1,0:T(8,128)(2,1)S(1)} %collective-permute-done.34.refs_12_), channel_id=1, source_target_pairs={{0,1},{1,0},{2,3},{3,2},{4,5},{5,4},{6,7},{7,6},{8,9},{9,8},{10,11... | collective-permute-start | bytes 393224 | tf_op jit(solution)/shard_map/ppermute | solution.py:22
  62.9 7.0 %collective-permute-start.32 = (bf16[512,128]{1,0:T(8,128)(2,1)S(1)}, bf16[512,128]{1,0:T(8,128)(2,1)S(1)}, u32[]{:S(2)}, u32[]{:S(2)}) collective-permute-start(bf16[512,128]{1,0:T(8,128)(2,1)S(1)} %collective-permute-done.30.refs_8_), channel_id=1, source_target_pairs={{0,4},{2,6},{4,0},{6,2},{8,12},{10,14},{12,8},{14,10},{16,20},{18,... | collective-permute-start | bytes 393224 | tf_op jit(solution)/shard_map/ppermute | solution.py:22
  64.1 7.4 %collective-permute-start.31 = (bf16[512,128]{1,0:T(8,128)(2,1)S(1)}, bf16[512,128]{1,0:T(8,128)(2,1)S(1)}, u32[]{:S(2)}, u32[]{:S(2)}) collective-permute-start(bf16[512,128]{1,0:T(8,128)(2,1)S(1)} %collective-permute-done.30.refs_8_), channel_id=1, source_target_pairs={{0,1},{1,0},{2,3},{3,2},{4,5},{5,4},{6,7},{7,6},{8,9},{9,8},{10,11... | collective-permute-start | bytes 393224 | tf_op jit(solution)/shard_map/ppermute | solution.py:22
  65.6 7.1 %collective-permute-start.28 = (bf16[512,128]{1,0:T(8,128)(2,1)S(1)}, bf16[512,128]{1,0:T(8,128)(2,1)S(1)}, u32[]{:S(2)}, u32[]{:S(2)}) collective-permute-start(bf16[512,128]{1,0:T(8,128)(2,1)S(1)} %collective-permute-done.26.refs_4_), channel_id=1, source_target_pairs={{0,4},{2,6},{4,0},{6,2},{8,12},{10,14},{12,8},{14,10},{16,20},{18,... | collective-permute-start | bytes 393224 | tf_op jit(solution)/shard_map/ppermute | solution.py:22
  66.4 13.6 %collective-permute-start.27 = (bf16[512,128]{1,0:T(8,128)(2,1)S(1)}, bf16[512,128]{1,0:T(8,128)(2,1)S(1)}, u32[]{:S(2)}, u32[]{:S(2)}) collective-permute-start(bf16[512,128]{1,0:T(8,128)(2,1)S(1)} %collective-permute-done.26.refs_4_), channel_id=1, source_target_pairs={{0,1},{1,0},{2,3},{3,2},{4,5},{5,4},{6,7},{7,6},{8,9},{9,8},{10,11... | collective-permute-start | bytes 393224 | tf_op jit(solution)/shard_map/ppermute | solution.py:22
  68.7 11.3 %collective-permute-start.25 = (bf16[512,128]{1,0:T(8,128)(2,1)S(1)}, bf16[512,128]{1,0:T(8,128)(2,1)S(1)}, u32[]{:S(2)}, u32[]{:S(2)}) collective-permute-start(bf16[512,128]{1,0:T(8,128)(2,1)S(1)} %collective-permute-done.23.refs_1_), channel_id=1, source_target_pairs={{0,4},{2,6},{4,0},{6,2},{8,12},{10,14},{12,8},{14,10},{16,20},{18,... | collective-permute-start | bytes 393224 | tf_op jit(solution)/shard_map/ppermute | solution.py:22
  69.9 10.0 %collective-permute-start.37 = (bf16[512,128]{1,0:T(8,128)(2,1)S(1)}, bf16[512,128]{1,0:T(8,128)(2,1)S(1)}, u32[]{:S(2)}, u32[]{:S(2)}) collective-permute-start(bf16[512,128]{1,0:T(8,128)(2,1)S(1)} %collective-permute-done.36.refs_14_), channel_id=1, source_target_pairs={{0,1},{1,0},{2,3},{3,2},{4,5},{5,4},{6,7},{7,6},{8,9},{9,8},{10,11... | collective-permute-start | bytes 393224 | tf_op jit(solution)/shard_map/ppermute | solution.py:22
  71.5 8.5 %collective-permute-start.33 = (bf16[512,128]{1,0:T(8,128)(2,1)S(1)}, bf16[512,128]{1,0:T(8,128)(2,1)S(1)}, u32[]{:S(2)}, u32[]{:S(2)}) collective-permute-start(bf16[512,128]{1,0:T(8,128)(2,1)S(1)} %collective-permute-done.31.refs_9_), channel_id=1, source_target_pairs={{0,4},{2,6},{4,0},{6,2},{8,12},{10,14},{12,8},{14,10},{16,20},{18,... | collective-permute-start | bytes 393224 | tf_op jit(solution)/shard_map/ppermute | solution.py:22
  72.8 7.2 %collective-permute-start.29 = (bf16[512,128]{1,0:T(8,128)(2,1)S(1)}, bf16[512,128]{1,0:T(8,128)(2,1)S(1)}, u32[]{:S(2)}, u32[]{:S(2)}) collective-permute-start(bf16[512,128]{1,0:T(8,128)(2,1)S(1)} %collective-permute-done.28.refs_6_), channel_id=1, source_target_pairs={{0,1},{1,0},{2,3},{3,2},{4,5},{5,4},{6,7},{7,6},{8,9},{9,8},{10,11... | collective-permute-start | bytes 393224 | tf_op jit(solution)/shard_map/ppermute | solution.py:22
  (17 other events, 94.1 us)

commit v2 on v1

--- a/solution.py
+++ b/solution.py
@@ -9,7 +9,7 @@
 
 
 BLK = 128
-GROUP = 8
+GROUP = 12
 BACK = 4
 PART = 512
 LANES = 128
@@ -231,51 +231,78 @@
     return lax.fori_loop(0, steps, step, jnp.zeros((BLK, width), F32))
 
 
-def first_kernel(nb, slots, counts, narrow, plan, v_own, v_far, *refs):
-    groups, (keep, send, src, sems) = split(refs, counts)
+def times_rows(nb, slots, first, plan, vals, source, ref, narrow):
     lk, lx, ln = plan_parts(plan, nb, slots)
+
+    def row(i, carry):
+        acc = rows_product(slots, first + i, i, lk, lx, ln, vals, source, source.shape[1])
+        put(ref, row_of(i, BLK), acc, narrow)
+        return carry
+
+    lax.fori_loop(0, nb, row, 0)
+
+
+def first_far_kernel(nb, slots, counts, narrow, plan, vals, *refs):
+    groups, (src, send, sems) = split(refs, counts)
     copies = load(groups, src, sems)
-    width = src.shape[1]
-    src[src.shape[0] - BLK :, :] = jnp.zeros((BLK, width), BF16)
+    src[src.shape[0] - BLK :, :] = jnp.zeros((BLK, src.shape[1]), BF16)
     for copy in copies:
         copy.wait()
-    for half, (vals, ref) in enumerate(((v_own, keep), (v_far, send))):
-
-        def row(i, carry, half=half, vals=vals, ref=ref):
-            r = half * nb + i
-            acc = rows_product(slots, r, i, lk, lx, ln, vals, src, width)
-            put(ref, row_of(i, BLK), acc, narrow)
-            return carry
-
-        lax.fori_loop(0, nb, row, 0)
-
-
-def second_kernel(
-    nb, slots, counts, narrow, plan, w1, w2, v_own, v_far, hg, hg_far, *refs
-):
-    lk, lx, ln = plan_parts(plan, nb, slots)
-    groups, (keep, send, gkeep, gsend, agg, hid, cot, mix, total, sems) = split(refs, counts)
-    copies = load(groups[:-2], agg, sems)
-    more = load(groups[-2:], cot, sems, len(copies))
-    blocks, width = agg.shape
-    chunk = nb * BLK
-    hid[blocks:, :] = jnp.zeros((BLK, width), BF16)
-    for copy in copies:
-        copy.wait()
-    total[...] = jnp.zeros_like(total)
-
-    for g in range(blocks // PART):
+    times_rows(nb, slots, nb, plan, vals, src, send, narrow)
+
+
+def first_own_kernel(nb, slots, narrow, plan, vals, src, keep):
+    times_rows(nb, slots, 0, plan, vals, src, keep, narrow)
+
+
+def activate(agg, w1, hg, hg_far, hid, total, places):
+    for g in range(agg.shape[0] // PART):
         rows = pl.ds(g * PART, PART)
+        there = pl.ds(places + g * PART, PART)
         a = agg[rows, :]
         first = jnp.dot(a, w1[...], preferred_element_type=F32)
         sig = 0.5 * jnp.tanh(0.5 * first) + 0.5
         act = first * sig
-        hid[rows, :] = act.astype(BF16)
+        hid[there, :] = act.astype(BF16)
         slope = sig + act * (1.0 - sig)
-        grad = ((hg[rows, :] + hg_far[rows, :]) * slope).astype(BF16)
+        grad = ((hg[there, :] + hg_far[there, :]) * slope).astype(BF16)
         total[...] += lax.dot_general(
             a, grad, (((0,), (0,)), ((), ())), preferred_element_type=F32
         )
+
+
+def half_kernel(counts, w1, hg, hg_far, *refs):
+    groups, (hid, total, agg, sems) = split(refs, counts)
+    copies = load(groups, agg, sems)
+    total[...] = jnp.zeros_like(total)
+    for copy in copies:
+        copy.wait()
+    activate(agg, w1, hg, hg_far, hid, total, 0)
+
+
+def second_kernel(
+    nb, slots, counts, narrow, plan, w1, v_own, v_far, hg, hg_far, half, *refs
+):
+    lk, lx, ln = plan_parts(plan, nb, slots)
+    part, *refs = refs
+    groups, (mix, gkeep, gsend, agg, hid, cot, total, sems) = split(
+        refs, counts
+    )
+    copies = load(groups[:-2], agg, sems)
+    more = load(groups[-2:], cot, sems, len(copies))
+    done = half.shape[0]
+    bring = pltpu.make_async_copy(
+        half, hid.at[pl.ds(0, done), :], sems.at[sum(counts)]
+    )
+    bring.start()
+    blocks, width = done + agg.shape[0], agg.shape[1]
+    chunk = nb * BLK
+    hid[blocks:, :] = jnp.zeros((BLK, width), BF16)
+    total[...] = part[...]
+    for copy in copies:
+        copy.wait()
+    activate(agg, w1, hg, hg_far, hid, total, done)
+    bring.wait()
     for half, vals in enumerate((v_own, v_far)):
 
         def row(i, carry, half=half, vals=vals):
@@ -303,6 +330,9 @@
         put(gkeep, everything, second, narrow)
         put(gsend, everything, total[...], narrow)
 
+
+def out_kernel(narrow, mix, w2, keep, send):
+    chunk = keep.shape[0]
     for half, ref in enumerate((keep, send)):
         mine = mix[half * chunk : (half + 1) * chunk, :]
         value = jnp.dot(mine, w2[...], preferred_element_type=F32)
@@ -395,17 +425,23 @@
     counts = tuple(len(g) for g in chunks)
     if pieces > 1:
         chunks[0][0] = in_hbm(feats)
-    keep, send = call(
-        functools.partial(first_kernel, nb, slots, counts, narrow),
-        [((rows, width), F32), ((rows, width), BF16)],
+    src, send = call(
+        functools.partial(first_far_kernel, nb, slots, counts, narrow),
+        [((blocks + BLK, width), BF16), ((rows, width), BF16)],
         [vmem()] * 2,
-        [smem()] + [vmem()] * 2 + [any_spec()] * sum(counts),
-        [
-            pltpu.VMEM((blocks + BLK, width), BF16),
-            pltpu.SemaphoreType.DMA((sum(counts),)),
-        ],
-        (plan, v_own, v_far, *[p for g in chunks for p in g]),
-        dense,
+        [smem(), vmem()] + [any_spec()] * sum(counts),
+        [pltpu.SemaphoreType.DMA((sum(counts),))],
+        (plan, v_far, *[p for g in chunks for p in g]),
+        dense // 2,
+    )
+    (keep,) = call(
+        functools.partial(first_own_kernel, nb, slots, narrow),
+        [((rows, width), F32)],
+        [vmem()],
+        [smem(), vmem(), vmem()],
+        [],
+        (plan, v_own, src),
+        dense // 2,
     )
 
     def back(first, vals, pieces):
@@ -445,29 +481,51 @@
     agg = reduce_rows(keep, send).astype(BF16)
 
     chunks = gather(widen(agg), pieces)
-    groups = chunks + [cot_own, cot_far]
+    early = (len(chunks) + 1) // 2
+    counts = tuple(len(g) for g in chunks[:early])
+    half, total = call(
+        functools.partial(half_kernel, counts),
+        [((early * rows, width), BF16), ((width, width), F32)],
+        [vmem()] * 2,
+        [vmem()] * 3 + [any_spec()] * sum(counts),
+        [
+            pltpu.VMEM((early * rows, width), BF16),
+            pltpu.SemaphoreType.DMA((sum(counts),)),
+        ],
+        (w_first, hg, hg_far, *[p for g in chunks[:early] for p in g]),
+        dense,
+    )
+    groups = chunks[early:] + [cot_own, cot_far]
     counts = tuple(len(g) for g in groups)
-    keep, send, gkeep, gsend = call(
+    mix, gkeep, gsend = call(
         functools.partial(second_kernel, nb, slots, counts, narrow),
         [
-            ((rows, width), F32),
-            ((rows, width), BF16),
+            ((2 * rows, width), BF16),
             ((width, width), F32),
             ((width, width), BF16),
         ],
-        [vmem()] * 4,
-        [smem()] + [vmem()] * 6 + [any_spec()] * sum(counts),
+        [vmem()] * 3,
+        [smem()] + [vmem()] * 7 + [any_spec()] * sum(counts),
         [
-            pltpu.VMEM((blocks, width), BF16),
+            pltpu.VMEM((blocks - early * rows, width), BF16),
             pltpu.VMEM((blocks + BLK, width), BF16),
             pltpu.VMEM((2 * rows, width), BF16),
-            pltpu.VMEM((2 * rows, width), BF16),
             pltpu.VMEM((width, width), F32),
-            pltpu.SemaphoreType.DMA((sum(counts),)),
+            pltpu.SemaphoreType.DMA((sum(counts) + 1,)),
         ],
-        (plan, w_first, w_second, v_own, v_far, hg, hg_far)
+        (plan, w_first, v_own, v_far, hg, hg_far, half, total)
         + tuple(p for g in groups for p in g),
-        4 * dense,
+        2 * dense,
+    )
+
+    keep, send = call(
+        functools.partial(out_kernel, narrow),
+        [((rows, width), F32), ((rows, width), BF16)],
+        [vmem()] * 2,
+        [vmem()] * 2,
+        [],
+        (mix, w_second),
+        dense // 8,
     )
 
     part = gkeep + swap(gsend, "dom", 1).astype(F32)

time: 110 us -> 107 us (0.973)
  starting transfers between devices: 50.2 us -> 46.6 us
    ppermute x46, starting transfers between devices: 50.2 us -> 46.6 us  [swap(): return lax.ppermute(value, axis, [(i, i ^ mask) for i in range(size)])]
    pallas_call x6 -> x9, Pallas kernels: 19.6 us -> 20.6 us  [call(): pl.pallas_call(kernel, out_shape=tuple((jax.ShapeDtypeStruct(*o) for o in...]
  transfers between devices with their start and end apart: 46 -> 46, of which waited for: 19 -> 16; matrix products, arithmetic and copies ran while one was open for 1% -> 1% of each run, Pallas kernels for 8% -> 12%
where the time goes in v2:
time: 107 us
  starting transfers between devices  46.6 us (44%)
  waiting for transfers between devices  38 us (36%)
  Pallas kernels  20.6 us (19%)
    ppermute x46, starting transfers between devices, swap(): return lax.ppermute(value, axis, [(i, i ^ mask) for i in range(size)])  46.6 us
    ppermute x46, waiting for transfers between devices, swap(): return lax.ppermute(value, axis, [(i, i ^ mask) for i in range(size)])  38 us
    pallas_call x9, Pallas kernels, call(): pl.pallas_call(kernel, out_shape=tuple((jax.ShapeDtypeStruct(*o) for o in...  20.6 us
  transfers between devices with their start and end apart: 46, of which 16 were waited for; matrix products, arithmetic and copies ran while one was open for 1% of the time, Pallas kernels for 12%

profile of v2, /device:TPU:0, one launch (start us, length us, event | category | flops | bytes accessed | tf_op | source)
XLA Modules:
  0.0 107.2 jit_solution(9413242632318549906)
XLA Ops:
  1.2 2.6 %collective-permute-start.9 = (bf16[512,128]{1,0:T(8,128)(2,1)}, bf16[512,128]{1,0:T(8,128)(2,1)S(1)}, u32[]{:S(2)}, u32[]{:S(2)}) collective-permute-start(bf16[512,128]{1,0:T(8,128)(2,1)} %refs_0_.5), channel_id=1, source_target_pairs={{0,8},{2,10},{4,12},{6,14},{8,0},{10,2},{12,4},{14,6},{16,24},{18,... | collective-permute-start | bytes 393224 | tf_op jit(solution)/shard_map/ppermute | solution.py:22
  3.8 2.6 %collective-permute-start.13 = (bf16[512,128]{1,0:T(8,128)(2,1)}, bf16[512,128]{1,0:T(8,128)(2,1)S(1)}, u32[]{:S(2)}, u32[]{:S(2)}) collective-permute-start(bf16[512,128]{1,0:T(8,128)(2,1)} %refs_0_.5), channel_id=1, source_target_pairs={{0,16},{2,18},{4,20},{6,22},{8,24},{10,26},{12,28},{14,30},{16,0},... | collective-permute-start | bytes 393224 | tf_op jit(solution)/shard_map/ppermute | solution.py:22
  9.1 1.7 %collective-permute-start.6 = (bf16[512,128]{1,0:T(8,128)(2,1)}, bf16[512,128]{1,0:T(8,128)(2,1)S(1)}, u32[]{:S(2)}, u32[]{:S(2)}) collective-permute-start(bf16[512,128]{1,0:T(8,128)(2,1)} %refs_0_.5), channel_id=1, source_target_pairs={{0,1},{1,0},{2,3},{3,2},{4,5},{5,4},{6,7},{7,6},{8,9},{9,8},{10,11... | collective-permute-start | bytes 393224 | tf_op jit(solution)/shard_map/ppermute | solution.py:22
  12.3 4.6 %collective-permute-done.13.refs_8_ = bf16[512,128]{1,0:T(8,128)(2,1)S(1)} collective-permute-done((bf16[512,128]{1,0:T(8,128)(2,1)}, bf16[512,128]{1,0:T(8,128)(2,1)S(1)}, u32[]{:S(2)}, u32[]{:S(2)}) %collective-permute-start.13) | collective-permute-done | bytes 131104 | tf_op jit(solution)/shard_map/ppermute | solution.py:22
  17.0 1.5 %collective-permute-start.11 = (bf16[512,128]{1,0:T(8,128)(2,1)S(1)}, bf16[512,128]{1,0:T(8,128)(2,1)S(1)}, u32[]{:S(2)}, u32[]{:S(2)}) collective-permute-start(bf16[512,128]{1,0:T(8,128)(2,1)S(1)} %collective-permute-done.9.refs_4_), channel_id=1, source_target_pairs={{0,4},{2,6},{4,0},{6,2},{8,12},{10,14},{12,8},{14,10},{16,20},{18,... | collective-permute-start | bytes 393224 | tf_op jit(solution)/shard_map/ppermute | solution.py:22
  18.5 1.5 %collective-permute-start.14 = (bf16[512,128]{1,0:T(8,128)(2,1)S(1)}, bf16[512,128]{1,0:T(8,128)(2,1)S(1)}, u32[]{:S(2)}, u32[]{:S(2)}) collective-permute-start(bf16[512,128]{1,0:T(8,128)(2,1)S(1)} %collective-permute-done.13.refs_8_), channel_id=1, source_target_pairs={{0,1},{1,0},{2,3},{3,2},{4,5},{5,4},{6,7},{7,6},{8,9},{9,8},{10,11... | collective-permute-start | bytes 393224 | tf_op jit(solution)/shard_map/ppermute | solution.py:22
  21.0 2.3 %collective-permute-done.11.refs_6_ = bf16[512,128]{1,0:T(8,128)(2,1)S(1)} collective-permute-done((bf16[512,128]{1,0:T(8,128)(2,1)S(1)}, bf16[512,128]{1,0:T(8,128)(2,1)S(1)}, u32[]{:S(2)}, u32[]{:S(2)}) %collective-permute-start.11) | collective-permute-done | bytes 131104 | tf_op jit(solution)/shard_map/ppermute | solution.py:22
  23.3 1.5 %collective-permute-start.15 = (bf16[512,128]{1,0:T(8,128)(2,1)S(1)}, bf16[512,128]{1,0:T(8,128)(2,1)S(1)}, u32[]{:S(2)}, u32[]{:S(2)}) collective-permute-start(bf16[512,128]{1,0:T(8,128)(2,1)S(1)} %collective-permute-done.13.refs_8_), channel_id=1, source_target_pairs={{0,4},{2,6},{4,0},{6,2},{8,12},{10,14},{12,8},{14,10},{16,20},{18,... | collective-permute-start | bytes 393224 | tf_op jit(solution)/shard_map/ppermute | solution.py:22
  24.8 1.5 %collective-permute-start.18 = (bf16[512,128]{1,0:T(8,128)(2,1)S(1)}, bf16[512,128]{1,0:T(8,128)(2,1)S(1)}, u32[]{:S(2)}, u32[]{:S(2)}) collective-permute-start(bf16[512,128]{1,0:T(8,128)(2,1)S(1)} %collective-permute-done.17.refs_12_), channel_id=1, source_target_pairs={{0,1},{1,0},{2,3},{3,2},{4,5},{5,4},{6,7},{7,6},{8,9},{9,8},{10,11... | collective-permute-start | bytes 393224 | tf_op jit(solution)/shard_map/ppermute | solution.py:22
  27.6 1.5 %collective-permute-start.12 = (bf16[512,128]{1,0:T(8,128)(2,1)S(1)}, bf16[512,128]{1,0:T(8,128)(2,1)S(1)}, u32[]{:S(2)}, u32[]{:S(2)}) collective-permute-start(bf16[512,128]{1,0:T(8,128)(2,1)S(1)} %collective-permute-done.11.refs_6_), channel_id=1, source_target_pairs={{0,1},{1,0},{2,3},{3,2},{4,5},{5,4},{6,7},{7,6},{8,9},{9,8},{10,11... | collective-permute-start | bytes 393224 | tf_op jit(solution)/shard_map/ppermute | solution.py:22
  29.2 1.7 %collective-permute-start.16 = (bf16[512,128]{1,0:T(8,128)(2,1)S(1)}, bf16[512,128]{1,0:T(8,128)(2,1)S(1)}, u32[]{:S(2)}, u32[]{:S(2)}) collective-permute-start(bf16[512,128]{1,0:T(8,128)(2,1)S(1)} %collective-permute-done.14.refs_9_), channel_id=1, source_target_pairs={{0,4},{2,6},{4,0},{6,2},{8,12},{10,14},{12,8},{14,10},{16,20},{18,... | collective-permute-start | bytes 393224 | tf_op jit(solution)/shard_map/ppermute | solution.py:22
  31.9 2.4 %shard_map.94 = (s32[456]{0:T(512)S(1)}, bf16[4,16,128,128]{3,2,1,0:T(8,128)(2,1)S(1)}) custom-call(s32[4,32]{1,0:T(4,128)} %refs_0_.3, s32[4]{0:T(128)} %refs_1_.1, s32[4,32]{1,0:T(4,128)S(1)} %collective-permute-done.refs_2_, s32[4]{0:T(128)S(1)} %collective-permute-done.1.refs_3_, bf16[4,16,128,128]{3,2,1,0:T(8,128)(2,1)} %refs_4_.1), custom_call_target="tpu_custom_call" | custom-call | flops 1048576 | bytes 4194304 | tf_op jit(solution)/shard_map/pallas_call | solution.py:373
  35.9 2.6 %shard_map.97 = (bf16[4224,256]{1,0:T(8,128)(2,1)S(1)}, bf16[512,256]{1,0:T(8,128)(2,1)S(1)}) custom-call(s32[456]{0:T(512)S(1)} %get-tuple-element.16.plan, bf16[4,16,128,128]{3,2,1,0:T(8,128)(2,1)S(1)} %collective-permute-done.2.vals.v_far, bf16[512,128]{1,0:T(8,128)(2,1)} %refs_0_.5, bf16[512,128]{1,0:T(8,128)(2,1)S(1)} %collective-permute-done.6.refs_1_, ...), custom_call_target="tpu_custom_call" | custom-call | flops 268435456 | bytes 4194304 | tf_op jit(solution)/shard_map/pallas_call | solution.py:373
  39.7 1.8 %shard_map.98 = f32[512,256]{1,0:T(8,128)S(1)} custom-call(s32[456]{0:T(512)S(1)} %get-tuple-element.16.plan, bf16[4,16,128,128]{3,2,1,0:T(8,128)(2,1)S(1)} %get-tuple-element.17.vals.v_own, bf16[4224,256]{1,0:T(8,128)(2,1)S(1)} %get-tuple-element.18.src), custom_call_target="tpu_custom_call" | custom-call | flops 268435456 | bytes 4194304 | tf_op jit(solution)/shard_map/pallas_call | solution.py:373
  42.3 2.2 %collective-permute-done.3.refs_1_.refs_10_ = bf16[512,128]{1,0:T(8,128)(2,1)S(1)} collective-permute-done((bf16[512,128]{1,0:T(8,128)(2,1)S(1)}, bf16[512,128]{1,0:T(8,128)(2,1)S(1)}, u32[]{:S(2)}, u32[]{:S(2)}) %collective-permute-start.3) | collective-permute-done | bytes 131104 | tf_op jit(solution)/shard_map/ppermute | solution.py:22
  44.5 2.8 %collective-permute-done.22 = bf16[512,128]{1,0:T(8,128)(2,1)S(1)} collective-permute-done((bf16[512,128]{1,0:T(8,128)(2,1)S(1)}, bf16[512,128]{1,0:T(8,128)(2,1)S(1)}, u32[]{:S(2)}, u32[]{:S(2)}) %collective-permute-start.22) | collective-permute-done | bytes 131104 | tf_op jit(solution)/shard_map/ppermute | solution.py:22
  49.1 1.8 %collective-permute-start.24 = (bf16[512,128]{1,0:T(8,128)(2,1)S(1)}, bf16[512,128]{1,0:T(8,128)(2,1)S(1)}, u32[]{:S(2)}, u32[]{:S(2)}) collective-permute-start(bf16[512,128]{1,0:T(8,128)(2,1)S(1)} %fusion.refs_0_), channel_id=1, source_target_pairs={{0,4},{2,6},{4,0},{6,2},{8,12},{10,14},{12,8},{14,10},{16,20},{18,... | collective-permute-start | bytes 393224 | tf_op jit(solution)/shard_map/ppermute | solution.py:22
  51.5 1.8 %collective-permute-start.34 = (bf16[512,128]{1,0:T(8,128)(2,1)S(1)}, bf16[512,128]{1,0:T(8,128)(2,1)S(1)}, u32[]{:S(2)}, u32[]{:S(2)}) collective-permute-start(bf16[512,128]{1,0:T(8,128)(2,1)S(1)} %fusion.refs_0_), channel_id=1, source_target_pairs={{0,24},{2,26},{4,28},{6,30},{8,16},{10,18},{12,20},{14,22},{16,8},... | collective-permute-start | bytes 393224 | tf_op jit(solution)/shard_map/ppermute | solution.py:22
  53.3 1.5 %collective-permute-start.28 = (bf16[512,128]{1,0:T(8,128)(2,1)S(1)}, bf16[512,128]{1,0:T(8,128)(2,1)S(1)}, u32[]{:S(2)}, u32[]{:S(2)}) collective-permute-start(bf16[512,128]{1,0:T(8,128)(2,1)S(1)} %collective-permute-done.26.refs_4_), channel_id=1, source_target_pairs={{0,4},{2,6},{4,0},{6,2},{8,12},{10,14},{12,8},{14,10},{16,20},{18,... | collective-permute-start | bytes 393224 | tf_op jit(solution)/shard_map/ppermute | solution.py:22
  56.7 5.8 %collective-permute-done.30.refs_1_ = bf16[512,128]{1,0:T(8,128)(2,1)S(1)} collective-permute-done((bf16[512,128]{1,0:T(8,128)(2,1)S(1)}, bf16[512,128]{1,0:T(8,128)(2,1)S(1)}, u32[]{:S(2)}, u32[]{:S(2)}) %collective-permute-start.30) | collective-permute-done | bytes 131104 | tf_op jit(solution)/shard_map/ppermute | solution.py:22
  67.2 1.6 %collective-permute-done.31.refs_2_ = bf16[512,128]{1,0:T(8,128)(2,1)S(1)} collective-permute-done((bf16[512,128]{1,0:T(8,128)(2,1)S(1)}, bf16[512,128]{1,0:T(8,128)(2,1)S(1)}, u32[]{:S(2)}, u32[]{:S(2)}) %collective-permute-start.31) | collective-permute-done | bytes 131104 | tf_op jit(solution)/shard_map/ppermute | solution.py:22
  70.7 3.2 %shard_map.95.hg = f32[4224,256]{1,0:T(8,128)S(1)} custom-call(s32[456]{0:T(512)S(1)} %get-tuple-element.16.plan, bf16[256,256]{1,0:T(8,128)(2,1)S(1)} %copy-done, bf16[4,16,128,128]{3,2,1,0:T(8,128)(2,1)S(1)} %get-tuple-element.17.vals.v_own, bf16[512,128]{1,0:T(8,128)(2,1)S(1)} %copy-done.2, bf16[512,128]{1,0:T(8,128)(2,1)S(1)} %collective-permute-done.3.refs_1_.refs_10_), custom_call_target="tpu_custom_call" | custom-call | flops 268435456 | bytes 4194304 | tf_op jit(solution)/shard_map/pallas_call | solution.py:373
  73.9 3.2 %shard_map.96.hg_far = f32[4224,256]{1,0:T(8,128)S(1)} custom-call(s32[456]{0:T(512)S(1)} %get-tuple-element.16.plan, bf16[256,256]{1,0:T(8,128)(2,1)S(1)} %copy-done, bf16[4,16,128,128]{3,2,1,0:T(8,128)(2,1)S(1)} %collective-permute-done.2.vals.v_far, bf16[512,128]{1,0:T(8,128)(2,1)S(1)} %collective-permute-done.4.refs_0_.refs_11_, ...), custom_call_target="tpu_custom_call" | custom-call | flops 268435456 | bytes 4194304 | tf_op jit(solution)/shard_map/pallas_call | solution.py:373
  78.7 4.8 %shard_map.100 = (bf16[1024,256]{1,0:T(8,128)(2,1)S(1)}, f32[256,256]{1,0:T(8,128)S(1)}, bf16[256,256]{1,0:T(8,128)(2,1)S(1)}) custom-call(s32[456]{0:T(512)S(1)} %get-tuple-element.16.plan, bf16[256,256]{1,0:T(8,128)(2,1)S(1)} %copy-done.1, bf16[4,16,128,128]{3,2,1,0:T(8,128)(2,1)S(1)} %get-tuple-element.17.vals.v_own, ...), custom_call_target="tpu_custom_call" | custom-call | flops 1073741824 | bytes 4194304 | tf_op jit(solution)/shard_map/pallas_call | solution.py:373
  85.0 4.3 %collective-permute-done.41 = bf16[256,128]{1,0:T(8,128)(2,1)S(1)} collective-permute-done((bf16[256,128]{1,0:T(8,128)(2,1)S(1)}, bf16[256,128]{1,0:T(8,128)(2,1)S(1)}, u32[]{:S(2)}, u32[]{:S(2)}) %collective-permute-start.41) | collective-permute-done | bytes 65568 | tf_op jit(solution)/shard_map/ppermute | solution.py:22
  89.3 2.1 %collective-permute-start.42 = (bf16[256,128]{1,0:T(8,128)(2,1)S(1)}, bf16[256,128]{1,0:T(8,128)(2,1)S(1)}, u32[]{:S(2)}, u32[]{:S(2)}) collective-permute-start(bf16[256,128]{1,0:T(8,128)(2,1)S(1)} %fusion.1), channel_id=1, source_target_pairs={{0,4},{2,6},{4,0},{6,2},{8,12},{10,14},{12,8},{14,10},{16,20},{18,... | collective-permute-start | bytes 196616 | tf_op jit(solution)/shard_map/ppermute | solution.py:22
  91.4 2.3 %collective-permute-done.42 = bf16[256,128]{1,0:T(8,128)(2,1)S(1)} collective-permute-done((bf16[256,128]{1,0:T(8,128)(2,1)S(1)}, bf16[256,128]{1,0:T(8,128)(2,1)S(1)}, u32[]{:S(2)}, u32[]{:S(2)}) %collective-permute-start.42) | collective-permute-done | bytes 65568 | tf_op jit(solution)/shard_map/ppermute | solution.py:22
  93.7 2.1 %collective-permute-start.43 = (bf16[256,128]{1,0:T(8,128)(2,1)S(1)}, bf16[256,128]{1,0:T(8,128)(2,1)S(1)}, u32[]{:S(2)}, u32[]{:S(2)}) collective-permute-start(bf16[256,128]{1,0:T(8,128)(2,1)S(1)} %add_convert_fusion.1), channel_id=1, source_target_pairs={{0,8},{2,10},{4,12},{6,14},{8,0},{10,2},{12,4},{14,6},{16,24},{18,... | collective-permute-start | bytes 196616 | tf_op jit(solution)/shard_map/ppermute | solution.py:22
  96.2 1.8 %collective-permute-done.43 = bf16[256,128]{1,0:T(8,128)(2,1)S(1)} collective-permute-done((bf16[256,128]{1,0:T(8,128)(2,1)S(1)}, bf16[256,128]{1,0:T(8,128)(2,1)S(1)}, u32[]{:S(2)}, u32[]{:S(2)}) %collective-permute-start.43) | collective-permute-done | bytes 65568 | tf_op jit(solution)/shard_map/ppermute | solution.py:22
  98.0 2.5 %collective-permute-start.44 = (bf16[256,128]{1,0:T(8,128)(2,1)S(1)}, bf16[256,128]{1,0:T(8,128)(2,1)S(1)}, u32[]{:S(2)}, u32[]{:S(2)}) collective-permute-start(bf16[256,128]{1,0:T(8,128)(2,1)S(1)} %add_convert_fusion), channel_id=1, source_target_pairs={{0,16},{2,18},{4,20},{6,22},{8,24},{10,26},{12,28},{14,30},{16,0},... | collective-permute-start | bytes 196616 | tf_op jit(solution)/shard_map/ppermute | solution.py:22
  100.8 2.4 %collective-permute-done.44 = bf16[256,128]{1,0:T(8,128)(2,1)S(1)} collective-permute-done((bf16[256,128]{1,0:T(8,128)(2,1)S(1)}, bf16[256,128]{1,0:T(8,128)(2,1)S(1)}, u32[]{:S(2)}, u32[]{:S(2)}) %collective-permute-start.44) | collective-permute-done | bytes 65568 | tf_op jit(solution)/shard_map/ppermute | solution.py:22
  103.4 2.4 %collective-permute-done.39 = bf16[512,128]{1,0:T(8,128)(2,1)S(1)} collective-permute-done((bf16[512,128]{1,0:T(8,128)(2,1)S(1)}, bf16[512,128]{1,0:T(8,128)(2,1)S(1)}, u32[]{:S(2)}, u32[]{:S(2)}) %collective-permute-start.39) | collective-permute-done | bytes 131104 | tf_op jit(solution)/shard_map/ppermute | solution.py:22
  (87 shorter events, 27.7 us)
Async XLA Ops:
  0.6 35.2 %collective-permute-start.2 = (bf16[4,16,128,128]{3,2,1,0:T(8,128)(2,1)}, bf16[4,16,128,128]{3,2,1,0:T(8,128)(2,1)S(1)}, u32[]{:S(2)}, u32[]{:S(2)}) collective-permute-start(bf16[4,16,128,128]{3,2,1,0:T(8,128)(2,1)} %refs_4_.1), channel_id=1, source_target_pairs={{0,2},{2,0},{4,6},{6,4},{8,10},{10,8},{12,14},{14,12},{16,18},{18,... | collective-permute-start | bytes 6291464 | tf_op jit(solution)/shard_map/ppermute | solution.py:22
  1.2 9.6 %collective-permute-start.9 = (bf16[512,128]{1,0:T(8,128)(2,1)}, bf16[512,128]{1,0:T(8,128)(2,1)S(1)}, u32[]{:S(2)}, u32[]{:S(2)}) collective-permute-start(bf16[512,128]{1,0:T(8,128)(2,1)} %refs_0_.5), channel_id=1, source_target_pairs={{0,8},{2,10},{4,12},{6,14},{8,0},{10,2},{12,4},{14,6},{16,24},{18,... | collective-permute-start | bytes 393224 | tf_op jit(solution)/shard_map/ppermute | solution.py:22
  3.8 13.1 %collective-permute-start.13 = (bf16[512,128]{1,0:T(8,128)(2,1)}, bf16[512,128]{1,0:T(8,128)(2,1)S(1)}, u32[]{:S(2)}, u32[]{:S(2)}) collective-permute-start(bf16[512,128]{1,0:T(8,128)(2,1)} %refs_0_.5), channel_id=1, source_target_pairs={{0,16},{2,18},{4,20},{6,22},{8,24},{10,26},{12,28},{14,30},{16,0},... | collective-permute-start | bytes 393224 | tf_op jit(solution)/shard_map/ppermute | solution.py:22
  6.4 12.0 %collective-permute-start.17 = (bf16[512,128]{1,0:T(8,128)(2,1)}, bf16[512,128]{1,0:T(8,128)(2,1)S(1)}, u32[]{:S(2)}, u32[]{:S(2)}) collective-permute-start(bf16[512,128]{1,0:T(8,128)(2,1)} %refs_0_.5), channel_id=1, source_target_pairs={{0,24},{2,26},{4,28},{6,30},{8,16},{10,18},{12,20},{14,22},{16,8},... | collective-permute-start | bytes 393224 | tf_op jit(solution)/shard_map/ppermute | solution.py:22
  9.1 10.9 %collective-permute-start.6 = (bf16[512,128]{1,0:T(8,128)(2,1)}, bf16[512,128]{1,0:T(8,128)(2,1)S(1)}, u32[]{:S(2)}, u32[]{:S(2)}) collective-permute-start(bf16[512,128]{1,0:T(8,128)(2,1)} %refs_0_.5), channel_id=1, source_target_pairs={{0,1},{1,0},{2,3},{3,2},{4,5},{5,4},{6,7},{7,6},{8,9},{9,8},{10,11... | collective-permute-start | bytes 393224 | tf_op jit(solution)/shard_map/ppermute | solution.py:22
  10.8 9.7 %collective-permute-start.7 = (bf16[512,128]{1,0:T(8,128)(2,1)}, bf16[512,128]{1,0:T(8,128)(2,1)S(1)}, u32[]{:S(2)}, u32[]{:S(2)}) collective-permute-start(bf16[512,128]{1,0:T(8,128)(2,1)} %refs_0_.5), channel_id=1, source_target_pairs={{0,4},{2,6},{4,0},{6,2},{8,12},{10,14},{12,8},{14,10},{16,20},{18,... | collective-permute-start | bytes 393224 | tf_op jit(solution)/shard_map/ppermute | solution.py:22
  17.0 6.4 %collective-permute-start.11 = (bf16[512,128]{1,0:T(8,128)(2,1)S(1)}, bf16[512,128]{1,0:T(8,128)(2,1)S(1)}, u32[]{:S(2)}, u32[]{:S(2)}) collective-permute-start(bf16[512,128]{1,0:T(8,128)(2,1)S(1)} %collective-permute-done.9.refs_4_), channel_id=1, source_target_pairs={{0,4},{2,6},{4,0},{6,2},{8,12},{10,14},{12,8},{14,10},{16,20},{18,... | collective-permute-start | bytes 393224 | tf_op jit(solution)/shard_map/ppermute | solution.py:22
  18.5 6.4 %collective-permute-start.14 = (bf16[512,128]{1,0:T(8,128)(2,1)S(1)}, bf16[512,128]{1,0:T(8,128)(2,1)S(1)}, u32[]{:S(2)}, u32[]{:S(2)}) collective-permute-start(bf16[512,128]{1,0:T(8,128)(2,1)S(1)} %collective-permute-done.13.refs_8_), channel_id=1, source_target_pairs={{0,1},{1,0},{2,3},{3,2},{4,5},{5,4},{6,7},{7,6},{8,9},{9,8},{10,11... | collective-permute-start | bytes 393224 | tf_op jit(solution)/shard_map/ppermute | solution.py:22
  20.0 6.4 %collective-permute-start.19 = (bf16[512,128]{1,0:T(8,128)(2,1)S(1)}, bf16[512,128]{1,0:T(8,128)(2,1)S(1)}, u32[]{:S(2)}, u32[]{:S(2)}) collective-permute-start(bf16[512,128]{1,0:T(8,128)(2,1)S(1)} %collective-permute-done.17.refs_12_), channel_id=1, source_target_pairs={{0,4},{2,6},{4,0},{6,2},{8,12},{10,14},{12,8},{14,10},{16,20},{18,... | collective-permute-start | bytes 393224 | tf_op jit(solution)/shard_map/ppermute | solution.py:22
  20.5 7.1 %collective-permute-start.10 = (bf16[512,128]{1,0:T(8,128)(2,1)S(1)}, bf16[512,128]{1,0:T(8,128)(2,1)S(1)}, u32[]{:S(2)}, u32[]{:S(2)}) collective-permute-start(bf16[512,128]{1,0:T(8,128)(2,1)S(1)} %collective-permute-done.9.refs_4_), channel_id=1, source_target_pairs={{0,1},{1,0},{2,3},{3,2},{4,5},{5,4},{6,7},{7,6},{8,9},{9,8},{10,11... | collective-permute-start | bytes 393224 | tf_op jit(solution)/shard_map/ppermute | solution.py:22
  23.3 5.9 %collective-permute-start.15 = (bf16[512,128]{1,0:T(8,128)(2,1)S(1)}, bf16[512,128]{1,0:T(8,128)(2,1)S(1)}, u32[]{:S(2)}, u32[]{:S(2)}) collective-permute-start(bf16[512,128]{1,0:T(8,128)(2,1)S(1)} %collective-permute-done.13.refs_8_), channel_id=1, source_target_pairs={{0,4},{2,6},{4,0},{6,2},{8,12},{10,14},{12,8},{14,10},{16,20},{18,... | collective-permute-start | bytes 393224 | tf_op jit(solution)/shard_map/ppermute | solution.py:22
  24.8 6.0 %collective-permute-start.18 = (bf16[512,128]{1,0:T(8,128)(2,1)S(1)}, bf16[512,128]{1,0:T(8,128)(2,1)S(1)}, u32[]{:S(2)}, u32[]{:S(2)}) collective-permute-start(bf16[512,128]{1,0:T(8,128)(2,1)S(1)} %collective-permute-done.17.refs_12_), channel_id=1, source_target_pairs={{0,1},{1,0},{2,3},{3,2},{4,5},{5,4},{6,7},{7,6},{8,9},{9,8},{10,11... | collective-permute-start | bytes 393224 | tf_op jit(solution)/shard_map/ppermute | solution.py:22
  26.4 8.0 %collective-permute-start.8 = (bf16[512,128]{1,0:T(8,128)(2,1)S(1)}, bf16[512,128]{1,0:T(8,128)(2,1)S(1)}, u32[]{:S(2)}, u32[]{:S(2)}) collective-permute-start(bf16[512,128]{1,0:T(8,128)(2,1)S(1)} %collective-permute-done.6.refs_1_), channel_id=1, source_target_pairs={{0,4},{2,6},{4,0},{6,2},{8,12},{10,14},{12,8},{14,10},{16,20},{18,... | collective-permute-start | bytes 393224 | tf_op jit(solution)/shard_map/ppermute | solution.py:22
  27.6 6.7 %collective-permute-start.12 = (bf16[512,128]{1,0:T(8,128)(2,1)S(1)}, bf16[512,128]{1,0:T(8,128)(2,1)S(1)}, u32[]{:S(2)}, u32[]{:S(2)}) collective-permute-start(bf16[512,128]{1,0:T(8,128)(2,1)S(1)} %collective-permute-done.11.refs_6_), channel_id=1, source_target_pairs={{0,1},{1,0},{2,3},{3,2},{4,5},{5,4},{6,7},{7,6},{8,9},{9,8},{10,11... | collective-permute-start | bytes 393224 | tf_op jit(solution)/shard_map/ppermute | solution.py:22
  38.6 5.9 %collective-permute-start.3 = (bf16[512,128]{1,0:T(8,128)(2,1)S(1)}, bf16[512,128]{1,0:T(8,128)(2,1)S(1)}, u32[]{:S(2)}, u32[]{:S(2)}) collective-permute-start(bf16[512,128]{1,0:T(8,128)(2,1)S(1)} %copy-done.2), channel_id=1, source_target_pairs={{0,1},{1,0},{2,3},{3,2},{4,5},{5,4},{6,7},{7,6},{8,9},{9,8},{10,11... | collective-permute-start | bytes 393224 | tf_op jit(solution)/shard_map/ppermute | solution.py:22
  42.1 8.7 %collective-permute-start.4 = (bf16[512,128]{1,0:T(8,128)(2,1)S(1)}, bf16[512,128]{1,0:T(8,128)(2,1)S(1)}, u32[]{:S(2)}, u32[]{:S(2)}) collective-permute-start(bf16[512,128]{1,0:T(8,128)(2,1)S(1)} %copy-done.2), channel_id=1, source_target_pairs={{0,2},{2,0},{4,6},{6,4},{8,10},{10,8},{12,14},{14,12},{16,18},{18,... | collective-permute-start | bytes 393224 | tf_op jit(solution)/shard_map/ppermute | solution.py:22
  44.5 7.0 %collective-permute-start.5 = (bf16[512,128]{1,0:T(8,128)(2,1)S(1)}, bf16[512,128]{1,0:T(8,128)(2,1)S(1)}, u32[]{:S(2)}, u32[]{:S(2)}) collective-permute-start(bf16[512,128]{1,0:T(8,128)(2,1)S(1)} %collective-permute-done.3.refs_1_.refs_10_), channel_id=1, source_target_pairs={{0,2},{2,0},{4,6},{6,4},{8,10},{10,8},{12,14},{14,12},{16,18},{18,... | collective-permute-start | bytes 393224 | tf_op jit(solution)/shard_map/ppermute | solution.py:22
  47.3 6.0 %collective-permute-start.26 = (bf16[512,128]{1,0:T(8,128)(2,1)S(1)}, bf16[512,128]{1,0:T(8,128)(2,1)S(1)}, u32[]{:S(2)}, u32[]{:S(2)}) collective-permute-start(bf16[512,128]{1,0:T(8,128)(2,1)S(1)} %fusion.refs_0_), channel_id=1, source_target_pairs={{0,8},{2,10},{4,12},{6,14},{8,0},{10,2},{12,4},{14,6},{16,24},{18,... | collective-permute-start | bytes 393224 | tf_op jit(solution)/shard_map/ppermute | solution.py:22
  48.6 6.3 %collective-permute-start.23 = (bf16[512,128]{1,0:T(8,128)(2,1)S(1)}, bf16[512,128]{1,0:T(8,128)(2,1)S(1)}, u32[]{:S(2)}, u32[]{:S(2)}) collective-permute-start(bf16[512,128]{1,0:T(8,128)(2,1)S(1)} %fusion.refs_0_), channel_id=1, source_target_pairs={{0,1},{1,0},{2,3},{3,2},{4,5},{5,4},{6,7},{7,6},{8,9},{9,8},{10,11... | collective-permute-start | bytes 393224 | tf_op jit(solution)/shard_map/ppermute | solution.py:22
  49.1 6.3 %collective-permute-start.24 = (bf16[512,128]{1,0:T(8,128)(2,1)S(1)}, bf16[512,128]{1,0:T(8,128)(2,1)S(1)}, u32[]{:S(2)}, u32[]{:S(2)}) collective-permute-start(bf16[512,128]{1,0:T(8,128)(2,1)S(1)} %fusion.refs_0_), channel_id=1, source_target_pairs={{0,4},{2,6},{4,0},{6,2},{8,12},{10,14},{12,8},{14,10},{16,20},{18,... | collective-permute-start | bytes 393224 | tf_op jit(solution)/shard_map/ppermute | solution.py:22
  50.9 11.6 %collective-permute-start.30 = (bf16[512,128]{1,0:T(8,128)(2,1)S(1)}, bf16[512,128]{1,0:T(8,128)(2,1)S(1)}, u32[]{:S(2)}, u32[]{:S(2)}) collective-permute-start(bf16[512,128]{1,0:T(8,128)(2,1)S(1)} %fusion.refs_0_), channel_id=1, source_target_pairs={{0,16},{2,18},{4,20},{6,22},{8,24},{10,26},{12,28},{14,30},{16,0},... | collective-permute-start | bytes 393224 | tf_op jit(solution)/shard_map/ppermute | solution.py:22
  51.5 11.6 %collective-permute-start.34 = (bf16[512,128]{1,0:T(8,128)(2,1)S(1)}, bf16[512,128]{1,0:T(8,128)(2,1)S(1)}, u32[]{:S(2)}, u32[]{:S(2)}) collective-permute-start(bf16[512,128]{1,0:T(8,128)(2,1)S(1)} %fusion.refs_0_), channel_id=1, source_target_pairs={{0,24},{2,26},{4,28},{6,30},{8,16},{10,18},{12,20},{14,22},{16,8},... | collective-permute-start | bytes 393224 | tf_op jit(solution)/shard_map/ppermute | solution.py:22
  53.3 10.9 %collective-permute-start.28 = (bf16[512,128]{1,0:T(8,128)(2,1)S(1)}, bf16[512,128]{1,0:T(8,128)(2,1)S(1)}, u32[]{:S(2)}, u32[]{:S(2)}) collective-permute-start(bf16[512,128]{1,0:T(8,128)(2,1)S(1)} %collective-permute-done.26.refs_4_), channel_id=1, source_target_pairs={{0,4},{2,6},{4,0},{6,2},{8,12},{10,14},{12,8},{14,10},{16,20},{18,... | collective-permute-start | bytes 393224 | tf_op jit(solution)/shard_map/ppermute | solution.py:22
  54.8 10.4 %collective-permute-start.25 = (bf16[512,128]{1,0:T(8,128)(2,1)S(1)}, bf16[512,128]{1,0:T(8,128)(2,1)S(1)}, u32[]{:S(2)}, u32[]{:S(2)}) collective-permute-start(bf16[512,128]{1,0:T(8,128)(2,1)S(1)} %collective-permute-done.23.refs_1_), channel_id=1, source_target_pairs={{0,4},{2,6},{4,0},{6,2},{8,12},{10,14},{12,8},{14,10},{16,20},{18,... | collective-permute-start | bytes 393224 | tf_op jit(solution)/shard_map/ppermute | solution.py:22
  55.4 11.2 %collective-permute-start.27 = (bf16[512,128]{1,0:T(8,128)(2,1)S(1)}, bf16[512,128]{1,0:T(8,128)(2,1)S(1)}, u32[]{:S(2)}, u32[]{:S(2)}) collective-permute-start(bf16[512,128]{1,0:T(8,128)(2,1)S(1)} %collective-permute-done.26.refs_4_), channel_id=1, source_target_pairs={{0,1},{1,0},{2,3},{3,2},{4,5},{5,4},{6,7},{7,6},{8,9},{9,8},{10,11... | collective-permute-start | bytes 393224 | tf_op jit(solution)/shard_map/ppermute | solution.py:22
  62.5 6.4 %collective-permute-start.31 = (bf16[512,128]{1,0:T(8,128)(2,1)S(1)}, bf16[512,128]{1,0:T(8,128)(2,1)S(1)}, u32[]{:S(2)}, u32[]{:S(2)}) collective-permute-start(bf16[512,128]{1,0:T(8,128)(2,1)S(1)} %collective-permute-done.30.refs_1_), channel_id=1, source_target_pairs={{0,1},{1,0},{2,3},{3,2},{4,5},{5,4},{6,7},{7,6},{8,9},{9,8},{10,11... | collective-permute-start | bytes 393224 | tf_op jit(solution)/shard_map/ppermute | solution.py:22
  63.2 6.4 %collective-permute-start.36 = (bf16[512,128]{1,0:T(8,128)(2,1)S(1)}, bf16[512,128]{1,0:T(8,128)(2,1)S(1)}, u32[]{:S(2)}, u32[]{:S(2)}) collective-permute-start(bf16[512,128]{1,0:T(8,128)(2,1)S(1)} %collective-permute-done.34.refs_5_), channel_id=1, source_target_pairs={{0,4},{2,6},{4,0},{6,2},{8,12},{10,14},{12,8},{14,10},{16,20},{18,... | collective-permute-start | bytes 393224 | tf_op jit(solution)/shard_map/ppermute | solution.py:22
  64.2 12.9 %collective-permute-start.29 = (bf16[512,128]{1,0:T(8,128)(2,1)S(1)}, bf16[512,128]{1,0:T(8,128)(2,1)S(1)}, u32[]{:S(2)}, u32[]{:S(2)}) collective-permute-start(bf16[512,128]{1,0:T(8,128)(2,1)S(1)} %collective-permute-done.28.refs_6_), channel_id=1, source_target_pairs={{0,1},{1,0},{2,3},{3,2},{4,5},{5,4},{6,7},{7,6},{8,9},{9,8},{10,11... | collective-permute-start | bytes 393224 | tf_op jit(solution)/shard_map/ppermute | solution.py:22
  65.2 13.4 %collective-permute-start.32 = (bf16[512,128]{1,0:T(8,128)(2,1)S(1)}, bf16[512,128]{1,0:T(8,128)(2,1)S(1)}, u32[]{:S(2)}, u32[]{:S(2)}) collective-permute-start(bf16[512,128]{1,0:T(8,128)(2,1)S(1)} %collective-permute-done.30.refs_1_), channel_id=1, source_target_pairs={{0,4},{2,6},{4,0},{6,2},{8,12},{10,14},{12,8},{14,10},{16,20},{18,... | collective-permute-start | bytes 393224 | tf_op jit(solution)/shard_map/ppermute | solution.py:22
  66.6 12.1 %collective-permute-start.35 = (bf16[512,128]{1,0:T(8,128)(2,1)S(1)}, bf16[512,128]{1,0:T(8,128)(2,1)S(1)}, u32[]{:S(2)}, u32[]{:S(2)}) collective-permute-start(bf16[512,128]{1,0:T(8,128)(2,1)S(1)} %collective-permute-done.34.refs_5_), channel_id=1, source_target_pairs={{0,1},{1,0},{2,3},{3,2},{4,5},{5,4},{6,7},{7,6},{8,9},{9,8},{10,11... | collective-permute-start | bytes 393224 | tf_op jit(solution)/shard_map/ppermute | solution.py:22
  68.9 9.8 %collective-permute-start.33 = (bf16[512,128]{1,0:T(8,128)(2,1)S(1)}, bf16[512,128]{1,0:T(8,128)(2,1)S(1)}, u32[]{:S(2)}, u32[]{:S(2)}) collective-permute-start(bf16[512,128]{1,0:T(8,128)(2,1)S(1)} %collective-permute-done.31.refs_2_), channel_id=1, source_target_pairs={{0,4},{2,6},{4,0},{6,2},{8,12},{10,14},{12,8},{14,10},{16,20},{18,... | collective-permute-start | bytes 393224 | tf_op jit(solution)/shard_map/ppermute | solution.py:22
  69.6 9.1 %collective-permute-start.37 = (bf16[512,128]{1,0:T(8,128)(2,1)S(1)}, bf16[512,128]{1,0:T(8,128)(2,1)S(1)}, u32[]{:S(2)}, u32[]{:S(2)}) collective-permute-start(bf16[512,128]{1,0:T(8,128)(2,1)S(1)} %collective-permute-done.36.refs_7_), channel_id=1, source_target_pairs={{0,1},{1,0},{2,3},{3,2},{4,5},{5,4},{6,7},{7,6},{8,9},{9,8},{10,11... | collective-permute-start | bytes 393224 | tf_op jit(solution)/shard_map/ppermute | solution.py:22
  (17 other events, 90.5 us)

commit v3 on v2

--- a/solution.py
+++ b/solution.py
@@ -529,15 +529,31 @@
     )
 
     part = gkeep + swap(gsend, "dom", 1).astype(F32)
-    mine = feature(part, 0)
+
+    def exchange(value, mask, axis="dom"):
+        return swap(value, axis, mask).astype(F32)
+
+    pieces = [feature(part, cx).astype(BF16) for cx in range(nc)]
+    across = []
+    if nd >= 4:
+        both = ("dom", "col")
+        for cx in range(1, nc):
+            across.append(exchange(pieces[cx], 2 * nc + cx, both))
+    mine = pieces[0].astype(F32)
     for cx in range(1, nc):
-        piece = swap(feature(part, cx).astype(BF16), "col", cx)
-        mine = mine + piece.astype(F32)
-    bit = 2
+        mine = mine + exchange(pieces[cx], cx, "col")
+    if nd >= 4:
+        mine = mine + sum(across, exchange(pieces[0], 2))
+    bit = 4
     while bit < nd:
         half = mine.astype(BF16)
-        mine = half.astype(F32) + swap(half, "dom", bit).astype(F32)
-        bit *= 2
+        if 4 * bit <= nd:
+            near, far = exchange(half, 2 * bit), exchange(half, 3 * bit)
+            mine = (half.astype(F32) + exchange(half, bit)) + (near + far)
+            bit *= 4
+        else:
+            mine = half.astype(F32) + exchange(half, bit)
+            bit *= 2
     other = swap(mine, "dom", 1)
     grad_first, grad_second = call(
         last_kernel,

time: 107 us -> 104 us (0.972)
  waiting for transfers between devices: 38 us -> 31.1 us
  starting transfers between devices: 46.6 us -> 49.7 us
    ppermute x46 -> x48, waiting for transfers between devices: 38 us -> 31.1 us  [swap(): return lax.ppermute(value, axis, [(i, i ^ mask) for i in range(size)])]
    ppermute x46 -> x48, starting transfers between devices: 46.6 us -> 49.7 us  [swap(): return lax.ppermute(value, axis, [(i, i ^ mask) for i in range(size)])]
  transfers between devices with their start and end apart: 46 -> 48, of which waited for: 16 -> 17; matrix products, arithmetic and copies ran while one was open for 1% -> 1% of each run, Pallas kernels for 12% -> 12%
where the time goes in v3:
time: 104 us; the launch traced here: 103 us
  starting transfers between devices  49.7 us (48%)
  waiting for transfers between devices  31.1 us (30%)
  Pallas kernels  20.6 us (20%)
    ppermute x48, starting transfers between devices, swap(): return lax.ppermute(value, axis, [(i, i ^ mask) for i in range(size)])  49.7 us
    ppermute x48, waiting for transfers between devices, swap(): return lax.ppermute(value, axis, [(i, i ^ mask) for i in range(size)])  31.1 us
    pallas_call x9, Pallas kernels, call(): pl.pallas_call(kernel, out_shape=tuple((jax.ShapeDtypeStruct(*o) for o in...  20.6 us
  transfers between devices with their start and end apart: 48, of which 17 were waited for; matrix products, arithmetic and copies ran while one was open for 1% of the time, Pallas kernels for 12%

profile of v3, /device:TPU:0, one launch (start us, length us, event | category | flops | bytes accessed | tf_op | source)
XLA Modules:
  0.0 103.4 jit_solution(14258309254780984118)
XLA Ops:
  1.2 2.6 %collective-permute-start.9 = (bf16[512,128]{1,0:T(8,128)(2,1)}, bf16[512,128]{1,0:T(8,128)(2,1)S(1)}, u32[]{:S(2)}, u32[]{:S(2)}) collective-permute-start(bf16[512,128]{1,0:T(8,128)(2,1)} %refs_0_.5), channel_id=1, source_target_pairs={{0,8},{2,10},{4,12},{6,14},{8,0},{10,2},{12,4},{14,6},{16,24},{18,... | collective-permute-start | bytes 393224 | tf_op jit(solution)/shard_map/ppermute | solution.py:22
  3.8 2.6 %collective-permute-start.13 = (bf16[512,128]{1,0:T(8,128)(2,1)}, bf16[512,128]{1,0:T(8,128)(2,1)S(1)}, u32[]{:S(2)}, u32[]{:S(2)}) collective-permute-start(bf16[512,128]{1,0:T(8,128)(2,1)} %refs_0_.5), channel_id=1, source_target_pairs={{0,16},{2,18},{4,20},{6,22},{8,24},{10,26},{12,28},{14,30},{16,0},... | collective-permute-start | bytes 393224 | tf_op jit(solution)/shard_map/ppermute | solution.py:22
  9.1 1.7 %collective-permute-start.6 = (bf16[512,128]{1,0:T(8,128)(2,1)}, bf16[512,128]{1,0:T(8,128)(2,1)S(1)}, u32[]{:S(2)}, u32[]{:S(2)}) collective-permute-start(bf16[512,128]{1,0:T(8,128)(2,1)} %refs_0_.5), channel_id=1, source_target_pairs={{0,1},{1,0},{2,3},{3,2},{4,5},{5,4},{6,7},{7,6},{8,9},{9,8},{10,11... | collective-permute-start | bytes 393224 | tf_op jit(solution)/shard_map/ppermute | solution.py:22
  10.8 1.5 %collective-permute-start.7 = (bf16[512,128]{1,0:T(8,128)(2,1)}, bf16[512,128]{1,0:T(8,128)(2,1)S(1)}, u32[]{:S(2)}, u32[]{:S(2)}) collective-permute-start(bf16[512,128]{1,0:T(8,128)(2,1)} %refs_0_.5), channel_id=1, source_target_pairs={{0,4},{2,6},{4,0},{6,2},{8,12},{10,14},{12,8},{14,10},{16,20},{18,... | collective-permute-start | bytes 393224 | tf_op jit(solution)/shard_map/ppermute | solution.py:22
  12.3 4.6 %collective-permute-done.13.refs_8_ = bf16[512,128]{1,0:T(8,128)(2,1)S(1)} collective-permute-done((bf16[512,128]{1,0:T(8,128)(2,1)}, bf16[512,128]{1,0:T(8,128)(2,1)S(1)}, u32[]{:S(2)}, u32[]{:S(2)}) %collective-permute-start.13) | collective-permute-done | bytes 131104 | tf_op jit(solution)/shard_map/ppermute | solution.py:22
  17.0 1.5 %collective-permute-start.11 = (bf16[512,128]{1,0:T(8,128)(2,1)S(1)}, bf16[512,128]{1,0:T(8,128)(2,1)S(1)}, u32[]{:S(2)}, u32[]{:S(2)}) collective-permute-start(bf16[512,128]{1,0:T(8,128)(2,1)S(1)} %collective-permute-done.9.refs_4_), channel_id=1, source_target_pairs={{0,4},{2,6},{4,0},{6,2},{8,12},{10,14},{12,8},{14,10},{16,20},{18,... | collective-permute-start | bytes 393224 | tf_op jit(solution)/shard_map/ppermute | solution.py:22
  18.5 1.5 %collective-permute-start.14 = (bf16[512,128]{1,0:T(8,128)(2,1)S(1)}, bf16[512,128]{1,0:T(8,128)(2,1)S(1)}, u32[]{:S(2)}, u32[]{:S(2)}) collective-permute-start(bf16[512,128]{1,0:T(8,128)(2,1)S(1)} %collective-permute-done.13.refs_8_), channel_id=1, source_target_pairs={{0,1},{1,0},{2,3},{3,2},{4,5},{5,4},{6,7},{7,6},{8,9},{9,8},{10,11... | collective-permute-start | bytes 393224 | tf_op jit(solution)/shard_map/ppermute | solution.py:22
  21.0 2.3 %collective-permute-done.11.refs_6_ = bf16[512,128]{1,0:T(8,128)(2,1)S(1)} collective-permute-done((bf16[512,128]{1,0:T(8,128)(2,1)S(1)}, bf16[512,128]{1,0:T(8,128)(2,1)S(1)}, u32[]{:S(2)}, u32[]{:S(2)}) %collective-permute-start.11) | collective-permute-done | bytes 131104 | tf_op jit(solution)/shard_map/ppermute | solution.py:22
  23.3 1.5 %collective-permute-start.15 = (bf16[512,128]{1,0:T(8,128)(2,1)S(1)}, bf16[512,128]{1,0:T(8,128)(2,1)S(1)}, u32[]{:S(2)}, u32[]{:S(2)}) collective-permute-start(bf16[512,128]{1,0:T(8,128)(2,1)S(1)} %collective-permute-done.13.refs_8_), channel_id=1, source_target_pairs={{0,4},{2,6},{4,0},{6,2},{8,12},{10,14},{12,8},{14,10},{16,20},{18,... | collective-permute-start | bytes 393224 | tf_op jit(solution)/shard_map/ppermute | solution.py:22
  24.8 1.5 %collective-permute-start.18 = (bf16[512,128]{1,0:T(8,128)(2,1)S(1)}, bf16[512,128]{1,0:T(8,128)(2,1)S(1)}, u32[]{:S(2)}, u32[]{:S(2)}) collective-permute-start(bf16[512,128]{1,0:T(8,128)(2,1)S(1)} %collective-permute-done.17.refs_12_), channel_id=1, source_target_pairs={{0,1},{1,0},{2,3},{3,2},{4,5},{5,4},{6,7},{7,6},{8,9},{9,8},{10,11... | collective-permute-start | bytes 393224 | tf_op jit(solution)/shard_map/ppermute | solution.py:22
  27.6 1.5 %collective-permute-start.12 = (bf16[512,128]{1,0:T(8,128)(2,1)S(1)}, bf16[512,128]{1,0:T(8,128)(2,1)S(1)}, u32[]{:S(2)}, u32[]{:S(2)}) collective-permute-start(bf16[512,128]{1,0:T(8,128)(2,1)S(1)} %collective-permute-done.11.refs_6_), channel_id=1, source_target_pairs={{0,1},{1,0},{2,3},{3,2},{4,5},{5,4},{6,7},{7,6},{8,9},{9,8},{10,11... | collective-permute-start | bytes 393224 | tf_op jit(solution)/shard_map/ppermute | solution.py:22
  29.2 1.7 %collective-permute-start.16 = (bf16[512,128]{1,0:T(8,128)(2,1)S(1)}, bf16[512,128]{1,0:T(8,128)(2,1)S(1)}, u32[]{:S(2)}, u32[]{:S(2)}) collective-permute-start(bf16[512,128]{1,0:T(8,128)(2,1)S(1)} %collective-permute-done.14.refs_9_), channel_id=1, source_target_pairs={{0,4},{2,6},{4,0},{6,2},{8,12},{10,14},{12,8},{14,10},{16,20},{18,... | collective-permute-start | bytes 393224 | tf_op jit(solution)/shard_map/ppermute | solution.py:22
  31.9 2.4 %shard_map.94 = (s32[456]{0:T(512)S(1)}, bf16[4,16,128,128]{3,2,1,0:T(8,128)(2,1)S(1)}) custom-call(s32[4,32]{1,0:T(4,128)} %refs_0_.3, s32[4]{0:T(128)} %refs_1_.1, s32[4,32]{1,0:T(4,128)S(1)} %collective-permute-done.refs_2_, s32[4]{0:T(128)S(1)} %collective-permute-done.1.refs_3_, bf16[4,16,128,128]{3,2,1,0:T(8,128)(2,1)} %refs_4_.1), custom_call_target="tpu_custom_call" | custom-call | flops 1048576 | bytes 4194304 | tf_op jit(solution)/shard_map/pallas_call | solution.py:373
  34.4 1.5 %collective-permute-done.20.refs_15_ = bf16[512,128]{1,0:T(8,128)(2,1)S(1)} collective-permute-done((bf16[512,128]{1,0:T(8,128)(2,1)S(1)}, bf16[512,128]{1,0:T(8,128)(2,1)S(1)}, u32[]{:S(2)}, u32[]{:S(2)}) %collective-permute-start.20) | collective-permute-done | bytes 131104 | tf_op jit(solution)/shard_map/ppermute | solution.py:22
  35.9 2.6 %shard_map.97 = (bf16[4224,256]{1,0:T(8,128)(2,1)S(1)}, bf16[512,256]{1,0:T(8,128)(2,1)S(1)}) custom-call(s32[456]{0:T(512)S(1)} %get-tuple-element.16.plan, bf16[4,16,128,128]{3,2,1,0:T(8,128)(2,1)S(1)} %collective-permute-done.2.vals.v_far, bf16[512,128]{1,0:T(8,128)(2,1)} %refs_0_.5, bf16[512,128]{1,0:T(8,128)(2,1)S(1)} %collective-permute-done.6.refs_1_, ...), custom_call_target="tpu_custom_call" | custom-call | flops 268435456 | bytes 4194304 | tf_op jit(solution)/shard_map/pallas_call | solution.py:373
  39.7 1.8 %shard_map.98 = f32[512,256]{1,0:T(8,128)S(1)} custom-call(s32[456]{0:T(512)S(1)} %get-tuple-element.16.plan, bf16[4,16,128,128]{3,2,1,0:T(8,128)(2,1)S(1)} %get-tuple-element.17.vals.v_own, bf16[4224,256]{1,0:T(8,128)(2,1)S(1)} %get-tuple-element.18.src), custom_call_target="tpu_custom_call" | custom-call | flops 268435456 | bytes 4194304 | tf_op jit(solution)/shard_map/pallas_call | solution.py:373
  42.3 2.2 %collective-permute-done.3.refs_1_.refs_10_ = bf16[512,128]{1,0:T(8,128)(2,1)S(1)} collective-permute-done((bf16[512,128]{1,0:T(8,128)(2,1)S(1)}, bf16[512,128]{1,0:T(8,128)(2,1)S(1)}, u32[]{:S(2)}, u32[]{:S(2)}) %collective-permute-start.3) | collective-permute-done | bytes 131104 | tf_op jit(solution)/shard_map/ppermute | solution.py:22
  44.5 2.8 %collective-permute-done.22 = bf16[512,128]{1,0:T(8,128)(2,1)S(1)} collective-permute-done((bf16[512,128]{1,0:T(8,128)(2,1)S(1)}, bf16[512,128]{1,0:T(8,128)(2,1)S(1)}, u32[]{:S(2)}, u32[]{:S(2)}) %collective-permute-start.22) | collective-permute-done | bytes 131104 | tf_op jit(solution)/shard_map/ppermute | solution.py:22
  49.1 1.8 %collective-permute-start.24 = (bf16[512,128]{1,0:T(8,128)(2,1)S(1)}, bf16[512,128]{1,0:T(8,128)(2,1)S(1)}, u32[]{:S(2)}, u32[]{:S(2)}) collective-permute-start(bf16[512,128]{1,0:T(8,128)(2,1)S(1)} %fusion.refs_0_), channel_id=1, source_target_pairs={{0,4},{2,6},{4,0},{6,2},{8,12},{10,14},{12,8},{14,10},{16,20},{18,... | collective-permute-start | bytes 393224 | tf_op jit(solution)/shard_map/ppermute | solution.py:22
  51.5 1.8 %collective-permute-start.34 = (bf16[512,128]{1,0:T(8,128)(2,1)S(1)}, bf16[512,128]{1,0:T(8,128)(2,1)S(1)}, u32[]{:S(2)}, u32[]{:S(2)}) collective-permute-start(bf16[512,128]{1,0:T(8,128)(2,1)S(1)} %fusion.refs_0_), channel_id=1, source_target_pairs={{0,24},{2,26},{4,28},{6,30},{8,16},{10,18},{12,20},{14,22},{16,8},... | collective-permute-start | bytes 393224 | tf_op jit(solution)/shard_map/ppermute | solution.py:22
  53.3 1.5 %collective-permute-start.28 = (bf16[512,128]{1,0:T(8,128)(2,1)S(1)}, bf16[512,128]{1,0:T(8,128)(2,1)S(1)}, u32[]{:S(2)}, u32[]{:S(2)}) collective-permute-start(bf16[512,128]{1,0:T(8,128)(2,1)S(1)} %collective-permute-done.26.refs_4_), channel_id=1, source_target_pairs={{0,4},{2,6},{4,0},{6,2},{8,12},{10,14},{12,8},{14,10},{16,20},{18,... | collective-permute-start | bytes 393224 | tf_op jit(solution)/shard_map/ppermute | solution.py:22
  56.7 5.8 %collective-permute-done.30.refs_1_ = bf16[512,128]{1,0:T(8,128)(2,1)S(1)} collective-permute-done((bf16[512,128]{1,0:T(8,128)(2,1)S(1)}, bf16[512,128]{1,0:T(8,128)(2,1)S(1)}, u32[]{:S(2)}, u32[]{:S(2)}) %collective-permute-start.30) | collective-permute-done | bytes 131104 | tf_op jit(solution)/shard_map/ppermute | solution.py:22
  67.2 1.6 %collective-permute-done.31.refs_2_ = bf16[512,128]{1,0:T(8,128)(2,1)S(1)} collective-permute-done((bf16[512,128]{1,0:T(8,128)(2,1)S(1)}, bf16[512,128]{1,0:T(8,128)(2,1)S(1)}, u32[]{:S(2)}, u32[]{:S(2)}) %collective-permute-start.31) | collective-permute-done | bytes 131104 | tf_op jit(solution)/shard_map/ppermute | solution.py:22
  70.7 3.2 %shard_map.95.hg = f32[4224,256]{1,0:T(8,128)S(1)} custom-call(s32[456]{0:T(512)S(1)} %get-tuple-element.16.plan, bf16[256,256]{1,0:T(8,128)(2,1)S(1)} %copy-done, bf16[4,16,128,128]{3,2,1,0:T(8,128)(2,1)S(1)} %get-tuple-element.17.vals.v_own, bf16[512,128]{1,0:T(8,128)(2,1)S(1)} %copy-done.2, bf16[512,128]{1,0:T(8,128)(2,1)S(1)} %collective-permute-done.3.refs_1_.refs_10_), custom_call_target="tpu_custom_call" | custom-call | flops 268435456 | bytes 4194304 | tf_op jit(solution)/shard_map/pallas_call | solution.py:373
  73.9 3.2 %shard_map.96.hg_far = f32[4224,256]{1,0:T(8,128)S(1)} custom-call(s32[456]{0:T(512)S(1)} %get-tuple-element.16.plan, bf16[256,256]{1,0:T(8,128)(2,1)S(1)} %copy-done, bf16[4,16,128,128]{3,2,1,0:T(8,128)(2,1)S(1)} %collective-permute-done.2.vals.v_far, bf16[512,128]{1,0:T(8,128)(2,1)S(1)} %collective-permute-done.4.refs_0_.refs_11_, ...), custom_call_target="tpu_custom_call" | custom-call | flops 268435456 | bytes 4194304 | tf_op jit(solution)/shard_map/pallas_call | solution.py:373
  77.2 1.5 %shard_map.99 = (bf16[2048,256]{1,0:T(8,128)(2,1)S(1)}, f32[256,256]{1,0:T(8,128)S(1)}) custom-call(bf16[256,256]{1,0:T(8,128)(2,1)S(1)} %copy-done.1, f32[4224,256]{1,0:T(8,128)S(1)} %shard_map.95.hg, f32[4224,256]{1,0:T(8,128)S(1)} %shard_map.96.hg_far, bf16[512,128]{1,0:T(8,128)(2,1)S(1)} %fusion.refs_0_, ...), custom_call_target="tpu_custom_call" | custom-call | flops 536870912 | bytes 4194304 | tf_op jit(solution)/shard_map/pallas_call | solution.py:373
  78.7 4.8 %shard_map.100 = (bf16[1024,256]{1,0:T(8,128)(2,1)S(1)}, f32[256,256]{1,0:T(8,128)S(1)}, bf16[256,256]{1,0:T(8,128)(2,1)S(1)}) custom-call(s32[456]{0:T(512)S(1)} %get-tuple-element.16.plan, bf16[256,256]{1,0:T(8,128)(2,1)S(1)} %copy-done.1, bf16[4,16,128,128]{3,2,1,0:T(8,128)(2,1)S(1)} %get-tuple-element.17.vals.v_own, ...), custom_call_target="tpu_custom_call" | custom-call | flops 1073741824 | bytes 4194304 | tf_op jit(solution)/shard_map/pallas_call | solution.py:373
  85.0 2.1 %collective-permute-start.42 = (bf16[256,128]{1,0:T(8,128)(2,1)S(1)}, bf16[256,128]{1,0:T(8,128)(2,1)S(1)}, u32[]{:S(2)}, u32[]{:S(2)}) collective-permute-start(bf16[256,128]{1,0:T(8,128)(2,1)S(1)} %get-tuple-element.29), channel_id=1, source_target_pairs={{0,4},{2,6},{4,0},{6,2},{8,12},{10,14},{12,8},{14,10},{16,20},{18,... | collective-permute-start | bytes 196616 | tf_op jit(solution)/shard_map/ppermute | solution.py:22
  89.5 2.8 %collective-permute-done.43 = bf16[256,128]{1,0:T(8,128)(2,1)S(1)} collective-permute-done((bf16[256,128]{1,0:T(8,128)(2,1)S(1)}, bf16[256,128]{1,0:T(8,128)(2,1)S(1)}, u32[]{:S(2)}, u32[]{:S(2)}) %collective-permute-start.43) | collective-permute-done | bytes 65568 | tf_op jit(solution)/shard_map/ppermute | solution.py:22
  92.3 1.6 %collective-permute-start.44 = (bf16[256,128]{1,0:T(8,128)(2,1)S(1)}, bf16[256,128]{1,0:T(8,128)(2,1)S(1)}, u32[]{:S(2)}, u32[]{:S(2)}) collective-permute-start(bf16[256,128]{1,0:T(8,128)(2,1)S(1)} %add_convert_fusion.1), channel_id=1, source_target_pairs={{0,8},{2,10},{4,12},{6,14},{8,0},{10,2},{12,4},{14,6},{16,24},{18,... | collective-permute-start | bytes 196616 | tf_op jit(solution)/shard_map/ppermute | solution.py:22
  94.7 2.1 %collective-permute-start.46 = (bf16[256,128]{1,0:T(8,128)(2,1)S(1)}, bf16[256,128]{1,0:T(8,128)(2,1)S(1)}, u32[]{:S(2)}, u32[]{:S(2)}) collective-permute-start(bf16[256,128]{1,0:T(8,128)(2,1)S(1)} %add_convert_fusion.1), channel_id=1, source_target_pairs={{0,24},{2,26},{4,28},{6,30},{8,16},{10,18},{12,20},{14,22},{16,8},... | collective-permute-start | bytes 196616 | tf_op jit(solution)/shard_map/ppermute | solution.py:22
  96.9 2.0 %collective-permute-start.39 = (bf16[512,128]{1,0:T(8,128)(2,1)S(1)}, bf16[512,128]{1,0:T(8,128)(2,1)S(1)}, u32[]{:S(2)}, u32[]{:S(2)}) collective-permute-start(bf16[512,128]{1,0:T(8,128)(2,1)S(1)} %slice.41), channel_id=1, source_target_pairs={{0,1},{1,0},{2,3},{3,2},{4,5},{5,4},{6,7},{7,6},{8,9},{9,8},{10,11... | collective-permute-start | bytes 393224 | tf_op jit(solution)/shard_map/ppermute | solution.py:22
  (89 shorter events, 28.8 us)
Async XLA Ops:
  0.6 35.2 %collective-permute-start.2 = (bf16[4,16,128,128]{3,2,1,0:T(8,128)(2,1)}, bf16[4,16,128,128]{3,2,1,0:T(8,128)(2,1)S(1)}, u32[]{:S(2)}, u32[]{:S(2)}) collective-permute-start(bf16[4,16,128,128]{3,2,1,0:T(8,128)(2,1)} %refs_4_.1), channel_id=1, source_target_pairs={{0,2},{2,0},{4,6},{6,4},{8,10},{10,8},{12,14},{14,12},{16,18},{18,... | collective-permute-start | bytes 6291464 | tf_op jit(solution)/shard_map/ppermute | solution.py:22
  1.2 9.6 %collective-permute-start.9 = (bf16[512,128]{1,0:T(8,128)(2,1)}, bf16[512,128]{1,0:T(8,128)(2,1)S(1)}, u32[]{:S(2)}, u32[]{:S(2)}) collective-permute-start(bf16[512,128]{1,0:T(8,128)(2,1)} %refs_0_.5), channel_id=1, source_target_pairs={{0,8},{2,10},{4,12},{6,14},{8,0},{10,2},{12,4},{14,6},{16,24},{18,... | collective-permute-start | bytes 393224 | tf_op jit(solution)/shard_map/ppermute | solution.py:22
  3.8 13.1 %collective-permute-start.13 = (bf16[512,128]{1,0:T(8,128)(2,1)}, bf16[512,128]{1,0:T(8,128)(2,1)S(1)}, u32[]{:S(2)}, u32[]{:S(2)}) collective-permute-start(bf16[512,128]{1,0:T(8,128)(2,1)} %refs_0_.5), channel_id=1, source_target_pairs={{0,16},{2,18},{4,20},{6,22},{8,24},{10,26},{12,28},{14,30},{16,0},... | collective-permute-start | bytes 393224 | tf_op jit(solution)/shard_map/ppermute | solution.py:22
  6.4 12.0 %collective-permute-start.17 = (bf16[512,128]{1,0:T(8,128)(2,1)}, bf16[512,128]{1,0:T(8,128)(2,1)S(1)}, u32[]{:S(2)}, u32[]{:S(2)}) collective-permute-start(bf16[512,128]{1,0:T(8,128)(2,1)} %refs_0_.5), channel_id=1, source_target_pairs={{0,24},{2,26},{4,28},{6,30},{8,16},{10,18},{12,20},{14,22},{16,8},... | collective-permute-start | bytes 393224 | tf_op jit(solution)/shard_map/ppermute | solution.py:22
  9.1 10.9 %collective-permute-start.6 = (bf16[512,128]{1,0:T(8,128)(2,1)}, bf16[512,128]{1,0:T(8,128)(2,1)S(1)}, u32[]{:S(2)}, u32[]{:S(2)}) collective-permute-start(bf16[512,128]{1,0:T(8,128)(2,1)} %refs_0_.5), channel_id=1, source_target_pairs={{0,1},{1,0},{2,3},{3,2},{4,5},{5,4},{6,7},{7,6},{8,9},{9,8},{10,11... | collective-permute-start | bytes 393224 | tf_op jit(solution)/shard_map/ppermute | solution.py:22
  10.8 9.7 %collective-permute-start.7 = (bf16[512,128]{1,0:T(8,128)(2,1)}, bf16[512,128]{1,0:T(8,128)(2,1)S(1)}, u32[]{:S(2)}, u32[]{:S(2)}) collective-permute-start(bf16[512,128]{1,0:T(8,128)(2,1)} %refs_0_.5), channel_id=1, source_target_pairs={{0,4},{2,6},{4,0},{6,2},{8,12},{10,14},{12,8},{14,10},{16,20},{18,... | collective-permute-start | bytes 393224 | tf_op jit(solution)/shard_map/ppermute | solution.py:22
  17.0 6.4 %collective-permute-start.11 = (bf16[512,128]{1,0:T(8,128)(2,1)S(1)}, bf16[512,128]{1,0:T(8,128)(2,1)S(1)}, u32[]{:S(2)}, u32[]{:S(2)}) collective-permute-start(bf16[512,128]{1,0:T(8,128)(2,1)S(1)} %collective-permute-done.9.refs_4_), channel_id=1, source_target_pairs={{0,4},{2,6},{4,0},{6,2},{8,12},{10,14},{12,8},{14,10},{16,20},{18,... | collective-permute-start | bytes 393224 | tf_op jit(solution)/shard_map/ppermute | solution.py:22
  18.5 6.4 %collective-permute-start.14 = (bf16[512,128]{1,0:T(8,128)(2,1)S(1)}, bf16[512,128]{1,0:T(8,128)(2,1)S(1)}, u32[]{:S(2)}, u32[]{:S(2)}) collective-permute-start(bf16[512,128]{1,0:T(8,128)(2,1)S(1)} %collective-permute-done.13.refs_8_), channel_id=1, source_target_pairs={{0,1},{1,0},{2,3},{3,2},{4,5},{5,4},{6,7},{7,6},{8,9},{9,8},{10,11... | collective-permute-start | bytes 393224 | tf_op jit(solution)/shard_map/ppermute | solution.py:22
  20.0 6.4 %collective-permute-start.19 = (bf16[512,128]{1,0:T(8,128)(2,1)S(1)}, bf16[512,128]{1,0:T(8,128)(2,1)S(1)}, u32[]{:S(2)}, u32[]{:S(2)}) collective-permute-start(bf16[512,128]{1,0:T(8,128)(2,1)S(1)} %collective-permute-done.17.refs_12_), channel_id=1, source_target_pairs={{0,4},{2,6},{4,0},{6,2},{8,12},{10,14},{12,8},{14,10},{16,20},{18,... | collective-permute-start | bytes 393224 | tf_op jit(solution)/shard_map/ppermute | solution.py:22
  20.5 7.1 %collective-permute-start.10 = (bf16[512,128]{1,0:T(8,128)(2,1)S(1)}, bf16[512,128]{1,0:T(8,128)(2,1)S(1)}, u32[]{:S(2)}, u32[]{:S(2)}) collective-permute-start(bf16[512,128]{1,0:T(8,128)(2,1)S(1)} %collective-permute-done.9.refs_4_), channel_id=1, source_target_pairs={{0,1},{1,0},{2,3},{3,2},{4,5},{5,4},{6,7},{7,6},{8,9},{9,8},{10,11... | collective-permute-start | bytes 393224 | tf_op jit(solution)/shard_map/ppermute | solution.py:22
  26.4 8.0 %collective-permute-start.8 = (bf16[512,128]{1,0:T(8,128)(2,1)S(1)}, bf16[512,128]{1,0:T(8,128)(2,1)S(1)}, u32[]{:S(2)}, u32[]{:S(2)}) collective-permute-start(bf16[512,128]{1,0:T(8,128)(2,1)S(1)} %collective-permute-done.6.refs_1_), channel_id=1, source_target_pairs={{0,4},{2,6},{4,0},{6,2},{8,12},{10,14},{12,8},{14,10},{16,20},{18,... | collective-permute-start | bytes 393224 | tf_op jit(solution)/shard_map/ppermute | solution.py:22
  27.6 6.7 %collective-permute-start.12 = (bf16[512,128]{1,0:T(8,128)(2,1)S(1)}, bf16[512,128]{1,0:T(8,128)(2,1)S(1)}, u32[]{:S(2)}, u32[]{:S(2)}) collective-permute-start(bf16[512,128]{1,0:T(8,128)(2,1)S(1)} %collective-permute-done.11.refs_6_), channel_id=1, source_target_pairs={{0,1},{1,0},{2,3},{3,2},{4,5},{5,4},{6,7},{7,6},{8,9},{9,8},{10,11... | collective-permute-start | bytes 393224 | tf_op jit(solution)/shard_map/ppermute | solution.py:22
  42.1 8.7 %collective-permute-start.4 = (bf16[512,128]{1,0:T(8,128)(2,1)S(1)}, bf16[512,128]{1,0:T(8,128)(2,1)S(1)}, u32[]{:S(2)}, u32[]{:S(2)}) collective-permute-start(bf16[512,128]{1,0:T(8,128)(2,1)S(1)} %copy-done.2), channel_id=1, source_target_pairs={{0,2},{2,0},{4,6},{6,4},{8,10},{10,8},{12,14},{14,12},{16,18},{18,... | collective-permute-start | bytes 393224 | tf_op jit(solution)/shard_map/ppermute | solution.py:22
  44.5 7.0 %collective-permute-start.5 = (bf16[512,128]{1,0:T(8,128)(2,1)S(1)}, bf16[512,128]{1,0:T(8,128)(2,1)S(1)}, u32[]{:S(2)}, u32[]{:S(2)}) collective-permute-start(bf16[512,128]{1,0:T(8,128)(2,1)S(1)} %collective-permute-done.3.refs_1_.refs_10_), channel_id=1, source_target_pairs={{0,2},{2,0},{4,6},{6,4},{8,10},{10,8},{12,14},{14,12},{16,18},{18,... | collective-permute-start | bytes 393224 | tf_op jit(solution)/shard_map/ppermute | solution.py:22
  48.6 6.3 %collective-permute-start.23 = (bf16[512,128]{1,0:T(8,128)(2,1)S(1)}, bf16[512,128]{1,0:T(8,128)(2,1)S(1)}, u32[]{:S(2)}, u32[]{:S(2)}) collective-permute-start(bf16[512,128]{1,0:T(8,128)(2,1)S(1)} %fusion.refs_0_), channel_id=1, source_target_pairs={{0,1},{1,0},{2,3},{3,2},{4,5},{5,4},{6,7},{7,6},{8,9},{9,8},{10,11... | collective-permute-start | bytes 393224 | tf_op jit(solution)/shard_map/ppermute | solution.py:22
  49.1 6.3 %collective-permute-start.24 = (bf16[512,128]{1,0:T(8,128)(2,1)S(1)}, bf16[512,128]{1,0:T(8,128)(2,1)S(1)}, u32[]{:S(2)}, u32[]{:S(2)}) collective-permute-start(bf16[512,128]{1,0:T(8,128)(2,1)S(1)} %fusion.refs_0_), channel_id=1, source_target_pairs={{0,4},{2,6},{4,0},{6,2},{8,12},{10,14},{12,8},{14,10},{16,20},{18,... | collective-permute-start | bytes 393224 | tf_op jit(solution)/shard_map/ppermute | solution.py:22
  50.9 11.6 %collective-permute-start.30 = (bf16[512,128]{1,0:T(8,128)(2,1)S(1)}, bf16[512,128]{1,0:T(8,128)(2,1)S(1)}, u32[]{:S(2)}, u32[]{:S(2)}) collective-permute-start(bf16[512,128]{1,0:T(8,128)(2,1)S(1)} %fusion.refs_0_), channel_id=1, source_target_pairs={{0,16},{2,18},{4,20},{6,22},{8,24},{10,26},{12,28},{14,30},{16,0},... | collective-permute-start | bytes 393224 | tf_op jit(solution)/shard_map/ppermute | solution.py:22
  51.5 11.6 %collective-permute-start.34 = (bf16[512,128]{1,0:T(8,128)(2,1)S(1)}, bf16[512,128]{1,0:T(8,128)(2,1)S(1)}, u32[]{:S(2)}, u32[]{:S(2)}) collective-permute-start(bf16[512,128]{1,0:T(8,128)(2,1)S(1)} %fusion.refs_0_), channel_id=1, source_target_pairs={{0,24},{2,26},{4,28},{6,30},{8,16},{10,18},{12,20},{14,22},{16,8},... | collective-permute-start | bytes 393224 | tf_op jit(solution)/shard_map/ppermute | solution.py:22
  53.3 10.9 %collective-permute-start.28 = (bf16[512,128]{1,0:T(8,128)(2,1)S(1)}, bf16[512,128]{1,0:T(8,128)(2,1)S(1)}, u32[]{:S(2)}, u32[]{:S(2)}) collective-permute-start(bf16[512,128]{1,0:T(8,128)(2,1)S(1)} %collective-permute-done.26.refs_4_), channel_id=1, source_target_pairs={{0,4},{2,6},{4,0},{6,2},{8,12},{10,14},{12,8},{14,10},{16,20},{18,... | collective-permute-start | bytes 393224 | tf_op jit(solution)/shard_map/ppermute | solution.py:22
  54.8 10.4 %collective-permute-start.25 = (bf16[512,128]{1,0:T(8,128)(2,1)S(1)}, bf16[512,128]{1,0:T(8,128)(2,1)S(1)}, u32[]{:S(2)}, u32[]{:S(2)}) collective-permute-start(bf16[512,128]{1,0:T(8,128)(2,1)S(1)} %collective-permute-done.23.refs_1_), channel_id=1, source_target_pairs={{0,4},{2,6},{4,0},{6,2},{8,12},{10,14},{12,8},{14,10},{16,20},{18,... | collective-permute-start | bytes 393224 | tf_op jit(solution)/shard_map/ppermute | solution.py:22
  55.4 11.2 %collective-permute-start.27 = (bf16[512,128]{1,0:T(8,128)(2,1)S(1)}, bf16[512,128]{1,0:T(8,128)(2,1)S(1)}, u32[]{:S(2)}, u32[]{:S(2)}) collective-permute-start(bf16[512,128]{1,0:T(8,128)(2,1)S(1)} %collective-permute-done.26.refs_4_), channel_id=1, source_target_pairs={{0,1},{1,0},{2,3},{3,2},{4,5},{5,4},{6,7},{7,6},{8,9},{9,8},{10,11... | collective-permute-start | bytes 393224 | tf_op jit(solution)/shard_map/ppermute | solution.py:22
  62.5 6.4 %collective-permute-start.31 = (bf16[512,128]{1,0:T(8,128)(2,1)S(1)}, bf16[512,128]{1,0:T(8,128)(2,1)S(1)}, u32[]{:S(2)}, u32[]{:S(2)}) collective-permute-start(bf16[512,128]{1,0:T(8,128)(2,1)S(1)} %collective-permute-done.30.refs_1_), channel_id=1, source_target_pairs={{0,1},{1,0},{2,3},{3,2},{4,5},{5,4},{6,7},{7,6},{8,9},{9,8},{10,11... | collective-permute-start | bytes 393224 | tf_op jit(solution)/shard_map/ppermute | solution.py:22
  63.2 6.4 %collective-permute-start.36 = (bf16[512,128]{1,0:T(8,128)(2,1)S(1)}, bf16[512,128]{1,0:T(8,128)(2,1)S(1)}, u32[]{:S(2)}, u32[]{:S(2)}) collective-permute-start(bf16[512,128]{1,0:T(8,128)(2,1)S(1)} %collective-permute-done.34.refs_5_), channel_id=1, source_target_pairs={{0,4},{2,6},{4,0},{6,2},{8,12},{10,14},{12,8},{14,10},{16,20},{18,... | collective-permute-start | bytes 393224 | tf_op jit(solution)/shard_map/ppermute | solution.py:22
  64.2 12.9 %collective-permute-start.29 = (bf16[512,128]{1,0:T(8,128)(2,1)S(1)}, bf16[512,128]{1,0:T(8,128)(2,1)S(1)}, u32[]{:S(2)}, u32[]{:S(2)}) collective-permute-start(bf16[512,128]{1,0:T(8,128)(2,1)S(1)} %collective-permute-done.28.refs_6_), channel_id=1, source_target_pairs={{0,1},{1,0},{2,3},{3,2},{4,5},{5,4},{6,7},{7,6},{8,9},{9,8},{10,11... | collective-permute-start | bytes 393224 | tf_op jit(solution)/shard_map/ppermute | solution.py:22
  65.2 13.4 %collective-permute-start.32 = (bf16[512,128]{1,0:T(8,128)(2,1)S(1)}, bf16[512,128]{1,0:T(8,128)(2,1)S(1)}, u32[]{:S(2)}, u32[]{:S(2)}) collective-permute-start(bf16[512,128]{1,0:T(8,128)(2,1)S(1)} %collective-permute-done.30.refs_1_), channel_id=1, source_target_pairs={{0,4},{2,6},{4,0},{6,2},{8,12},{10,14},{12,8},{14,10},{16,20},{18,... | collective-permute-start | bytes 393224 | tf_op jit(solution)/shard_map/ppermute | solution.py:22
  66.6 12.1 %collective-permute-start.35 = (bf16[512,128]{1,0:T(8,128)(2,1)S(1)}, bf16[512,128]{1,0:T(8,128)(2,1)S(1)}, u32[]{:S(2)}, u32[]{:S(2)}) collective-permute-start(bf16[512,128]{1,0:T(8,128)(2,1)S(1)} %collective-permute-done.34.refs_5_), channel_id=1, source_target_pairs={{0,1},{1,0},{2,3},{3,2},{4,5},{5,4},{6,7},{7,6},{8,9},{9,8},{10,11... | collective-permute-start | bytes 393224 | tf_op jit(solution)/shard_map/ppermute | solution.py:22
  68.9 9.8 %collective-permute-start.33 = (bf16[512,128]{1,0:T(8,128)(2,1)S(1)}, bf16[512,128]{1,0:T(8,128)(2,1)S(1)}, u32[]{:S(2)}, u32[]{:S(2)}) collective-permute-start(bf16[512,128]{1,0:T(8,128)(2,1)S(1)} %collective-permute-done.31.refs_2_), channel_id=1, source_target_pairs={{0,4},{2,6},{4,0},{6,2},{8,12},{10,14},{12,8},{14,10},{16,20},{18,... | collective-permute-start | bytes 393224 | tf_op jit(solution)/shard_map/ppermute | solution.py:22
  69.6 9.1 %collective-permute-start.37 = (bf16[512,128]{1,0:T(8,128)(2,1)S(1)}, bf16[512,128]{1,0:T(8,128)(2,1)S(1)}, u32[]{:S(2)}, u32[]{:S(2)}) collective-permute-start(bf16[512,128]{1,0:T(8,128)(2,1)S(1)} %collective-permute-done.36.refs_7_), channel_id=1, source_target_pairs={{0,1},{1,0},{2,3},{3,2},{4,5},{5,4},{6,7},{7,6},{8,9},{9,8},{10,11... | collective-permute-start | bytes 393224 | tf_op jit(solution)/shard_map/ppermute | solution.py:22
  88.9 7.9 %collective-permute-start.38 = (bf16[512,256]{1,0:T(8,128)(2,1)S(1)}, bf16[512,256]{1,0:T(8,128)(2,1)S(1)}, u32[]{:S(2)}, u32[]{:S(2)}) collective-permute-start(bf16[512,256]{1,0:T(8,128)(2,1)S(1)} %get-tuple-element.24), channel_id=1, source_target_pairs={{0,2},{2,0},{4,6},{6,4},{8,10},{10,8},{12,14},{14,12},{16,18},{18,... | collective-permute-start | bytes 786440 | tf_op jit(solution)/shard_map/ppermute | solution.py:22
  92.3 6.6 %collective-permute-start.44 = (bf16[256,128]{1,0:T(8,128)(2,1)S(1)}, bf16[256,128]{1,0:T(8,128)(2,1)S(1)}, u32[]{:S(2)}, u32[]{:S(2)}) collective-permute-start(bf16[256,128]{1,0:T(8,128)(2,1)S(1)} %add_convert_fusion.1), channel_id=1, source_target_pairs={{0,8},{2,10},{4,12},{6,14},{8,0},{10,2},{12,4},{14,6},{16,24},{18,... | collective-permute-start | bytes 196616 | tf_op jit(solution)/shard_map/ppermute | solution.py:22
  93.9 6.1 %collective-permute-start.45 = (bf16[256,128]{1,0:T(8,128)(2,1)S(1)}, bf16[256,128]{1,0:T(8,128)(2,1)S(1)}, u32[]{:S(2)}, u32[]{:S(2)}) collective-permute-start(bf16[256,128]{1,0:T(8,128)(2,1)S(1)} %add_convert_fusion.1), channel_id=1, source_target_pairs={{0,16},{2,18},{4,20},{6,22},{8,24},{10,26},{12,28},{14,30},{16,0},... | collective-permute-start | bytes 196616 | tf_op jit(solution)/shard_map/ppermute | solution.py:22
  94.7 6.2 %collective-permute-start.46 = (bf16[256,128]{1,0:T(8,128)(2,1)S(1)}, bf16[256,128]{1,0:T(8,128)(2,1)S(1)}, u32[]{:S(2)}, u32[]{:S(2)}) collective-permute-start(bf16[256,128]{1,0:T(8,128)(2,1)S(1)} %add_convert_fusion.1), channel_id=1, source_target_pairs={{0,24},{2,26},{4,28},{6,30},{8,16},{10,18},{12,20},{14,22},{16,8},... | collective-permute-start | bytes 196616 | tf_op jit(solution)/shard_map/ppermute | solution.py:22
  (19 other events, 104.2 us)
